TPU v7x, 32 devices: a whole 2x2x4 slice. The times are simulated.
32 devices in a mesh: dp: 8 (over y, x, core), fsdp: 4 (over z).
Axes of the slice: x: 2, y: 2, z: 4, core: 2. Of those that a mesh axis runs over, the one named last changes fastest.
Arguments:
- token_ids: int32 [2, 32, 256], P(None, ('dp', 'fsdp')), may hold values from 0 to 51199
- doc_lengths: int32 [2, 32, 3], P(None, ('dp', 'fsdp')), may hold values from 1 to 128, 256 in all within a row
- doc_order: int32 [2, 32, 3], P(None, ('dp', 'fsdp')), may hold values from 0 to 2, each once within a row
- loss_slots: int32 [2, 32, 32], P(None, ('dp', 'fsdp')), may hold values from 0 to 255, as said below
- targets: int32 [2, 32, 32], P(None, ('dp', 'fsdp')), may hold values from 0 to 51199
- loss_mask: int32 [2, 32, 32], P(None, ('dp', 'fsdp')), may hold values from 0 to 1, as said below
- token_table: float32 [51200, 768], P(('dp', 'fsdp'))
- position_table: float32 [256, 768], P(('dp', 'fsdp')), may hold values from -0.21875 to 0.21875
- attend_weight: float32 [2, 768, 2304], P(None, ('dp', 'fsdp')), may hold values from -0.21875 to 0.21875
- project_weight: float32 [2, 768, 768], P(None, ('dp', 'fsdp')), may hold values from -0.875 to 0.875
- expand_weight: float32 [2, 768, 3072], P(None, ('dp', 'fsdp')), may hold values from -0.21875 to 0.21875
- contract_weight: float32 [2, 3072, 768], P(None, ('dp', 'fsdp')), may hold values from -0.109375 to 0.109375
- vector_params: float32 [19968], P(('dp', 'fsdp'))
- table_moments: float32 [2, 51200, 768], P(None, ('dp', 'fsdp'))
- position_moments: float32 [2, 256, 768], P(None, ('dp', 'fsdp'))
- attend_moments: float32 [2, 2, 768, 2304], P(None, None, ('dp', 'fsdp'))
- project_moments: float32 [2, 2, 768, 768], P(None, None, ('dp', 'fsdp'))
- expand_moments: float32 [2, 2, 768, 3072], P(None, None, ('dp', 'fsdp'))
- contract_moments: float32 [2, 2, 3072, 768], P(None, None, ('dp', 'fsdp'))
- vector_moments: float32 [2, 19968], P(None, ('dp', 'fsdp'))
Outputs:
- loss: float32 [], replicated
- grad_norm: float32 [], replicated
- new_table: float32 [51200, 768], P(('dp', 'fsdp'))
- new_positions: float32 [256, 768], P(('dp', 'fsdp'))
- new_attend: float32 [2, 768, 2304], P(None, ('dp', 'fsdp'))
- new_project: float32 [2, 768, 768], P(None, ('dp', 'fsdp'))
- new_expand: float32 [2, 768, 3072], P(None, ('dp', 'fsdp'))
- new_contract: float32 [2, 3072, 768], P(None, ('dp', 'fsdp'))
- new_vectors: float32 [19968], P(('dp', 'fsdp'))
- table_state: float32 [2, 51200, 768], P(None, ('dp', 'fsdp'))
- position_state: float32 [2, 256, 768], P(None, ('dp', 'fsdp'))
- attend_state: float32 [2, 2, 768, 2304], P(None, None, ('dp', 'fsdp'))
- project_state: float32 [2, 2, 768, 768], P(None, None, ('dp', 'fsdp'))
- expand_state: float32 [2, 2, 768, 3072], P(None, None, ('dp', 'fsdp'))
- contract_state: float32 [2, 2, 3072, 768], P(None, None, ('dp', 'fsdp'))
- vector_state: float32 [2, 19968], P(None, ('dp', 'fsdp'))
- table_copy: bfloat16 [51200, 768], P(('dp', 'fsdp'))
- position_copy: bfloat16 [256, 768], P(('dp', 'fsdp'))
- attend_copy: bfloat16 [2, 768, 2304], P(None, ('dp', 'fsdp'))
- project_copy: bfloat16 [2, 768, 768], P(None, ('dp', 'fsdp'))
- expand_copy: bfloat16 [2, 768, 3072], P(None, ('dp', 'fsdp'))
- contract_copy: bfloat16 [2, 3072, 768], P(None, ('dp', 'fsdp'))
- vector_copy: bfloat16 [19968], P(('dp', 'fsdp'))
Inputs may be any that keep to these rules, and one draw needn't show every extreme that they name: `doc_lengths`: each row's 3 lengths sum to 256. `doc_order`: each row is a permutation of its 3 places. `loss_slots`: each row's 32 positions are distinct and increasing. `loss_mask`: the first loss position of each row is valid.
All inputs are finite; a program needn't handle non-finite values.
Results may differ from a plain program's by a relative error of at most 0.0095.
Values may be sent and summed in bfloat16 or wider, within the bound.
No kernel may reach another device: no remote copies, remote signals or barrier semaphores. Data moves between devices by JAX's collectives and lax.ppermute only.
A program may use at most 384 MiB of HBM per device.

v0:
```python
import jax
import jax.numpy as jnp
from jax import lax
from jax.sharding import PartitionSpec as P

HEADS = 12


norm_eps = 1e-05
gelu_scale = 0.7978845608
gelu_cubic = 0.044715
beta_one = 0.5
beta_two = 0.5
learn_rate = 0.03
decay_rate = 0.1
adam_eps = 1e-08
clip_limit = 0.25
adam_step = 3
masked_score = -1e30


def merged(value, axis, join):
    pieces = jax.tree.map(lambda part: lax.all_gather(part, axis), value)
    head = jax.tree.map(lambda part: part[0], pieces)
    tail = jax.tree.map(lambda part: part[1:], pieces)
    subtotal, _ = lax.scan(lambda subtotal, share: (join(subtotal, share), None), head, tail)
    return subtotal


def positions_of(lengths, order, slot):
    places = jnp.arange(lengths.shape[0], dtype=jnp.int32)
    place = jnp.sum(places[None, :] * (order[None, :] == places[:, None]).astype(jnp.int32), axis=1)
    offset = jnp.sum(lengths[None, :] * (place[None, :] < place[:, None]).astype(jnp.int32), axis=1)
    ends = jnp.cumsum(lengths)
    starts = ends - lengths
    stored = jnp.arange(slot, dtype=jnp.int32)
    document = jnp.sum((stored[:, None] >= ends[None, :]).astype(jnp.int32), axis=1)
    onehot = (document[:, None] == places[None, :]).astype(jnp.int32)
    position = stored + jnp.sum(onehot * (offset - starts)[None, :], axis=1)
    return (position, document)


def vocab_place(words, rows_each, groups, member):
    shard = words // rows_each
    owned = shard % groups == member
    local = shard // groups * rows_each + words % rows_each
    return (local, owned)


def norm_forward(state, gain, bias):
    average = jnp.mean(state, axis=-1, keepdims=True)
    centered = state - average
    inverse = lax.rsqrt(jnp.mean(centered * centered, axis=-1, keepdims=True) + norm_eps)
    scaled = centered * inverse
    return (scaled * gain + bias, scaled, inverse)


def norm_backward(grad, scaled, inverse, gain):
    shaped = grad * gain
    inner = (
        shaped
        - jnp.mean(shaped, axis=-1, keepdims=True)
        - scaled * jnp.mean(shaped * scaled, axis=-1, keepdims=True)
    )
    return (inner * inverse, jnp.sum(grad * scaled, axis=0), jnp.sum(grad, axis=0))


def gelu_tanh(value):
    return 0.5 * value * (1.0 + jnp.tanh(gelu_scale * (value + gelu_cubic * value * value * value)))


def gelu_slope(value):
    bent = jnp.tanh(gelu_scale * (value + gelu_cubic * value * value * value))
    return 0.5 * (1.0 + bent) + 0.5 * value * (1.0 - bent * bent) * gelu_scale * (
        1.0 + 3.0 * gelu_cubic * value * value
    )


def outer_sum(left, right):
    return lax.dot_general(
        left, right, (((0,), (0,)), ((), ())), preferred_element_type=jnp.float32
    )


def times_transpose(left, right):
    return lax.dot_general(
        left, right, (((1,), (1,)), ((), ())), preferred_element_type=jnp.float32
    )


def attend_forward(query, keys, values, allowed):
    scale = query.shape[-1] ** (-0.5)
    raw = jnp.einsum("qhd,khd->hqk", query, keys, preferred_element_type=jnp.float32)
    scores = jnp.where(allowed[None], raw * scale, masked_score)
    peak = jnp.max(scores, axis=-1, keepdims=True)
    log_total = peak + jnp.log(jnp.sum(jnp.exp(scores - peak), axis=-1, keepdims=True))
    probs = jnp.exp(scores - log_total).astype(jnp.bfloat16)
    attended = jnp.einsum("hqk,khd->qhd", probs, values, preferred_element_type=jnp.float32)
    return (attended, log_total)


def attend_backward(query, keys, values, allowed, log_total, grad_attended):
    scale = query.shape[-1] ** (-0.5)
    raw = jnp.einsum("qhd,khd->hqk", query, keys, preferred_element_type=jnp.float32)
    scores = jnp.where(allowed[None], raw * scale, masked_score)
    probs = jnp.exp(scores - log_total)
    grad_values = jnp.einsum(
        "hqk,qhd->khd",
        probs.astype(jnp.bfloat16),
        grad_attended,
        preferred_element_type=jnp.float32,
    )
    grad_probs = jnp.einsum(
        "qhd,khd->hqk", grad_attended, values, preferred_element_type=jnp.float32
    )
    grad_scores = probs * (grad_probs - jnp.sum(probs * grad_probs, axis=-1, keepdims=True))
    grad_raw = (grad_scores * scale).astype(jnp.bfloat16)
    grad_query = jnp.einsum("hqk,khd->qhd", grad_raw, keys, preferred_element_type=jnp.float32)
    grad_keys = jnp.einsum("hqk,qhd->khd", grad_raw, query, preferred_element_type=jnp.float32)
    return (grad_query, grad_keys, grad_values)


def combine_stats(first, second):
    peak = jnp.maximum(first[0], second[0])
    total = first[1] * jnp.exp(first[0] - peak) + second[1] * jnp.exp(second[0] - peak)
    return (peak, total)


def layer_pieces(vectors, base, width, hidden_width):
    pieces = [vectors[base + index * width : base + (index + 1) * width] for index in range(8)]
    return pieces + [vectors[base + 8 * width : base + 8 * width + hidden_width]]


def adam_update(weight, moments, grad, decay):
    first = beta_one * moments[0] + (1.0 - beta_one) * grad
    root = jnp.sqrt(beta_two * moments[1] * moments[1] + (1.0 - beta_two) * grad * grad)
    rise = (
        first / (1.0 - beta_one**adam_step) / (root / (1.0 - beta_two**adam_step) ** 0.5 + adam_eps)
    )
    fresh = weight - learn_rate * (rise + decay * weight)
    return (fresh, jnp.stack([first, root]), fresh.astype(jnp.bfloat16))


def shards(
    token_ids,
    doc_lengths,
    doc_order,
    loss_slots,
    targets,
    loss_mask,
    token_table,
    position_table,
    attend_weight,
    project_weight,
    expand_weight,
    contract_weight,
    vector_params,
    table_moments,
    position_moments,
    attend_moments,
    project_moments,
    expand_moments,
    contract_moments,
    vector_moments,
):
    groups = lax.axis_size("fsdp")
    member = lax.axis_index("fsdp")
    micro_count = token_ids.shape[0]
    slot = token_ids.shape[2]
    loss_rows = loss_slots.shape[2]
    width = token_table.shape[1]
    layers = attend_weight.shape[0]
    hidden_width = expand_weight.shape[2]
    rows_each = token_table.shape[0]
    heads = HEADS
    head = width // heads
    block = 8 * width + hidden_width
    vector_total = layers * block + 2 * width
    vocab_part = lax.all_gather(token_table.astype(jnp.bfloat16), "dp", axis=0, tiled=True)
    group_tokens, group_targets, group_mask = (
        lax.all_gather(token_ids, "fsdp", axis=1, tiled=True),
        lax.all_gather(targets, "fsdp", axis=1, tiled=True),
        lax.all_gather(loss_mask, "fsdp", axis=1, tiled=True),
    )

    def fetch():
        return (
            lax.all_gather(attend_weight.astype(jnp.bfloat16), ("dp", "fsdp"), axis=1, tiled=True),
            lax.all_gather(project_weight.astype(jnp.bfloat16), ("dp", "fsdp"), axis=1, tiled=True),
            lax.all_gather(expand_weight.astype(jnp.bfloat16), ("dp", "fsdp"), axis=1, tiled=True),
            lax.all_gather(
                contract_weight.astype(jnp.bfloat16), ("dp", "fsdp"), axis=1, tiled=True
            ),
            lax.all_gather(vector_params.astype(jnp.bfloat16), ("dp", "fsdp"), axis=0, tiled=True),
            lax.all_gather(position_table.astype(jnp.bfloat16), ("dp", "fsdp"), axis=0, tiled=True),
        )

    count = lax.psum(jnp.sum(loss_mask).astype(jnp.float32), ("dp", "fsdp"))
    attend_grad = jnp.zeros((layers, width, 3 * width), jnp.float32)
    project_grad = jnp.zeros((layers, width, width), jnp.float32)
    expand_grad = jnp.zeros((layers, width, hidden_width), jnp.float32)
    contract_grad = jnp.zeros((layers, hidden_width, width), jnp.float32)
    vector_grad = jnp.zeros((vector_total,), jnp.float32)
    position_grad = jnp.zeros((slot, width), jnp.float32)
    table_grad = jnp.zeros(vocab_part.shape, jnp.float32)
    entropy_local = jnp.zeros((), jnp.float32)
    for micro in range(micro_count):
        fetched = fetch()
        attend_all, project_all, expand_all, contract_all, vectors_all, position_all = fetched
        vectors_f = vectors_all.astype(jnp.float32)
        position, document = positions_of(doc_lengths[micro, 0], doc_order[micro, 0], slot)
        stored = jnp.arange(slot, dtype=jnp.int32)
        allowed = (document[:, None] == document[None, :]) & (stored[None, :] <= stored[:, None])
        words_all = group_tokens[micro].reshape(-1)
        word_local, word_owned = vocab_place(words_all, rows_each, groups, member)
        picked = jnp.take(vocab_part, word_local, axis=0).astype(jnp.float32)
        embedded = lax.psum_scatter(
            jnp.where(word_owned[:, None], picked, 0.0).astype(jnp.bfloat16),
            "fsdp",
            scatter_dimension=0,
            tiled=True,
        ).astype(jnp.float32)
        state = embedded + jnp.take(position_all, position, axis=0).astype(jnp.float32)
        saved = []
        for layer in range(layers):
            (
                gain_one,
                bias_one,
                query_bias,
                value_bias,
                project_bias,
                gain_two,
                bias_two,
                contract_bias,
                expand_bias,
            ) = layer_pieces(vectors_f, layer * block, width, hidden_width)
            normed, scaled_one, inverse_one = norm_forward(state, gain_one, bias_one)
            normed_b = normed.astype(jnp.bfloat16)
            mixed = jnp.dot(
                normed_b, attend_all[layer], preferred_element_type=jnp.float32
            ) + jnp.concatenate([query_bias, jnp.zeros_like(query_bias), value_bias])
            mixed_b = mixed.astype(jnp.bfloat16)
            query = mixed_b[:, :width].reshape(slot, heads, head)
            keys = mixed_b[:, width : 2 * width].reshape(slot, heads, head)
            values = mixed_b[:, 2 * width :].reshape(slot, heads, head)
            attended, log_total = attend_forward(query, keys, values, allowed)
            attended_b = attended.reshape(slot, width).astype(jnp.bfloat16)
            middle = (
                state
                + jnp.dot(attended_b, project_all[layer], preferred_element_type=jnp.float32)
                + project_bias
            )
            normed_two, scaled_two, inverse_two = norm_forward(middle, gain_two, bias_two)
            normed_two_b = normed_two.astype(jnp.bfloat16)
            before = (
                jnp.dot(normed_two_b, expand_all[layer], preferred_element_type=jnp.float32)
                + expand_bias
            )
            active_b = gelu_tanh(before).astype(jnp.bfloat16)
            state = (
                middle
                + jnp.dot(active_b, contract_all[layer], preferred_element_type=jnp.float32)
                + contract_bias
            )
            saved.append(
                (
                    normed_b,
                    scaled_one,
                    inverse_one,
                    mixed_b,
                    log_total,
                    attended_b,
                    scaled_two,
                    inverse_two,
                    normed_two_b,
                    before,
                    active_b,
                )
            )
        top = layers * block
        final_gain = vectors_f[top : top + width]
        final_bias = vectors_f[top + width : top + 2 * width]
        slots = loss_slots[micro, 0]
        final, scaled_final, inverse_final = norm_forward(
            jnp.take(state, slots, axis=0), final_gain, final_bias
        )
        group_rows = lax.all_gather(final.astype(jnp.bfloat16), "fsdp", axis=0, tiled=True)
        logits = times_transpose(group_rows, vocab_part)
        target_local, target_owned = vocab_place(
            group_targets[micro].reshape(-1), rows_each, groups, member
        )
        column = jnp.arange(logits.shape[1], dtype=jnp.int32)
        hit = (column[None, :] == target_local[:, None]) & target_owned[:, None]
        peak = jnp.max(logits, axis=1)
        totals = jnp.sum(jnp.exp(logits - peak[:, None]), axis=1)
        chosen = jnp.sum(jnp.where(hit, logits, 0.0), axis=1)
        peak_all, totals_all = merged((peak, totals), "fsdp", combine_stats)
        log_rows = peak_all + jnp.log(totals_all)
        valid = group_mask[micro].reshape(-1).astype(jnp.float32)
        own_part = jnp.sum(
            lax.dynamic_slice_in_dim(log_rows * valid, member * loss_rows, loss_rows)
        )
        entropy_local = entropy_local + own_part - jnp.sum(chosen * valid)
        grad_logits = (
            (jnp.exp(logits - log_rows[:, None]) - hit.astype(jnp.float32)) * valid[:, None]
        ).astype(jnp.bfloat16)
        partial_rows = jnp.dot(grad_logits, vocab_part, preferred_element_type=jnp.float32)
        grad_final = lax.psum_scatter(
            partial_rows.astype(jnp.bfloat16), "fsdp", scatter_dimension=0, tiled=True
        ).astype(jnp.float32)
        table_grad = table_grad + outer_sum(grad_logits, group_rows)
        grad_rows, grad_final_gain, grad_final_bias = norm_backward(
            grad_final, scaled_final, inverse_final, final_gain
        )
        grad_state = jnp.zeros((slot, width), jnp.float32).at[slots].add(grad_rows)
        fetched = fetch()
        attend_all, project_all, expand_all, contract_all, vectors_all, position_all = fetched
        vectors_f = vectors_all.astype(jnp.float32)
        layer_grads = [None] * layers
        for layer in reversed(range(layers)):
            (
                normed_b,
                scaled_one,
                inverse_one,
                mixed_b,
                log_total,
                attended_b,
                scaled_two,
                inverse_two,
                normed_two_b,
                before,
                active_b,
            ) = saved[layer]
            (
                gain_one,
                bias_one,
                query_bias,
                value_bias,
                project_bias,
                gain_two,
                bias_two,
                contract_bias,
                expand_bias,
            ) = layer_pieces(vectors_f, layer * block, width, hidden_width)
            grad_out = grad_state.astype(jnp.bfloat16)
            contract_grad = contract_grad.at[layer].add(outer_sum(active_b, grad_out))
            grad_contract_bias = jnp.sum(grad_out.astype(jnp.float32), axis=0)
            grad_active = times_transpose(grad_out, contract_all[layer])
            grad_before = (grad_active * gelu_slope(before)).astype(jnp.bfloat16)
            expand_grad = expand_grad.at[layer].add(outer_sum(normed_two_b, grad_before))
            grad_expand_bias = jnp.sum(grad_before.astype(jnp.float32), axis=0)
            grad_normed_two = times_transpose(grad_before, expand_all[layer])
            grad_mid, grad_gain_two, grad_bias_two = norm_backward(
                grad_normed_two, scaled_two, inverse_two, gain_two
            )
            grad_middle = grad_state + grad_mid
            grad_project = grad_middle.astype(jnp.bfloat16)
            project_grad = project_grad.at[layer].add(outer_sum(attended_b, grad_project))
            grad_project_bias = jnp.sum(grad_project.astype(jnp.float32), axis=0)
            grad_attended = (
                times_transpose(grad_project, project_all[layer])
                .astype(jnp.bfloat16)
                .reshape(slot, heads, head)
            )
            query = mixed_b[:, :width].reshape(slot, heads, head)
            keys = mixed_b[:, width : 2 * width].reshape(slot, heads, head)
            values = mixed_b[:, 2 * width :].reshape(slot, heads, head)
            grad_query, grad_keys, grad_values = attend_backward(
                query, keys, values, allowed, log_total, grad_attended
            )
            grad_mixed = jnp.concatenate(
                [
                    grad_query.reshape(slot, width),
                    grad_keys.reshape(slot, width),
                    grad_values.reshape(slot, width),
                ],
                axis=1,
            ).astype(jnp.bfloat16)
            attend_grad = attend_grad.at[layer].add(outer_sum(normed_b, grad_mixed))
            grad_mixed_f = grad_mixed.astype(jnp.float32)
            grad_query_bias = jnp.sum(grad_mixed_f[:, :width], axis=0)
            grad_value_bias = jnp.sum(grad_mixed_f[:, 2 * width :], axis=0)
            grad_normed = times_transpose(grad_mixed, attend_all[layer])
            grad_in, grad_gain_one, grad_bias_one = norm_backward(
                grad_normed, scaled_one, inverse_one, gain_one
            )
            grad_state = grad_middle + grad_in
            layer_grads[layer] = jnp.concatenate(
                [
                    grad_gain_one,
                    grad_bias_one,
                    grad_query_bias,
                    grad_value_bias,
                    grad_project_bias,
                    grad_gain_two,
                    grad_bias_two,
                    grad_contract_bias,
                    grad_expand_bias,
                ]
            )
        vector_grad = vector_grad + jnp.concatenate(
            layer_grads + [grad_final_gain, grad_final_bias]
        )
        position_grad = position_grad.at[position].add(grad_state)
        group_grad = lax.all_gather(grad_state.astype(jnp.bfloat16), "fsdp", axis=0, tiled=True)
        table_grad = table_grad.at[word_local].add(
            jnp.where(word_owned[:, None], group_grad.astype(jnp.float32), 0.0)
        )
    attend_sum, project_sum, expand_sum, contract_sum, vector_sum, position_sum = (
        lax.psum_scatter(attend_grad, ("dp", "fsdp"), scatter_dimension=1, tiled=True),
        lax.psum_scatter(project_grad, ("dp", "fsdp"), scatter_dimension=1, tiled=True),
        lax.psum_scatter(expand_grad, ("dp", "fsdp"), scatter_dimension=1, tiled=True),
        lax.psum_scatter(contract_grad, ("dp", "fsdp"), scatter_dimension=1, tiled=True),
        lax.psum_scatter(vector_grad, ("dp", "fsdp"), scatter_dimension=0, tiled=True),
        lax.psum_scatter(position_grad, ("dp", "fsdp"), scatter_dimension=0, tiled=True),
    )
    table_sum = lax.psum_scatter(
        table_grad.astype(jnp.bfloat16), "dp", scatter_dimension=0, tiled=True
    ).astype(jnp.float32)
    sums = (table_sum, position_sum, attend_sum, project_sum, expand_sum, contract_sum, vector_sum)
    squares = jnp.zeros((), jnp.float32)
    for grad in sums:
        squares = squares + jnp.sum(grad * grad)
    square_total, entropy_total = lax.psum((squares, entropy_local), ("dp", "fsdp"))
    grad_norm = jnp.sqrt(square_total) / count
    factor = clip_limit / jnp.maximum(grad_norm, clip_limit)
    loss = entropy_total / count
    weights = (
        token_table,
        position_table,
        attend_weight,
        project_weight,
        expand_weight,
        contract_weight,
        vector_params,
    )
    moments = (
        table_moments,
        position_moments,
        attend_moments,
        project_moments,
        expand_moments,
        contract_moments,
        vector_moments,
    )
    decays = (decay_rate, decay_rate, decay_rate, decay_rate, decay_rate, decay_rate, 0.0)
    table_new, position_new, attend_new, project_new, expand_new, contract_new, vector_new = [
        adam_update(weight, moment, grad / count * factor, decay)
        for weight, moment, grad, decay in zip(weights, moments, sums, decays)
    ]
    return (
        loss,
        grad_norm,
        table_new[0],
        position_new[0],
        attend_new[0],
        project_new[0],
        expand_new[0],
        contract_new[0],
        vector_new[0],
        table_new[1],
        position_new[1],
        attend_new[1],
        project_new[1],
        expand_new[1],
        contract_new[1],
        vector_new[1],
        table_new[2],
        position_new[2],
        attend_new[2],
        project_new[2],
        expand_new[2],
        contract_new[2],
        vector_new[2],
    )


def solution(mesh):
    return jax.shard_map(
        shards,
        mesh=mesh,
        in_specs=(
            P(None, ("dp", "fsdp"), None),
            P(None, ("dp", "fsdp"), None),
            P(None, ("dp", "fsdp"), None),
            P(None, ("dp", "fsdp"), None),
            P(None, ("dp", "fsdp"), None),
            P(None, ("dp", "fsdp"), None),
            P(("dp", "fsdp"), None),
            P(("dp", "fsdp"), None),
            P(None, ("dp", "fsdp"), None),
            P(None, ("dp", "fsdp"), None),
            P(None, ("dp", "fsdp"), None),
            P(None, ("dp", "fsdp"), None),
            P(("dp", "fsdp")),
            P(None, ("dp", "fsdp"), None),
            P(None, ("dp", "fsdp"), None),
            P(None, None, ("dp", "fsdp"), None),
            P(None, None, ("dp", "fsdp"), None),
            P(None, None, ("dp", "fsdp"), None),
            P(None, None, ("dp", "fsdp"), None),
            P(None, ("dp", "fsdp")),
        ),
        out_specs=(
            P(),
            P(),
            P(("dp", "fsdp"), None),
            P(("dp", "fsdp"), None),
            P(None, ("dp", "fsdp"), None),
            P(None, ("dp", "fsdp"), None),
            P(None, ("dp", "fsdp"), None),
            P(None, ("dp", "fsdp"), None),
            P(("dp", "fsdp")),
            P(None, ("dp", "fsdp"), None),
            P(None, ("dp", "fsdp"), None),
            P(None, None, ("dp", "fsdp"), None),
            P(None, None, ("dp", "fsdp"), None),
            P(None, None, ("dp", "fsdp"), None),
            P(None, None, ("dp", "fsdp"), None),
            P(None, ("dp", "fsdp")),
            P(("dp", "fsdp"), None),
            P(("dp", "fsdp"), None),
            P(None, ("dp", "fsdp"), None),
            P(None, ("dp", "fsdp"), None),
            P(None, ("dp", "fsdp"), None),
            P(None, ("dp", "fsdp"), None),
            P(("dp", "fsdp")),
        ),
        check_vma=False,
    )
```

profile of v0, /device:TPU:0, one launch (start us, length us, event | category | flops | bytes accessed | tf_op | source)
XLA Modules:
  0.0 2099.2 jit_solution(10116574689707495103)
XLA Ops:
  12.3 13.6 all_gather.82
  28.4 88.6 %all-gather.16.cloned.1.call-done = bf16[12800,768]{1,0:T(8,128)(2,1)} async-done(((bf16[1600,768]{1,0:T(8,128)(2,1)}), bf16[12800,768]{1,0:T(8,128)(2,1)}) %all-gather.16.cloned.1.call-update) | async-done | bytes 19660816 | tf_op jit(solution)/shard_map/all_gather | solution.py:179
  117.0 13.6 gather_fusion
  137.1 76.2 %all_gather.84 = bf16[256,768]{1,0:T(8,128)(2,1)S(1)} all-gather(bf16[8,768]{1,0:T(8,128)(2,1)S(1)} %convert_element_type.397), channel_id=1, replica_groups=mesh['dp'=8,'fsdp'=4] {'dp','fsdp'}, dimensions={0}, use_global_device_ids=true | all-gather | bytes 405504 | tf_op jit(solution)/shard_map/all_gather | solution.py:195
  216.4 7.9 all_gather.96
  224.7 9.4 all_gather.95
  236.4 38.8 %all-reduce = bf16[19968]{0:T(1024)(128)(2,1)S(1)} all-reduce(bf16[19968]{0:T(1024)(128)(2,1)S(1)} %dynamic-update-slice.48), channel_id=1, replica_groups=mesh['dp'=8,'fsdp'=4] {'dp','fsdp'}, use_global_device_ids=true, to_apply=%add | all-reduce | flops 19968 | bytes 79872
  283.3 13.7 gather_fusion.3
  319.2 66.9 %all-gather.22.cloned.1.call-done = bf16[2,768,3072]{2,1,0:T(8,128)(2,1)} async-done(((bf16[2,24,3072]{2,1,0:T(8,128)(2,1)}), bf16[2,768,3072]{2,1,0:T(8,128)(2,1)}) %all-gather.22.cloned.1.call-update) | async-done | bytes 9437200 | tf_op jit(solution)/shard_map/all_gather | solution.py:190
  391.6 77.8 %all-gather.24.cloned.1.call-done = bf16[2,3072,768]{2,1,0:T(8,128)(2,1)} async-done(((bf16[2,96,768]{2,1,0:T(8,128)(2,1)}), bf16[2,3072,768]{2,1,0:T(8,128)(2,1)}) %all-gather.24.cloned.1.call-update) | async-done | bytes 9437200 | tf_op jit(solution)/shard_map/all_gather | solution.py:191
  487.5 9.3 fusion.361
  567.6 14.3 all_gather.97
  582.0 11.2 fusion.363
  597.1 9.4 all-gather.7
  607.1 7.7 all-gather.6
  615.3 14.5 all_gather.90
  629.8 11.2 fusion.362
  644.9 9.5 all-gather.5
  654.4 7.6 all-gather.4
  666.9 13.4 convolution_convert_fusion.12
  681.2 13.3 convolution_convert_fusion.13
  698.8 20.5 reduce-scatter.15.cloned.1.call-done
  723.0 7.9 convert_reduce_fusion
  757.0 7.4 fusion.152
  764.4 7.4 fusion.155
  782.2 7.4 fusion.140
  789.7 7.5 fusion.143
  834.0 7.6 fusion.134
  841.6 7.6 fusion.137
  973.7 11.1 pad_maximum_fusion.2
  984.9 7.2 bitcast_dynamic-update-slice_fusion.2
  992.2 7.3 fusion.16
  1007.1 7.3 pad_maximum_fusion.1
  1019.3 7.1 fusion.14
  1032.3 6.8 pad_maximum_fusion
  1044.5 8.9 fusion.15
  1054.4 18.8 fusion.332
  1073.3 32.5 %convolution_add_fusion = f32[12800,768]{1,0:T(8,128)} fusion(f32[12800,768]{1,0:T(8,128)} %fusion.332, bf16[128,768]{1,0:T(8,128)(2,1)S(1)} %copy-done.69, f32[128,12800]{1,0:T(8,128)} %copy-done.1, f32[128]{0:T(128)S(1)} %copy-done.266, f32[128]{0:T(128)S(1)} %copy-done.277, s32[128]{0:T(128)S(1)} %copy-done.260, pred[128]{0:T(512)(128)(4,1)S(1)} %copy-done.263), kind=kOutput, calls=%fused_computation.30 | convolution fusion | flops 2537881600 | bytes 85395072 | tf_op jit(solution)/shard_map/dot_general | solution.py:80
  1105.7 34.0 %scatter_custom_fusion.1 = f32[12800,768]{1,0:T(8,128)} fusion(f32[12800,768]{1,0:T(8,128)} %convolution_add_fusion, s32[1024]{0:T(1024)S(1)} %bitcast.568, bf16[1024,768]{1,0:T(8,128)(2,1)} %all-gather.26.cloned.1.call-done, f32[]{:T(128)} %constant.614.clone.1, pred[1024]{0:T(1024)(128)(4,1)S(1)} %copy-done.246), kind=kCustom, calls=%fused_computation.135 | custom fusion | flops 2359296 | bytes 40896000 | tf_op jit(solution)/shard_map/scatter-add | solution.py:406
  1139.8 33.7 %scatter_custom_fusion.3 = f32[12800,768]{1,0:T(8,128)} fusion(f32[12800,768]{1,0:T(8,128)} %scatter_custom_fusion.1, s32[1024]{0:T(1024)S(1)} %bitcast.567, bf16[1024,768]{1,0:T(8,128)(2,1)} %all-gather.28.cloned.1.call-done, f32[]{:T(128)} %constant.614.clone.1, pred[1024]{0:T(1024)(128)(4,1)S(1)} %copy-done.244), kind=kCustom, calls=%fused_computation.126 | custom fusion | flops 2359296 | bytes 40896000 | tf_op jit(solution)/shard_map/scatter-add | solution.py:406
  1173.5 20.5 convert_element_type.482
  1204.2 82.6 %reduce-scatter.25.cloned.1.call-done = f32[2,24,768]{2,1,0:T(8,128)} async-done(((f32[2,768,768]{2,1,0:T(8,128)}), f32[2,24,768]{2,1,0:T(8,128)}) %reduce-scatter.25.cloned.1.call-update) | async-done | bytes 147472 | tf_op jit(solution)/shard_map/reduce_scatter | solution.py:411
  1288.3 166.3 %reduce-scatter.23.cloned.1.call-done = f32[2,24,2304]{2,1,0:T(8,128)} async-done(((f32[2,768,2304]{2,1,0:T(8,128)}), f32[2,24,2304]{2,1,0:T(8,128)}) %reduce-scatter.23.cloned.1.call-update) | async-done | bytes 442384 | tf_op jit(solution)/shard_map/reduce_scatter | solution.py:410
  1456.3 208.6 %reduce-scatter.29.cloned.1.call-done = f32[2,96,768]{2,1,0:T(8,128)} async-done(((f32[2,3072,768]{2,1,0:T(8,128)}), f32[2,96,768]{2,1,0:T(8,128)}) %reduce-scatter.29.cloned.1.call-update) | async-done | bytes 589840 | tf_op jit(solution)/shard_map/reduce_scatter | solution.py:413
  1666.8 208.9 %reduce-scatter.27.cloned.1.call-done = f32[2,24,3072]{2,1,0:T(8,128)} async-done(((f32[2,768,3072]{2,1,0:T(8,128)}), f32[2,24,3072]{2,1,0:T(8,128)}) %reduce-scatter.27.cloned.1.call-update) | async-done | bytes 589840 | tf_op jit(solution)/shard_map/reduce_scatter | solution.py:412
  1877.5 130.8 %reduce-scatter.19.cloned.1.call-done = bf16[1600,768]{1,0:T(8,128)(2,1)} async-done(((bf16[12800,768]{1,0:T(8,128)(2,1)}), bf16[1600,768]{1,0:T(8,128)(2,1)}) %reduce-scatter.19.cloned.1.call-update) | async-done | bytes 2457616 | tf_op jit(solution)/shard_map/reduce_scatter | solution.py:417
  2016.4 39.3 %all-reduce.2 = (f32[]{:T(128)}, f32[]{:T(128)}, f32[]{:T(128)}) all-reduce(f32[]{:T(128)S(6)} %sub.516, f32[]{:T(128)S(6)} %convert_element_type.449, f32[]{:T(128)S(6)} %add.1137), channel_id=1, replica_groups=mesh['dp'=8,'fsdp'=4] {'dp','fsdp'}, use_global_device_ids=true, to_apply=%region_54.58 | all-reduce | flops 3 | bytes 24 | tf_op jit(solution)/shard_map/psum | solution.py:424
  2075.4 9.2 fusion.330
  (1010 shorter events, 428.1 us)
Async XLA Ops:
  8.0 108.9 %all-gather.16.cloned.1.call-start = ((), (), s32[]{:S(2)}) async-start(), calls=%async_computation.10 | async-start | bytes 22118400 | tf_op jit(solution)/shard_map/all_gather | solution.py:179
  12.2 286.7 %reduce-scatter.11.cloned.1.call-start = ((), (), s32[]{:S(2)}) async-start(), calls=%async_computation.11 | async-start | bytes 1966080 | tf_op jit(solution)/shard_map/reduce_scatter | solution.py:217
  27.8 102.8 %copy-start.245 = (pred[1024]{0:T(1024)(128)(4,1)}, pred[1024]{0:T(1024)(128)(4,1)S(1)}, u32[]{:S(2)}) copy-start(pred[1024]{0:T(1024)(128)(4,1)S(1)} %get-tuple-element.476) | copy-start | bytes 3076
  132.4 169.2 %all-gather.18.cloned.1.call-start = ((), (), s32[]{:S(2)}) async-start(), calls=%async_computation.12 | async-start | bytes 7299072 | tf_op jit(solution)/shard_map/all_gather | solution.py:188
  133.2 183.6 %all-gather.20.cloned.1.call-start = ((), (), s32[]{:S(2)}) async-start(), calls=%async_computation.13 | async-start | bytes 2433024 | tf_op jit(solution)/shard_map/all_gather | solution.py:189
  133.9 252.2 %all-gather.22.cloned.1.call-start = ((), (), s32[]{:S(2)}) async-start(), calls=%async_computation.14 | async-start | bytes 9732096 | tf_op jit(solution)/shard_map/all_gather | solution.py:190
  134.8 334.7 %all-gather.24.cloned.1.call-start = ((), (), s32[]{:S(2)}) async-start(), calls=%async_computation.15 | async-start | bytes 9732096 | tf_op jit(solution)/shard_map/all_gather | solution.py:191
  135.6 374.2 %reduce-scatter.13.cloned.1.call-start = ((), (), s32[]{:S(2)}) async-start(), calls=%async_computation.16 | async-start | bytes 1966080 | tf_op jit(solution)/shard_map/reduce_scatter | solution.py:217
  137.0 143.7 %copy-start.208 = (s32[256]{0:T(256)}, s32[256]{0:T(256)S(1)}, u32[]{:S(2)}) copy-start(s32[256]{0:T(256)S(1)} %select_reduce_fusion.4) | copy-start | bytes 3076
  213.3 62.0 %copy-start.287 = (s32[2,1,32]{2,1,0:T(1,128)S(1)}, s32[2,1,32]{2,1,0:T(1,128)}, u32[]{:S(2)}) copy-start(s32[2,1,32]{2,1,0:T(1,128)} %param.65) | copy-start | bytes 772
  213.3 70.0 %copy-start.222 = (s32[1024]{0:T(1024)S(1)}, s32[1024]{0:T(1024)}, u32[]{:S(2)}) copy-start(s32[1024]{0:T(1024)} %get-tuple-element.569) | copy-start | bytes 12292
  214.5 102.4 %copy-start.31 = (bf16[256,768]{1,0:T(8,128)(2,1)}, bf16[256,768]{1,0:T(8,128)(2,1)S(1)}, u32[]{:S(2)}) copy-start(bf16[256,768]{1,0:T(8,128)(2,1)S(1)} %gather_fusion.1) | copy-start | bytes 1179652
  277.1 235.4 %copy-start.134 = (f32[768]{0:T(1024)}, f32[768]{0:T(1024)S(1)}, u32[]{:S(2)}) copy-start(f32[768]{0:T(1024)S(1)} %get-tuple-element.467) | copy-start | bytes 9220
  277.1 262.9 %copy-start.132 = (f32[768]{0:T(1024)}, f32[768]{0:T(1024)S(1)}, u32[]{:S(2)}) copy-start(f32[768]{0:T(1024)S(1)} %get-tuple-element.459) | copy-start | bytes 9220
  277.1 277.2 %copy-start.129 = (f32[768]{0:T(1024)}, f32[768]{0:T(1024)S(1)}, u32[]{:S(2)}) copy-start(f32[768]{0:T(1024)S(1)} %get-tuple-element.455) | copy-start | bytes 9220
  298.8 400.0 %reduce-scatter.17.cloned.1.call-start = ((), (), s32[]{:S(2)}) async-start(), calls=%async_computation.19 | async-start | bytes 245760 | tf_op jit(solution)/shard_map/reduce_scatter | solution.py:308
  316.8 69.3 %copy-start.138 = (f32[768]{0:T(1024)S(1)}, f32[768]{0:T(1024)}, u32[]{:S(2)}) copy-start(f32[768]{0:T(1024)} %get-tuple-element.464) | copy-start | bytes 9220
  316.8 69.3 %copy-start.239 = (f32[3072]{0:T(1024)S(1)}, f32[3072]{0:T(1024)}, u32[]{:S(2)}) copy-start(f32[3072]{0:T(1024)} %get-tuple-element.474) | copy-start | bytes 36868
  318.9 150.5 %copy-start.42 = (f32[256,768]{1,0:T(8,128)}, f32[256,768]{1,0:T(8,128)S(1)}, u32[]{:S(2)}) copy-start(f32[256,768]{1,0:T(8,128)S(1)} %get-tuple-element.537) | copy-start | bytes 2359300
  318.9 72.7 %copy-start.169 = (f32[256]{0:T(256)}, f32[256]{0:T(256)S(1)}, u32[]{:S(2)}) copy-start(f32[256]{0:T(256)S(1)} %broadcast_multiply_fusion.22) | copy-start | bytes 3076
  319.2 72.5 %copy-start.216 = (f32[256]{0:T(256)}, f32[256]{0:T(256)S(1)}, u32[]{:S(2)}) copy-start(f32[256]{0:T(256)S(1)} %add_rsqrt_fusion.6) | copy-start | bytes 3076
  386.1 83.3 %copy-start.284 = (f32[768]{0:T(1024)S(1)}, f32[768]{0:T(1024)}, u32[]{:S(2)}) copy-start(f32[768]{0:T(1024)} %get-tuple-element.465) | copy-start | bytes 9220
  509.5 57.3 %copy-start.256 = (f32[32]{0:T(128)}, f32[32]{0:T(128)S(1)}, u32[]{:S(2)}) copy-start(f32[32]{0:T(128)S(1)} %broadcast_multiply_fusion.29) | copy-start | bytes 388
  509.8 57.1 %copy-start.272 = (f32[32]{0:T(128)}, f32[32]{0:T(128)S(1)}, u32[]{:S(2)}) copy-start(f32[32]{0:T(128)S(1)} %add_rsqrt_fusion.9) | copy-start | bytes 388
  554.0 195.2 %copy-start.4 = (f32[256,768]{1,0:T(8,128)}, f32[256,768]{1,0:T(8,128)S(1)}, u32[]{:S(2)}) copy-start(f32[256,768]{1,0:T(8,128)S(1)} %get-tuple-element.533) | copy-start | bytes 2359300
  680.3 38.9 %reduce-scatter.15.cloned.1.call-start = ((), (), s32[]{:S(2)}) async-start(), calls=%async_computation.17 | async-start | bytes 245760 | tf_op jit(solution)/shard_map/reduce_scatter | solution.py:308
  681.1 38.2 %copy-start.153 = (f32[768]{0:T(1024)S(1)}, f32[768]{0:T(1024)}, u32[]{:S(2)}) copy-start(f32[768]{0:T(1024)} %get-tuple-element.471) | copy-start | bytes 9220
  681.1 38.2 %copy-start.182 = (pred[32]{0:T(512)(128)(4,1)S(1)}, pred[32]{0:T(512)(128)(4,1)}, u32[]{:S(2)}) copy-start(pred[32]{0:T(512)(128)(4,1)} %get-tuple-element.514) | copy-start | bytes 100
  681.1 38.2 %copy-start.184 = (pred[32]{0:T(512)(128)(4,1)S(1)}, pred[32]{0:T(512)(128)(4,1)}, u32[]{:S(2)}) copy-start(pred[32]{0:T(512)(128)(4,1)} %get-tuple-element.401) | copy-start | bytes 100
  681.1 38.1 %copy-start.257 = (f32[32]{0:T(128)S(1)}, f32[32]{0:T(128)}, u32[]{:S(2)}) copy-start(f32[32]{0:T(128)} %copy-done.256) | copy-start | bytes 388
  681.1 38.1 %copy-start.259 = (f32[32]{0:T(128)S(1)}, f32[32]{0:T(128)}, u32[]{:S(2)}) copy-start(f32[32]{0:T(128)} %copy-done.258) | copy-start | bytes 388
  681.1 38.1 %copy-start.273 = (f32[32]{0:T(128)S(1)}, f32[32]{0:T(128)}, u32[]{:S(2)}) copy-start(f32[32]{0:T(128)} %copy-done.272) | copy-start | bytes 388
  681.2 38.1 %copy-start.275 = (f32[32]{0:T(128)S(1)}, f32[32]{0:T(128)}, u32[]{:S(2)}) copy-start(f32[32]{0:T(128)} %copy-done.274) | copy-start | bytes 388
  694.5 411.2 %all-gather.26.cloned.1.call-start = ((), (), s32[]{:S(2)}) async-start(), calls=%async_computation.18 | async-start | bytes 1966080 | tf_op jit(solution)/shard_map/all_gather | solution.py:405
  818.5 36.1 %copy-start.36 = (f32[256,768]{1,0:T(8,128)}, f32[256,768]{1,0:T(8,128)S(1)}, u32[]{:S(2)}) copy-start(f32[256,768]{1,0:T(8,128)S(1)} %get-tuple-element.390) | copy-start | bytes 2359300
  887.2 252.6 %all-gather.28.cloned.1.call-start = ((), (), s32[]{:S(2)}) async-start(), calls=%async_computation.20 | async-start | bytes 1966080 | tf_op jit(solution)/shard_map/all_gather | solution.py:405
  920.6 280.8 %all-reduce.5.cloned.1.call-start = ((), (), s32[]{:S(2)}) async-start(), calls=%async_computation.27 | async-start | bytes 163840
  944.1 258.7 %reduce-scatter.21.cloned.1.call-start = ((), (), s32[]{:S(2)}) async-start(), calls=%async_computation.22 | async-start | bytes 811008 | tf_op jit(solution)/shard_map/reduce_scatter | solution.py:415
  952.7 334.0 %reduce-scatter.25.cloned.1.call-start = ((), (), s32[]{:S(2)}) async-start(), calls=%async_computation.24 | async-start | bytes 4866048 | tf_op jit(solution)/shard_map/reduce_scatter | solution.py:411
  962.8 491.7 %reduce-scatter.23.cloned.1.call-start = ((), (), s32[]{:S(2)}) async-start(), calls=%async_computation.23 | async-start | bytes 14598144 | tf_op jit(solution)/shard_map/reduce_scatter | solution.py:410
  999.5 665.4 %reduce-scatter.29.cloned.1.call-start = ((), (), s32[]{:S(2)}) async-start(), calls=%async_computation.26 | async-start | bytes 19464192 | tf_op jit(solution)/shard_map/reduce_scatter | solution.py:413
  1026.6 849.1 %reduce-scatter.27.cloned.1.call-start = ((), (), s32[]{:S(2)}) async-start(), calls=%async_computation.25 | async-start | bytes 19464192 | tf_op jit(solution)/shard_map/reduce_scatter | solution.py:412
  1053.5 954.8 %reduce-scatter.19.cloned.1.call-start = ((), (), s32[]{:S(2)}) async-start(), calls=%async_computation.21 | async-start | bytes 22118400 | tf_op jit(solution)/shard_map/reduce_scatter | solution.py:417
  1194.1 822.3 %copy-start.271 = (f32[2,624]{1,0:T(2,128)S(1)}, f32[2,624]{1,0:T(2,128)}, u32[]{:S(2)}) copy-start(f32[2,624]{1,0:T(2,128)} %param.81) | copy-start | bytes 14980
  1194.1 863.0 %copy-start.213 = (f32[624]{0:T(1024)S(1)}, f32[624]{0:T(1024)}, u32[]{:S(2)}) copy-start(f32[624]{0:T(1024)} %param.74) | copy-start | bytes 7492
  1194.1 867.0 %copy-start.64 = (f32[2,96,768]{2,1,0:T(8,128)S(1)}, f32[2,96,768]{2,1,0:T(8,128)}, u32[]{:S(2)}) copy-start(f32[2,96,768]{2,1,0:T(8,128)} %param.73) | copy-start | bytes 1769476
  1194.2 867.0 %copy-start.120 = (f32[2,2,96,768]{3,2,1,0:T(8,128)S(1)}, f32[2,2,96,768]{3,2,1,0:T(8,128)}, u32[]{:S(2)}) copy-start(f32[2,2,96,768]{3,2,1,0:T(8,128)} %param.80) | copy-start | bytes 3538948
  1664.9 396.3 %copy-start.67 = (f32[2,96,768]{2,1,0:T(8,128)S(1)}, f32[2,96,768]{2,1,0:T(8,128)}, u32[]{:S(2)}) copy-start(f32[2,96,768]{2,1,0:T(8,128)} %reduce-scatter.29.cloned.1.call-done) | copy-start | bytes 1769476
  (287 other events, 1853.0 us)
Sparse Core Ops, SparseCore 0:
  12.3 104.6 all-gather.15
  132.5 42.2 reduce-scatter.10
  298.9 42.3 reduce-scatter.12
  680.5 18.2 reduce-scatter.16
  701.4 17.7 reduce-scatter.14
  887.3 35.2 all-gather.25
  924.2 35.9 all-gather.27
Sparse Core Ops, SparseCore 1:
  136.5 90.7 all-gather.17
  230.8 55.9 all-gather.19
  290.3 95.7 all-gather.21
  389.8 79.6 all-gather.23
  944.2 125.7 all-reduce.4
  1075.7 98.4 reduce-scatter.20
  1180.0 106.7 reduce-scatter.24
  1292.6 161.9 reduce-scatter.22
  1460.8 204.0 reduce-scatter.28
  1671.3 204.3 reduce-scatter.26
  1879.2 129.0 reduce-scatter.18
where the time goes:
time: 2110 us; the launch traced here: 2100 us
  waiting for transfers between devices  1050 us (50%)
  matrix products  396 us (19%)
  blocking collectives  248 us (12%)
  other arithmetic  235 us (11%)
  local copies, waits for them, and re-layouts  130 us (6%)
  between operations  32.7 us (2%)
    reduce_scatter x1, waiting for transfers between devices, shards(): lax.psum_scatter(expand_grad, ('dp', 'fsdp'), scatter_dimension=1, tiled=...  209 us
    reduce_scatter x1, waiting for transfers between devices, shards(): lax.psum_scatter(contract_grad, ('dp', 'fsdp'), scatter_dimension=1, tile...  209 us
    reduce_scatter x1, waiting for transfers between devices, shards(): lax.psum_scatter(attend_grad, ('dp', 'fsdp'), scatter_dimension=1, tiled=...  166 us
    reduce_scatter x1, waiting for transfers between devices, shards(): lax.psum_scatter(table_grad.astype(jnp.bfloat16), 'dp', scatter_dimension...  131 us
    dot_general x18, matrix products, outer_sum(): lax.dot_general(left, right, (((0,), (0,)), ((), ())), preferred_element_...  121 us
    all_gather x1, waiting for transfers between devices, shards(): lax.all_gather(token_table.astype(jnp.bfloat16), 'dp', axis=0, tiled=True)  88.6 us
    reduce_scatter x1, waiting for transfers between devices, shards(): lax.psum_scatter(project_grad, ('dp', 'fsdp'), scatter_dimension=1, tiled...  82.6 us
    dot_general x18, matrix products, times_transpose(): lax.dot_general(left, right, (((1,), (1,)), ((), ())), preferred_element_...  82.4 us
  transfers between devices with their start and end apart: 18, of which 10 were waited for; matrix products, arithmetic and copies ran while one was open for 20% of the time, Pallas kernels for 0%

commit v1 on v0

v1 whole, which is shorter than its diff:
```python
import functools

import jax
import jax.numpy as jnp
from jax import lax
from jax.experimental import pallas as pl
from jax.sharding import PartitionSpec as P

HEADS = 12


norm_eps = 1e-05
gelu_scale = 0.7978845608
gelu_cubic = 0.044715
beta_one = 0.5
beta_two = 0.5
learn_rate = 0.03
decay_rate = 0.1
adam_eps = 1e-08
clip_limit = 0.25
adam_step = 3
masked_score = -1e30


def positions_of(lengths, order, slot):
    places = jnp.arange(lengths.shape[0], dtype=jnp.int32)
    place = jnp.sum(places[None, :] * (order[None, :] == places[:, None]).astype(jnp.int32), axis=1)
    offset = jnp.sum(lengths[None, :] * (place[None, :] < place[:, None]).astype(jnp.int32), axis=1)
    ends = jnp.cumsum(lengths)
    starts = ends - lengths
    stored = jnp.arange(slot, dtype=jnp.int32)
    document = jnp.sum((stored[:, None] >= ends[None, :]).astype(jnp.int32), axis=1)
    onehot = (document[:, None] == places[None, :]).astype(jnp.int32)
    position = stored + jnp.sum(onehot * (offset - starts)[None, :], axis=1)
    return (position, document)


def norm_forward(state, gain, bias):
    average = jnp.mean(state, axis=-1, keepdims=True)
    centered = state - average
    inverse = lax.rsqrt(jnp.mean(centered * centered, axis=-1, keepdims=True) + norm_eps)
    scaled = centered * inverse
    return (scaled * gain + bias, scaled, inverse)


def norm_backward(grad, scaled, inverse, gain):
    shaped = grad * gain
    inner = (
        shaped
        - jnp.mean(shaped, axis=-1, keepdims=True)
        - scaled * jnp.mean(shaped * scaled, axis=-1, keepdims=True)
    )
    return (inner * inverse, jnp.sum(grad * scaled, axis=0), jnp.sum(grad, axis=0))


def gelu_tanh(value):
    return 0.5 * value * (1.0 + jnp.tanh(gelu_scale * (value + gelu_cubic * value * value * value)))


def gelu_slope(value):
    bent = jnp.tanh(gelu_scale * (value + gelu_cubic * value * value * value))
    return 0.5 * (1.0 + bent) + 0.5 * value * (1.0 - bent * bent) * gelu_scale * (
        1.0 + 3.0 * gelu_cubic * value * value
    )


def outer_sum(left, right):
    return lax.dot_general(
        left, right, (((0,), (0,)), ((), ())), preferred_element_type=jnp.float32
    )


def times_transpose(left, right):
    return lax.dot_general(
        left, right, (((1,), (1,)), ((), ())), preferred_element_type=jnp.float32
    )


BOTH = ("dp", "fsdp")


def swapped(value, axis, flip):
    size = lax.axis_size(axis)
    return lax.ppermute(value, axis, [(index, index ^ flip) for index in range(size)])


def spread(value):
    count = lax.axis_size("dp") * lax.axis_size("fsdp")
    return lax.all_to_all(jnp.broadcast_to(value[None], (count,) + value.shape), BOTH, 0, 0, tiled=True)


def relative_offsets():
    quads, fsdp = lax.axis_size("dp") // 2, lax.axis_size("fsdp")
    return jnp.array(
        [
            (quad * 2 + core) * fsdp + deep
            for core in range(2)
            for quad in range(quads)
            for deep in range(fsdp)
        ],
        jnp.int32,
    )


def gather_rows(rows):
    quads, fsdp = lax.axis_size("dp") // 2, lax.axis_size("fsdp")
    held = jnp.stack([rows] + [swapped(rows, "fsdp", flip) for flip in range(1, fsdp)])
    held = jnp.stack([held] + [swapped(held, "dp", 2 * flip) for flip in range(1, quads)])
    held = jnp.stack([held, swapped(held, "dp", 1)])
    return held.reshape((-1,) + rows.shape[1:])


def sum_low(pieces):
    total = pieces[0].astype(jnp.float32)
    for piece in pieces[1:]:
        total = total + piece.astype(jnp.float32)
    return total


def scatter_rows(partial):
    quads, fsdp = lax.axis_size("dp") // 2, lax.axis_size("fsdp")
    width = partial.shape[1]
    part = partial.astype(jnp.bfloat16).reshape(2, quads, fsdp, -1, width)
    part = sum_low([part[0], swapped(part[1], "dp", 1)]).astype(jnp.bfloat16)
    part = sum_low(
        [part[0]] + [swapped(part[flip], "dp", 2 * flip) for flip in range(1, quads)]
    ).astype(jnp.bfloat16)
    return sum_low([part[0]] + [swapped(part[flip], "fsdp", flip) for flip in range(1, fsdp)])


def take_one(value, index, axis):
    return lax.dynamic_index_in_dim(value, index, axis, keepdims=False)


def send_core(pieces):
    quads, fsdp = lax.axis_size("dp") // 2, lax.axis_size("fsdp")
    core = lax.axis_index("dp") % 2
    views = [piece.reshape((quads, 2, fsdp) + piece.shape[1:]) for piece in pieces]

    def half(which):
        return jnp.concatenate([take_one(view, which, 1) for view in views], axis=2)

    return [half(core), swapped(half(1 - core), "dp", 1)]


def send_quads(parts):
    quads = lax.axis_size("dp") // 2
    quad = lax.axis_index("dp") // 2
    part = sum_low(parts).astype(jnp.bfloat16)
    return [take_one(part, quad, 0)] + [
        swapped(take_one(part, quad ^ flip, 0), "dp", 2 * flip) for flip in range(1, quads)
    ]


def send_deep(parts):
    fsdp, deep = lax.axis_size("fsdp"), lax.axis_index("fsdp")
    part = sum_low(parts).astype(jnp.bfloat16)
    return [take_one(part, deep, 0)] + [
        swapped(take_one(part, deep ^ flip, 0), "fsdp", flip) for flip in range(1, fsdp)
    ]


def lanes_to_rows(value, devices, width):
    view = value.reshape(devices, -1, value.shape[1])
    return [view[:, :, at : at + width] for at in range(0, value.shape[1], width)]


def rows_to_lanes(value, parts):
    rows = value.shape[0] // parts
    return jnp.concatenate([value[index * rows : (index + 1) * rows] for index in range(parts)], axis=1)


def dotted(left, right, left_at, right_at):
    return lax.dot_general(
        left, right, (((left_at,), (right_at,)), ((), ())), preferred_element_type=jnp.float32
    )


def allowed_of(row_ref, column_ref):
    slot = row_ref.shape[2]
    here = lax.broadcasted_iota(jnp.int32, (slot, slot), 0)
    there = lax.broadcasted_iota(jnp.int32, (slot, slot), 1)
    return (column_ref[0] == row_ref[0]) & (there <= here)


def attend_kernel(head, row_ref, column_ref, mixed_ref, attended_ref, log_ref):
    slot, width = attended_ref.shape
    allowed = allowed_of(row_ref, column_ref)
    for base in range(0, width, 2 * head):
        query, keys, values = [
            mixed_ref[:, part * width + base : part * width + base + 2 * head] for part in range(3)
        ]
        results, logs = [], []
        for at in (0, head):
            raw = dotted(query[:, at : at + head], keys[:, at : at + head], 1, 1)
            scores = jnp.where(allowed, raw * head ** (-0.5), masked_score)
            peak = jnp.max(scores, axis=1, keepdims=True)
            log_total = peak + jnp.log(jnp.sum(jnp.exp(scores - peak), axis=1, keepdims=True))
            probs = jnp.exp(scores - log_total).astype(jnp.bfloat16)
            results.append(dotted(probs, values[:, at : at + head], 1, 0))
            logs.append(jnp.broadcast_to(log_total, (slot, head)))
        attended_ref[:, base : base + 2 * head] = jnp.concatenate(results, axis=1).astype(jnp.bfloat16)
        log_ref[:, base : base + 2 * head] = jnp.concatenate(logs, axis=1)


def attend_back_kernel(head, row_ref, column_ref, mixed_ref, log_ref, grad_ref, out_ref):
    width = grad_ref.shape[1]
    allowed = allowed_of(row_ref, column_ref)
    scale = head ** (-0.5)
    for base in range(0, width, 2 * head):
        query, keys, values = [
            mixed_ref[:, part * width + base : part * width + base + 2 * head] for part in range(3)
        ]
        grads = grad_ref[:, base : base + 2 * head]
        logs = log_ref[:, base : base + 2 * head]
        parts = [[], [], []]
        for at in (0, head):
            q, k, v, g = [value[:, at : at + head] for value in (query, keys, values, grads)]
            scores = jnp.where(allowed, dotted(q, k, 1, 1) * scale, masked_score)
            probs = jnp.exp(scores - logs[:, at : at + 1])
            parts[2].append(dotted(probs.astype(jnp.bfloat16), g, 0, 0))
            slopes = dotted(g, v, 1, 1)
            slopes = probs * (slopes - jnp.sum(probs * slopes, axis=1, keepdims=True))
            slopes = (slopes * scale).astype(jnp.bfloat16)
            parts[0].append(dotted(slopes, k, 1, 0))
            parts[1].append(dotted(slopes, q, 0, 0))
        for which in range(3):
            out_ref[:, which * width + base : which * width + base + 2 * head] = jnp.concatenate(
                parts[which], axis=1
            ).astype(jnp.bfloat16)


def attend_specs(document, width):
    _, slot = document.shape
    return [
        pl.BlockSpec((1, 1, slot), lambda m: (m, 0, 0)),
        pl.BlockSpec((1, slot, 1), lambda m: (m, 0, 0)),
        pl.BlockSpec((slot, 3 * width), lambda m: (m, 0)),
    ], pl.BlockSpec((slot, width), lambda m: (m, 0))


def attend_cost(document, width, dots):
    micro, slot = document.shape
    return pl.CostEstimate(
        flops=2 * dots * micro * slot * slot * width,
        transcendentals=2 * micro * slot * slot * HEADS,
        bytes_accessed=16 * micro * slot * width,
    )


def attend_forward(mixed, document):
    rows, width = mixed.shape[0], mixed.shape[1] // 3
    specs, thin = attend_specs(document, width)
    return pl.pallas_call(
        functools.partial(attend_kernel, width // HEADS),
        grid=(document.shape[0],),
        in_specs=specs,
        out_specs=[thin, thin],
        out_shape=[
            jax.ShapeDtypeStruct((rows, width), jnp.bfloat16),
            jax.ShapeDtypeStruct((rows, width), jnp.float32),
        ],
        cost_estimate=attend_cost(document, width, 2),
        name="attend_forward",
    )(document[:, None, :], document[:, :, None], mixed)


def attend_backward(mixed, document, log_total, grad_attended):
    width = mixed.shape[1] // 3
    specs, thin = attend_specs(document, width)
    return pl.pallas_call(
        functools.partial(attend_back_kernel, width // HEADS),
        grid=(document.shape[0],),
        in_specs=specs + [thin, thin],
        out_specs=specs[2],
        out_shape=jax.ShapeDtypeStruct(mixed.shape, jnp.bfloat16),
        cost_estimate=attend_cost(document, width, 5),
        name="attend_backward",
    )(document[:, None, :], document[:, :, None], mixed, log_total, grad_attended)


def layer_pieces(vectors, base, width, hidden_width):
    pieces = [vectors[base + index * width : base + (index + 1) * width] for index in range(8)]
    return pieces + [vectors[base + 8 * width : base + 8 * width + hidden_width]]


def adam_update(weight, moments, grad, decay):
    first = beta_one * moments[0] + (1.0 - beta_one) * grad
    root = jnp.sqrt(beta_two * moments[1] * moments[1] + (1.0 - beta_two) * grad * grad)
    rise = (
        first / (1.0 - beta_one**adam_step) / (root / (1.0 - beta_two**adam_step) ** 0.5 + adam_eps)
    )
    fresh = weight - learn_rate * (rise + decay * weight)
    return (fresh, jnp.stack([first, root]), fresh.astype(jnp.bfloat16))


def shards(
    token_ids,
    doc_lengths,
    doc_order,
    loss_slots,
    targets,
    loss_mask,
    token_table,
    position_table,
    attend_weight,
    project_weight,
    expand_weight,
    contract_weight,
    vector_params,
    table_moments,
    position_moments,
    attend_moments,
    project_moments,
    expand_moments,
    contract_moments,
    vector_moments,
):
    low = jnp.bfloat16
    fsdp = lax.axis_size("fsdp")
    devices = lax.axis_size("dp") * fsdp
    me = lax.axis_index("dp") * fsdp + lax.axis_index("fsdp")
    micro_count, _, slot = token_ids.shape
    loss_rows = loss_slots.shape[2]
    tokens = micro_count * slot
    width = token_table.shape[1]
    layers, row_share = attend_weight.shape[:2]
    hidden_width = expand_weight.shape[2]
    hidden_share = contract_weight.shape[1]
    rows_each = token_table.shape[0]
    position_share = position_table.shape[0]
    vector_share = vector_params.shape[0]
    block = 8 * width + hidden_width
    vector_rows = -(-vector_share // width)
    small_rows = position_share + vector_rows

    words = token_ids.reshape(tokens)
    owner = words // rows_each
    local = words % rows_each
    earlier = jnp.arange(tokens)[None, :] < jnp.arange(tokens)[:, None]
    first = jnp.logical_not(jnp.any((words[:, None] == words[None, :]) & earlier, axis=1))
    rank = jnp.sum(
        (first[None, :] & (owner[:, None] == owner[None, :]) & (words[None, :] < words[:, None])).astype(jnp.int32),
        axis=1,
    )
    slots_each = max(16, 2 * tokens // devices)
    slots_all = devices * slots_each

    def seats(turn):
        within = rank - turn * slots_each
        return jnp.where((within >= 0) & (within < slots_each), owner * slots_each + within, -1)

    def requests(turn, *marks):
        seat = seats(turn)
        asked = jnp.max(
            jnp.where(seat[None, :] == jnp.arange(slots_all)[:, None], local[None, :], -1), axis=1
        )
        table = jnp.concatenate(
            [asked.reshape(devices, slots_each), jnp.broadcast_to(jnp.max(rank), (devices, 1))]
            + [jnp.broadcast_to(mark.reshape(1, -1), (devices, mark.size)) for mark in marks],
            axis=1,
        )
        return lax.all_to_all(table, BOTH, 0, 0, tiled=True)

    def wanted_of(heard):
        asked = heard[:, :slots_each].reshape(-1)
        return (asked[:, None] == jnp.arange(rows_each)[None, :]).astype(low)

    def seat_matrix(turn):
        return (seats(turn)[:, None] == jnp.arange(slots_all)[None, :]).astype(low)

    table_b = token_table.astype(low)

    def looked_up(turn, heard):
        rows = jnp.dot(wanted_of(heard), table_b, preferred_element_type=jnp.float32).astype(low)
        rows = lax.all_to_all(rows, BOTH, 0, 0, tiled=True)
        return jnp.dot(seat_matrix(turn), rows, preferred_element_type=jnp.float32)

    heard_first = requests(0, targets, loss_mask)
    turns = jnp.max(heard_first[:, slots_each]) // slots_each + 1
    embedded = looked_up(0, heard_first)
    _, embedded = lax.while_loop(
        lambda carry: carry[0] < turns,
        lambda carry: (carry[0] + 1, carry[1] + looked_up(carry[0], requests(carry[0]))),
        (jnp.int32(1), embedded),
    )

    small = jnp.concatenate(
        [
            position_table.astype(low),
            jnp.pad(vector_params.astype(low), (0, vector_rows * width - vector_share)).reshape(vector_rows, width),
        ]
    )
    mixed_share = [
        jnp.concatenate(
            [attend_weight[layer], project_weight[layer], expand_weight[layer]], axis=1
        ).astype(low)
        for layer in range(layers)
    ]
    small_all = spread(small).reshape(devices, small_rows, width)
    mixed_all = [lax.all_gather(share, BOTH, axis=0, tiled=True) for share in mixed_share]
    contract_all = lax.all_gather(contract_weight.astype(low), BOTH, axis=1, tiled=True)
    attend_all = [share[:, : 3 * width] for share in mixed_all]
    project_all = [share[:, 3 * width : 4 * width] for share in mixed_all]
    expand_all = [share[:, 4 * width :] for share in mixed_all]
    position_all = small_all[:, :position_share].reshape(-1, width)
    vectors_f = (
        small_all[:, position_share:].reshape(devices, -1)[:, :vector_share].reshape(-1).astype(jnp.float32)
    )

    order = me ^ relative_offsets()
    marks = jnp.take(heard_first[:, slots_each + 1 :].reshape(devices, 2, -1), order, axis=0)
    target_local = marks[:, 0].reshape(-1) - me * rows_each
    valid = marks[:, 1].reshape(-1).astype(jnp.float32)

    placed = [positions_of(doc_lengths[micro, 0], doc_order[micro, 0], slot) for micro in range(micro_count)]
    position = jnp.concatenate([pair[0] for pair in placed])
    document = jnp.stack([pair[1] for pair in placed])
    stored = jnp.arange(slot, dtype=jnp.int32)
    position_hot = (position[:, None] == stored[None, :]).astype(low)
    state = embedded + jnp.dot(position_hot, position_all, preferred_element_type=jnp.float32)

    saved = []
    for layer in range(layers):
        (
            gain_one,
            bias_one,
            query_bias,
            value_bias,
            project_bias,
            gain_two,
            bias_two,
            contract_bias,
            expand_bias,
        ) = layer_pieces(vectors_f, layer * block, width, hidden_width)
        normed, scaled_one, inverse_one = norm_forward(state, gain_one, bias_one)
        normed_b = normed.astype(low)
        mixed = jnp.dot(
            normed_b, attend_all[layer], preferred_element_type=jnp.float32
        ) + jnp.concatenate([query_bias, jnp.zeros_like(query_bias), value_bias])
        mixed_b = mixed.astype(low)
        attended_b, log_total = attend_forward(mixed_b, document)
        middle = (
            state
            + jnp.dot(attended_b, project_all[layer], preferred_element_type=jnp.float32)
            + project_bias
        )
        normed_two, scaled_two, inverse_two = norm_forward(middle, gain_two, bias_two)
        normed_two_b = normed_two.astype(low)
        before = (
            jnp.dot(normed_two_b, expand_all[layer], preferred_element_type=jnp.float32)
            + expand_bias
        )
        active_b = gelu_tanh(before).astype(low)
        state = (
            middle
            + jnp.dot(active_b, contract_all[layer], preferred_element_type=jnp.float32)
            + contract_bias
        )
        saved.append(
            (
                normed_b,
                scaled_one,
                inverse_one,
                mixed_b,
                log_total,
                attended_b,
                scaled_two,
                inverse_two,
                normed_two_b,
                before,
                active_b,
            )
        )

    top = layers * block
    final_gain = vectors_f[top : top + width]
    final_bias = vectors_f[top + width : top + 2 * width]
    slots = (loss_slots[:, 0] + slot * jnp.arange(micro_count, dtype=jnp.int32)[:, None]).reshape(-1)
    final, scaled_final, inverse_final = norm_forward(
        jnp.take(state, slots, axis=0), final_gain, final_bias
    )
    rows_all = gather_rows(final.astype(low))
    logits = times_transpose(rows_all, table_b)
    hit = jnp.arange(rows_each, dtype=jnp.int32)[None, :] == target_local[:, None]
    peak = jnp.max(logits, axis=1)
    totals = jnp.sum(jnp.exp(logits - peak[:, None]), axis=1)
    chosen = jnp.sum(jnp.where(hit, logits, 0.0), axis=1)
    stats = jnp.stack([peak.reshape(devices, -1), totals.reshape(devices, -1)], axis=1)
    inverse = jnp.argsort(order)
    stats_all = spread(jnp.take(stats, inverse, axis=0).reshape(devices, -1))
    stats_all = stats_all.reshape(devices, devices, 2, -1)
    peak_all = jnp.max(stats_all[:, :, 0], axis=0)
    totals_all = jnp.sum(stats_all[:, :, 1] * jnp.exp(stats_all[:, :, 0] - peak_all[None]), axis=0)
    log_rows = jnp.take(peak_all + jnp.log(totals_all), order, axis=0).reshape(-1)
    own = micro_count * loss_rows
    entropy_local = jnp.sum(log_rows[:own] * valid[:own]) - jnp.sum(chosen * valid)
    grad_logits = (
        (jnp.exp(logits - log_rows[:, None]) - hit.astype(jnp.float32)) * valid[:, None]
    ).astype(low)
    grad_final = scatter_rows(jnp.dot(grad_logits, table_b, preferred_element_type=jnp.float32))
    table_grad = outer_sum(grad_logits, rows_all)
    grad_rows, grad_final_gain, grad_final_bias = norm_backward(
        grad_final, scaled_final, inverse_final, final_gain
    )
    slot_hot = (jnp.arange(tokens, dtype=jnp.int32)[:, None] == slots[None, :]).astype(jnp.float32)
    grad_state = jnp.dot(slot_hot, grad_rows, precision=lax.Precision.HIGHEST)

    layer_grads = [None] * layers
    wide_sent, narrow_sent = [None] * layers, [None] * layers
    for layer in reversed(range(layers)):
        (
            normed_b,
            scaled_one,
            inverse_one,
            mixed_b,
            log_total,
            attended_b,
            scaled_two,
            inverse_two,
            normed_two_b,
            before,
            active_b,
        ) = saved[layer]
        gain_one, _, _, _, _, gain_two, _, _, _ = layer_pieces(vectors_f, layer * block, width, hidden_width)
        grad_out = grad_state.astype(low)
        contract_grad = outer_sum(active_b, grad_out).astype(low)
        grad_contract_bias = jnp.sum(grad_out.astype(jnp.float32), axis=0)
        grad_active = times_transpose(grad_out, contract_all[layer])
        grad_before = (grad_active * gelu_slope(before)).astype(low)
        expand_grad = outer_sum(normed_two_b, grad_before).astype(low)
        wide_sent[layer] = send_core(
            [contract_grad.reshape(devices, hidden_share, width)]
            + lanes_to_rows(expand_grad, devices, width)
        )
        grad_expand_bias = jnp.sum(grad_before.astype(jnp.float32), axis=0)
        grad_normed_two = times_transpose(grad_before, expand_all[layer])
        grad_mid, grad_gain_two, grad_bias_two = norm_backward(
            grad_normed_two, scaled_two, inverse_two, gain_two
        )
        grad_middle = grad_state + grad_mid
        grad_project = grad_middle.astype(low)
        wide_sent[layer] = send_quads(wide_sent[layer])
        project_grad = outer_sum(attended_b, grad_project).astype(low)
        grad_project_bias = jnp.sum(grad_project.astype(jnp.float32), axis=0)
        grad_attended = times_transpose(grad_project, project_all[layer]).astype(low)
        if layer < layers - 1:
            wide_sent[layer + 1] = send_deep(wide_sent[layer + 1])
        grad_mixed = attend_backward(mixed_b, document, log_total, grad_attended)
        attend_grad = outer_sum(normed_b, grad_mixed).astype(low)
        narrow_sent[layer] = send_core(
            lanes_to_rows(attend_grad, devices, width) + lanes_to_rows(project_grad, devices, width)
        )
        grad_mixed_f = grad_mixed.astype(jnp.float32)
        grad_query_bias = jnp.sum(grad_mixed_f[:, :width], axis=0)
        grad_value_bias = jnp.sum(grad_mixed_f[:, 2 * width :], axis=0)
        grad_normed = times_transpose(grad_mixed, attend_all[layer])
        grad_in, grad_gain_one, grad_bias_one = norm_backward(
            grad_normed, scaled_one, inverse_one, gain_one
        )
        grad_state = grad_middle + grad_in
        narrow_sent[layer] = send_quads(narrow_sent[layer])
        layer_grads[layer] = jnp.concatenate(
            [
                grad_gain_one,
                grad_bias_one,
                grad_query_bias,
                grad_value_bias,
                grad_project_bias,
                grad_gain_two,
                grad_bias_two,
                grad_contract_bias,
                grad_expand_bias,
            ]
        )

    grad_embedded = grad_state.astype(low)
    position_grad = outer_sum(position_hot, grad_embedded).astype(low)
    vector_grad = jnp.concatenate(layer_grads + [grad_final_gain, grad_final_bias])
    vector_grad = jnp.pad(
        vector_grad.astype(low).reshape(devices, vector_share),
        ((0, 0), (0, vector_rows * width - vector_share)),
    )

    def returned(turn):
        return outer_sum(seat_matrix(turn), grad_embedded).astype(low).reshape(devices, slots_each, width)

    came = lax.all_to_all(
        jnp.concatenate(
            [
                returned(0),
                position_grad.reshape(devices, position_share, width),
                vector_grad.reshape(devices, vector_rows, width),
            ],
            axis=1,
        ),
        BOTH,
        0,
        0,
        tiled=True,
    )
    small_sum = jnp.sum(came[:, slots_each:].astype(jnp.float32), axis=0)
    table_grad = table_grad + outer_sum(wanted_of(heard_first), came[:, :slots_each].reshape(slots_all, width))

    def later_turn(carry):
        turn, total = carry
        rows = lax.all_to_all(returned(turn), BOTH, 0, 0, tiled=True).reshape(slots_all, width)
        return (turn + 1, total + outer_sum(wanted_of(requests(turn)), rows))

    _, table_sum = lax.while_loop(lambda carry: carry[0] < turns, later_turn, (jnp.int32(1), table_grad))
    for layer in range(1, layers):
        narrow_sent[layer] = send_deep(narrow_sent[layer])
    wide_sent[0] = send_deep(wide_sent[0])
    narrow_sent[0] = send_deep(narrow_sent[0])
    wide_sums = [sum_low(sent) for sent in wide_sent]
    narrow_sums = [sum_low(sent) for sent in narrow_sent]

    contract_sum = jnp.stack([total[:hidden_share] for total in wide_sums])
    expand_sum = jnp.stack(
        [rows_to_lanes(total[hidden_share:], hidden_width // width) for total in wide_sums]
    )
    attend_sum = jnp.stack([rows_to_lanes(total[: 3 * row_share], 3) for total in narrow_sums])
    project_sum = jnp.stack([total[3 * row_share : 4 * row_share] for total in narrow_sums])
    position_sum = small_sum[:position_share]
    vector_sum = small_sum[position_share:].reshape(-1)[:vector_share]

    sums = (table_sum, position_sum, attend_sum, project_sum, expand_sum, contract_sum, vector_sum)
    squares = jnp.zeros((), jnp.float32)
    for grad in sums:
        squares = squares + jnp.sum(grad * grad)
    scalars = jnp.stack([squares, entropy_local, jnp.sum(loss_mask).astype(jnp.float32)])
    square_total, entropy_total, count = jnp.sum(spread(scalars).reshape(devices, 3), axis=0)
    grad_norm = jnp.sqrt(square_total) / count
    factor = clip_limit / jnp.maximum(grad_norm, clip_limit)
    loss = entropy_total / count
    weights = (
        token_table,
        position_table,
        attend_weight,
        project_weight,
        expand_weight,
        contract_weight,
        vector_params,
    )
    moments = (
        table_moments,
        position_moments,
        attend_moments,
        project_moments,
        expand_moments,
        contract_moments,
        vector_moments,
    )
    decays = (decay_rate, decay_rate, decay_rate, decay_rate, decay_rate, decay_rate, 0.0)
    table_new, position_new, attend_new, project_new, expand_new, contract_new, vector_new = [
        adam_update(weight, moment, grad / count * factor, decay)
        for weight, moment, grad, decay in zip(weights, moments, sums, decays)
    ]
    return (
        loss,
        grad_norm,
        table_new[0],
        position_new[0],
        attend_new[0],
        project_new[0],
        expand_new[0],
        contract_new[0],
        vector_new[0],
        table_new[1],
        position_new[1],
        attend_new[1],
        project_new[1],
        expand_new[1],
        contract_new[1],
        vector_new[1],
        table_new[2],
        position_new[2],
        attend_new[2],
        project_new[2],
        expand_new[2],
        contract_new[2],
        vector_new[2],
    )


def solution(mesh):
    return jax.shard_map(
        shards,
        mesh=mesh,
        in_specs=(
            P(None, ("dp", "fsdp"), None),
            P(None, ("dp", "fsdp"), None),
            P(None, ("dp", "fsdp"), None),
            P(None, ("dp", "fsdp"), None),
            P(None, ("dp", "fsdp"), None),
            P(None, ("dp", "fsdp"), None),
            P(("dp", "fsdp"), None),
            P(("dp", "fsdp"), None),
            P(None, ("dp", "fsdp"), None),
            P(None, ("dp", "fsdp"), None),
            P(None, ("dp", "fsdp"), None),
            P(None, ("dp", "fsdp"), None),
            P(("dp", "fsdp")),
            P(None, ("dp", "fsdp"), None),
            P(None, ("dp", "fsdp"), None),
            P(None, None, ("dp", "fsdp"), None),
            P(None, None, ("dp", "fsdp"), None),
            P(None, None, ("dp", "fsdp"), None),
            P(None, None, ("dp", "fsdp"), None),
            P(None, ("dp", "fsdp")),
        ),
        out_specs=(
            P(),
            P(),
            P(("dp", "fsdp"), None),
            P(("dp", "fsdp"), None),
            P(None, ("dp", "fsdp"), None),
            P(None, ("dp", "fsdp"), None),
            P(None, ("dp", "fsdp"), None),
            P(None, ("dp", "fsdp"), None),
            P(("dp", "fsdp")),
            P(None, ("dp", "fsdp"), None),
            P(None, ("dp", "fsdp"), None),
            P(None, None, ("dp", "fsdp"), None),
            P(None, None, ("dp", "fsdp"), None),
            P(None, None, ("dp", "fsdp"), None),
            P(None, None, ("dp", "fsdp"), None),
            P(None, ("dp", "fsdp")),
            P(("dp", "fsdp"), None),
            P(("dp", "fsdp"), None),
            P(None, ("dp", "fsdp"), None),
            P(None, ("dp", "fsdp"), None),
            P(None, ("dp", "fsdp"), None),
            P(None, ("dp", "fsdp"), None),
            P(("dp", "fsdp")),
        ),
        check_vma=False,
    )
```

time: 2110 us -> 989 us (0.47)
  waiting for transfers between devices: 1050 us -> 440 us
  blocking collectives: 248 us -> 14.1 us
  matrix products: 396 us -> 169 us
  other arithmetic: 235 us -> 120 us
  starting transfers between devices: 1.88 us -> 75.3 us
  Pallas kernels: 0 us -> 58.5 us
  local copies, waits for them, and re-layouts: 130 us -> 72.2 us
    reduce_scatter x10 -> x0, waiting for transfers between devices: 821 us -> none  [the longest x1 209 us: shards(): lax.psum_scatter(expand_grad, ('dp', 'fsdp'), scatter_dimension=1, tiled=...]
    ppermute x0 -> x42, waiting for transfers between devices: none -> 217 us  [swapped(): lax.ppermute(value, axis, [(index, index ^ flip) for index in range(size)])]
    all_gather x10 -> x0, blocking collectives: 170 us -> none  [the longest x1 76.2 us: fetch(): lax.all_gather(position_table.astype(jnp.bfloat16), ('dp', 'fsdp'), axis=...]
    scatter-add x10 -> x0, other arithmetic: 106 us -> none  [the longest x2 67.7 us: shards(): table_grad.at[word_local]]
    all_gather x7 -> x3, waiting for transfers between devices: 233 us -> 128 us  [the longest x2 74.9 us: shards(): lax.all_gather(share, BOTH, axis=0, tiled=True)]
    dot_general x26 -> x5, matrix products: 126 us -> 22.1 us  [the longest x1 11 us: shards(): jnp.dot(grad_logits, table_b, preferred_element_type=jnp.float32)]
    all_to_all x0 -> x5, waiting for transfers between devices: none -> 95.2 us  [the longest x1 53.9 us: looked_up(): rows = lax.all_to_all(rows, BOTH, 0, 0, tiled=True)]
    dot_general x18 -> x12, matrix products: 121 us -> 58.5 us  [outer_sum(): lax.dot_general(left, right, (((0,), (0,)), ((), ())), preferred_element_...]
  transfers between devices with their start and end apart: 18 -> 50, of which waited for: 10 -> 28; matrix products, arithmetic and copies ran while one was open for 20% -> 15% of each run, Pallas kernels for 0% -> 1%
where the time goes in v1:
time: 989 us; the launch traced here: 980 us
  waiting for transfers between devices  440 us (44%)
  matrix products  169 us (17%)
  other arithmetic  120 us (12%)
  starting transfers between devices  75.3 us (8%)
  local copies, waits for them, and re-layouts  72.2 us (7%)
  Pallas kernels  58.5 us (6%)
  between operations  30.8 us (3%)
  blocking collectives  14.1 us (1%)
    ppermute x42, waiting for transfers between devices, swapped(): lax.ppermute(value, axis, [(index, index ^ flip) for index in range(size)])  217 us
    all_gather x2, waiting for transfers between devices, shards(): lax.all_gather(share, BOTH, axis=0, tiled=True)  74.9 us
    dot_general x12, matrix products, outer_sum(): lax.dot_general(left, right, (((0,), (0,)), ((), ())), preferred_element_...  58.5 us
    all_to_all x1, waiting for transfers between devices, looked_up(): rows = lax.all_to_all(rows, BOTH, 0, 0, tiled=True)  53.9 us
    all_gather x1, waiting for transfers between devices, shards(): lax.all_gather(contract_weight.astype(low), BOTH, axis=1, tiled=True)  53.2 us
    ppermute x42, starting transfers between devices, swapped(): lax.ppermute(value, axis, [(index, index ^ flip) for index in range(size)])  51.5 us
    dot_general x9, matrix products, times_transpose(): lax.dot_general(left, right, (((1,), (1,)), ((), ())), preferred_element_...  46.2 us
    all_to_all x2, waiting for transfers between devices, spread(): lax.all_to_all(jnp.broadcast_to(value[None], (count,) + value.shape), BOT...  33.9 us
  transfers between devices with their start and end apart: 50, of which 28 were waited for; matrix products, arithmetic and copies ran while one was open for 15% of the time, Pallas kernels for 1%

profile of v1, /device:TPU:0, one launch (start us, length us, event | category | flops | bytes accessed | tf_op | source)
XLA Modules:
  0.0 980.1 jit_solution(6738310352920646072)
XLA Ops:
  18.0 7.3 all-to-all-start.4
  25.5 7.4 all-to-all-done.4
  41.0 6.1 fusion.60
  47.1 20.5 %all-to-all-done.6 = bf16[32,9,768]{2,1,0:T(8,128)(2,1)S(1)} async-done(((bf16[32,9,768]{2,1,0:T(8,128)(2,1)}), bf16[32,9,768]{2,1,0:T(8,128)(2,1)S(1)}, u32[]{:S(2)}, u32[]{:S(2)}) %all-to-all-start.6) | async-done | bytes 442400 | tf_op jit(solution)/shard_map/all_to_all | solution.py:89
  67.5 5.5 all-to-all-start.5
  80.6 53.9 %all-to-all-done.5 = bf16[32,32,768]{2,1,0:T(8,128)(2,1)S(1)} async-done(((bf16[32,32,768]{2,1,0:T(8,128)(2,1)}), bf16[32,32,768]{2,1,0:T(8,128)(2,1)S(1)}, u32[]{:S(2)}, u32[]{:S(2)}) %all-to-all-start.5) | async-done | bytes 1572896 | tf_op jit(solution)/shard_map/all_to_all | solution.py:376
  139.3 5.7 fusion.30.mixed_ref
  144.9 9.9 %attend_forward.2 = (bf16[512,768]{1,0:T(8,128)(2,1)}, f32[512,768]{1,0:T(8,128)}) custom-call(s32[2,1,256]{2,1,0:T(1,128)} %broadcast_in_dim.134.row_ref, s32[2,256,1]{2,1,0:T(8,128)} %copy.281.column_ref, bf16[512,2304]{1,0:T(8,128)(2,1)} %fusion.30.mixed_ref), custom_call_target="tpu_custom_call" | custom-call | flops 402653184 | bytes 6291456 | tf_op jit(solution)/shard_map/attend_forward/pallas_call | solution.py:254
  157.5 7.0 fusion.40
  164.6 53.2 %all-gather.6.cloned.1.call-done = bf16[2,3072,768]{2,1,0:T(8,128)(2,1)} async-done(((bf16[2,96,768]{2,1,0:T(8,128)(2,1)}), bf16[2,3072,768]{2,1,0:T(8,128)(2,1)}) %all-gather.6.cloned.1.call-update) | async-done | bytes 9437200 | tf_op jit(solution)/shard_map/all_gather | solution.py:402
  217.8 8.2 fusion.228
  226.3 74.9 %all-gather.8.cloned.1.call-done = bf16[768,6144]{1,0:T(8,128)(2,1)} async-done(((bf16[24,6144]{1,0:T(8,128)(2,1)}), bf16[768,6144]{1,0:T(8,128)(2,1)}) %all-gather.8.cloned.1.call-update) | async-done | bytes 9437200 | tf_op jit(solution)/shard_map/all_gather | solution.py:401
  301.2 5.6 fusion.31.mixed_ref
  306.8 20.0 %attend_forward.3 = (bf16[512,768]{1,0:T(8,128)(2,1)}, f32[512,768]{1,0:T(8,128)}) custom-call(s32[2,1,256]{2,1,0:T(1,128)} %broadcast_in_dim.134.row_ref, s32[2,256,1]{2,1,0:T(8,128)} %copy.281.column_ref, bf16[512,2304]{1,0:T(8,128)(2,1)} %fusion.31.mixed_ref), custom_call_target="tpu_custom_call" | custom-call | flops 402653184 | bytes 6291456 | tf_op jit(solution)/shard_map/attend_forward/pallas_call | solution.py:254
  329.6 5.5 fusion.36
  351.4 6.2 collective-permute-done.1
  361.2 8.5 collective-permute-done.3
  369.7 6.5 collective-permute-done.4
  384.1 11.1 %fusion.230 = (f32[2048]{0:T(1024)S(1)}, f32[2048,1600]{0,1:T(8,128)}) fusion(bf16[2048,768]{1,0:T(8,128)(2,1)S(1)} %bitcast.560, bf16[1600,768]{1,0:T(8,128)(2,1)} %convert_element_type.443), kind=kOutput, calls=%fused_computation.588 | convolution fusion | flops 5036439552 | bytes 18718720 | tf_op jit(solution)/shard_map/dot_general | solution.py:74
  395.3 6.8 select_reduce_fusion.2
  410.0 13.4 %all-to-all-done.7 = f32[32,32,128]{2,1,0:T(8,128)S(1)} async-done(((f32[32,32,128]{2,1,0:T(8,128)}), f32[32,32,128]{2,1,0:T(8,128)S(1)}, u32[]{:S(2)}, u32[]{:S(2)}) %all-to-all-start.7) | async-done | bytes 524320 | tf_op jit(solution)/shard_map/all_to_all | solution.py:89
  428.5 11.0 %convolution_convert_fusion.6 = bf16[2048,768]{1,0:T(8,128)(2,1)S(1)} fusion(bf16[1600,768]{1,0:T(8,128)(2,1)} %convert_element_type.443, f32[2048,1600]{0,1:T(8,128)} %get-tuple-element.462, f32[2048]{0:T(1024)S(1)} %convert_element_type.464, s32[2048]{0:T(1024)S(1)} %sub.288, f32[2048]{0:T(1024)S(1)} %select_n.282), kind=kOutput, calls=%fused_computation.91 | convolution fusion | flops 5054398464 | bytes 18735104 | tf_op jit(solution)/shard_map/dot_general | solution.py:501
  450.1 8.7 collective-permute-done.10
  458.9 8.0 collective-permute-done.8
  481.1 9.3 convolution_convert_fusion.1
  490.4 8.2 fusion.232
  511.6 14.1 %attend_backward.2 = bf16[512,2304]{1,0:T(8,128)(2,1)} custom-call(s32[2,1,256]{2,1,0:T(1,128)} %broadcast_in_dim.134.row_ref, s32[2,256,1]{2,1,0:T(8,128)} %copy.281.column_ref, bf16[512,2304]{1,0:T(8,128)(2,1)} %fusion.31.mixed_ref, f32[512,768]{1,0:T(8,128)} %get-tuple-element.176.log_ref, bf16[512,768]{1,0:T(8,128)(2,1)} %convolution_convert_fusion.10.grad_ref), custom_call_target="tpu_custom_call" | custom-call | flops 1006632960 | bytes 6291456 | tf_op jit(solution)/shard_map/attend_backward/pallas_call | solution.py:271
  525.8 6.3 convolution_convert_fusion.4
  537.4 5.6 convolution_convert_fusion.3
  543.0 7.5 fusion.231
  550.5 6.6 convolution_convert_fusion.2
  564.9 14.5 %attend_backward.3 = bf16[512,2304]{1,0:T(8,128)(2,1)} custom-call(s32[2,1,256]{2,1,0:T(1,128)} %broadcast_in_dim.134.row_ref, s32[2,256,1]{2,1,0:T(8,128)} %copy.281.column_ref, bf16[512,2304]{1,0:T(8,128)(2,1)} %fusion.30.mixed_ref, f32[512,768]{1,0:T(8,128)} %get-tuple-element.177.log_ref, bf16[512,768]{1,0:T(8,128)(2,1)} %convolution_convert_fusion.9.grad_ref), custom_call_target="tpu_custom_call" | custom-call | flops 1006632960 | bytes 6291456 | tf_op jit(solution)/shard_map/attend_backward/pallas_call | solution.py:271
  609.1 5.4 multiply_reduce_fusion.5
  647.6 25.8 %collective-permute-done.15 = bf16[4,96,768]{2,1,0:T(8,128)(2,1)S(1)} collective-permute-done((bf16[4,96,768]{2,1,0:T(8,128)(2,1)S(1)}, bf16[4,96,768]{2,1,0:T(8,128)(2,1)S(1)}, u32[]{:S(2)}, u32[]{:S(2)}) %collective-permute-start.15) | collective-permute-done | bytes 589856 | tf_op jit(solution)/shard_map/ppermute | solution.py:84
  677.3 16.9 %collective-permute-done.17 = bf16[4,96,768]{2,1,0:T(8,128)(2,1)S(1)} collective-permute-done((bf16[4,96,768]{2,1,0:T(8,128)(2,1)S(1)}, bf16[4,96,768]{2,1,0:T(8,128)(2,1)S(1)}, u32[]{:S(2)}, u32[]{:S(2)}) %collective-permute-start.17) | collective-permute-done | bytes 589856 | tf_op jit(solution)/shard_map/ppermute | solution.py:84
  694.5 11.2 %collective-permute-done.22 = bf16[4,96,768]{2,1,0:T(8,128)(2,1)S(1)} collective-permute-done((bf16[4,96,768]{2,1,0:T(8,128)(2,1)S(1)}, bf16[4,96,768]{2,1,0:T(8,128)(2,1)S(1)}, u32[]{:S(2)}, u32[]{:S(2)}) %collective-permute-start.22) | collective-permute-done | bytes 589856 | tf_op jit(solution)/shard_map/ppermute | solution.py:84
  708.8 10.0 %collective-permute-done.24 = bf16[4,96,768]{2,1,0:T(8,128)(2,1)S(1)} collective-permute-done((bf16[4,96,768]{2,1,0:T(8,128)(2,1)S(1)}, bf16[4,96,768]{2,1,0:T(8,128)(2,1)S(1)}, u32[]{:S(2)}, u32[]{:S(2)}) %collective-permute-start.24) | collective-permute-done | bytes 589856 | tf_op jit(solution)/shard_map/ppermute | solution.py:84
  731.4 6.4 collective-permute-done.26
  743.5 5.8 fusion.12
  749.3 5.2 add_convert_fusion.1
  759.9 10.8 %convolution_add_fusion.2 = f32[1600,768]{1,0:T(8,128)} fusion(f32[1600,768]{1,0:T(8,128)} %fusion.12, bf16[2048,768]{1,0:T(8,128)(2,1)S(1)} %bitcast.561, f32[2048,1600]{0,1:T(8,128)S(1)} %bitcast.532, f32[2048]{0:T(1024)S(1)} %copy-done.109, s32[2048]{0:T(1024)S(1)} %copy-done.79, f32[2048]{0:T(1024)S(1)} %copy-done.111), kind=kOutput, calls=%fused_computation.88 | convolution fusion | flops 5054054400 | bytes 26107904 | tf_op jit(solution)/shard_map/dot_general | solution.py:68
  796.7 30.3 %collective-permute-done.30 = bf16[4,192,768]{2,1,0:T(8,128)(2,1)} collective-permute-done((bf16[4,192,768]{2,1,0:T(8,128)(2,1)}, bf16[4,192,768]{2,1,0:T(8,128)(2,1)}, u32[]{:S(2)}, u32[]{:S(2)}) %collective-permute-start.30) | collective-permute-done | bytes 1179680 | tf_op jit(solution)/shard_map/ppermute | solution.py:84
  832.3 5.8 collective-permute-done.36
  839.5 35.6 %collective-permute-done.37 = bf16[4,192,768]{2,1,0:T(8,128)(2,1)} collective-permute-done((bf16[4,192,768]{2,1,0:T(8,128)(2,1)}, bf16[4,192,768]{2,1,0:T(8,128)(2,1)}, u32[]{:S(2)}, u32[]{:S(2)}) %collective-permute-start.37) | collective-permute-done | bytes 1179680 | tf_op jit(solution)/shard_map/ppermute | solution.py:84
  885.2 7.0 collective-permute-done.39
  892.2 12.3 %collective-permute-done.40 = bf16[192,768]{1,0:T(8,128)(2,1)S(1)} collective-permute-done((bf16[192,768]{1,0:T(8,128)(2,1)S(1)}, bf16[192,768]{1,0:T(8,128)(2,1)S(1)}, u32[]{:S(2)}, u32[]{:S(2)}) %collective-permute-start.40) | collective-permute-done | bytes 294944 | tf_op jit(solution)/shard_map/ppermute | solution.py:84
  910.5 14.1 %all_to_all.88 = f32[32,1,3]{2,1,0:T(1,128)S(1)} all-to-all(f32[32,1,3]{2,1,0:T(1,128)S(1)} %broadcast_in_dim.152), channel_id=1, replica_groups=mesh['dp'=8,'fsdp'=4] {'dp','fsdp'}, dimensions={0} | all-to-all | bytes 768 | tf_op jit(solution)/shard_map/all_to_all | solution.py:89
  929.9 13.7 %fusion.198 = (f32[1,1600,768]{2,1,0:T(8,128)}, f32[1,1600,768]{2,1,0:T(8,128)}, bf16[1600,768]{1,0:T(8,128)(2,1)}, f32[1600,768]{1,0:T(8,128)}) fusion(f32[]{:T(128)S(6)} %div.348, f32[1600,768]{1,0:T(8,128)} %get-tuple-element.717, f32[]{:T(128)} %bitcast.163, f32[2,1600,768]{2,1,0:T(8,128)} %param.38, f32[1600,768]{1,0:T(8,128)} %param.31), kind=kLoop, calls=%fused_computation.562 | loop fusion | flops 22118400 | bytes 36864008 | tf_op jit(solution)/shard_map/stack | solution.py:294
  (683 shorter events, 290.1 us)
Async XLA Ops:
  7.2 132.0 %all-gather.4.cloned.1.call-start = ((), (), s32[]{:S(2)}) async-start(), calls=%async_computation.10 | async-start | bytes 9732096 | tf_op jit(solution)/shard_map/all_gather | solution.py:401
  10.4 207.4 %all-gather.6.cloned.1.call-start = ((), (), s32[]{:S(2)}) async-start(), calls=%async_computation.11 | async-start | bytes 9732096 | tf_op jit(solution)/shard_map/all_gather | solution.py:402
  11.2 289.9 %all-gather.8.cloned.1.call-start = ((), (), s32[]{:S(2)}) async-start(), calls=%async_computation.12 | async-start | bytes 9732096 | tf_op jit(solution)/shard_map/all_gather | solution.py:401
  18.0 14.9 %all-to-all-start.4 = ((s32[32,1,161]{2,1,0:T(1,128)}), s32[32,1,161]{2,1,0:T(1,128)S(1)}, u32[]{:S(2)}, u32[]{:S(2)}) async-start(s32[32,1,161]{2,1,0:T(1,128)} %all_to_all.60), calls=%async_computation.4 | async-start | bytes 65536 | tf_op jit(solution)/shard_map/all_to_all | solution.py:363
  33.9 33.7 %all-to-all-start.6 = ((bf16[32,9,768]{2,1,0:T(8,128)(2,1)}), bf16[32,9,768]{2,1,0:T(8,128)(2,1)S(1)}, u32[]{:S(2)}, u32[]{:S(2)}) async-start(bf16[32,9,768]{2,1,0:T(8,128)(2,1)} %broadcast_in_dim.133), calls=%async_computation.6 | async-start | bytes 1572864 | tf_op jit(solution)/shard_map/all_to_all | solution.py:89
  67.5 66.9 %all-to-all-start.5 = ((bf16[32,32,768]{2,1,0:T(8,128)(2,1)}), bf16[32,32,768]{2,1,0:T(8,128)(2,1)S(1)}, u32[]{:S(2)}, u32[]{:S(2)}) async-start(bf16[32,32,768]{2,1,0:T(8,128)(2,1)} %bitcast.9), calls=%async_computation.5 | async-start | bytes 3145728 | tf_op jit(solution)/shard_map/all_to_all | solution.py:376
  345.6 5.8 collective-permute-start
  347.0 10.6 %collective-permute-start.1 = (bf16[64,768]{1,0:T(8,128)(2,1)S(1)}, bf16[64,768]{1,0:T(8,128)(2,1)S(1)}, u32[]{:S(2)}, u32[]{:S(2)}) collective-permute-start(bf16[64,768]{1,0:T(8,128)(2,1)S(1)} %add_convert_fusion.9), channel_id=1, source_target_pairs={{0,2},{1,3},{2,0},{3,1},{4,6},{5,7},{6,4},{7,5},{8,10},{9,11},{10,... | collective-permute-start | bytes 294920 | tf_op jit(solution)/shard_map/ppermute | solution.py:84
  348.1 9.5 collective-permute-start.2
  357.7 12.1 %collective-permute-start.3 = (bf16[4,64,768]{2,1,0:T(8,128)(2,1)S(1)}, bf16[4,64,768]{2,1,0:T(8,128)(2,1)S(1)}, u32[]{:S(2)}, u32[]{:S(2)}) collective-permute-start(bf16[4,64,768]{2,1,0:T(8,128)(2,1)S(1)} %get-tuple-element.382), channel_id=1, source_target_pairs={{0,8},{4,12},{8,0},{12,4},{16,24},{20,28},{24,16},{28,20},{1,9},{5... | collective-permute-start | bytes 1179656 | tf_op jit(solution)/shard_map/ppermute | solution.py:84
  359.2 17.0 %collective-permute-start.4 = (bf16[4,64,768]{2,1,0:T(8,128)(2,1)S(1)}, bf16[4,64,768]{2,1,0:T(8,128)(2,1)S(1)}, u32[]{:S(2)}, u32[]{:S(2)}) collective-permute-start(bf16[4,64,768]{2,1,0:T(8,128)(2,1)S(1)} %get-tuple-element.382), channel_id=1, source_target_pairs={{0,16},{4,20},{8,24},{12,28},{16,0},{20,4},{24,8},{28,12},{1,17},{... | collective-permute-start | bytes 1179656 | tf_op jit(solution)/shard_map/ppermute | solution.py:84
  359.8 16.5 %collective-permute-start.5 = (bf16[4,64,768]{2,1,0:T(8,128)(2,1)S(1)}, bf16[4,64,768]{2,1,0:T(8,128)(2,1)S(1)}, u32[]{:S(2)}, u32[]{:S(2)}) collective-permute-start(bf16[4,64,768]{2,1,0:T(8,128)(2,1)S(1)} %get-tuple-element.382), channel_id=1, source_target_pairs={{0,24},{4,28},{8,16},{12,20},{16,8},{20,12},{24,0},{28,4},{1,25},{... | collective-permute-start | bytes 1179656 | tf_op jit(solution)/shard_map/ppermute | solution.py:84
  403.9 19.5 %all-to-all-start.7 = ((f32[32,32,128]{2,1,0:T(8,128)}), f32[32,32,128]{2,1,0:T(8,128)S(1)}, u32[]{:S(2)}, u32[]{:S(2)}) async-start(f32[32,32,128]{2,1,0:T(8,128)} %broadcast_in_dim.146), calls=%async_computation.7 | async-start | bytes 1048576 | tf_op jit(solution)/shard_map/all_to_all | solution.py:89
  445.9 13.0 %collective-permute-start.10 = (bf16[4,64,768]{2,1,0:T(8,128)(2,1)S(1)}, bf16[4,64,768]{2,1,0:T(8,128)(2,1)S(1)}, u32[]{:S(2)}, u32[]{:S(2)}) collective-permute-start(bf16[4,64,768]{2,1,0:T(8,128)(2,1)S(1)} %get-tuple-element.312), channel_id=1, source_target_pairs={{0,24},{4,28},{8,16},{12,20},{16,8},{20,12},{24,0},{28,4},{1,25},{... | collective-permute-start | bytes 1179656 | tf_op jit(solution)/shard_map/ppermute | solution.py:84
  447.4 19.4 %collective-permute-start.8 = (bf16[4,64,768]{2,1,0:T(8,128)(2,1)S(1)}, bf16[4,64,768]{2,1,0:T(8,128)(2,1)}, u32[]{:S(2)}, u32[]{:S(2)}) collective-permute-start(bf16[4,64,768]{2,1,0:T(8,128)(2,1)S(1)} %get-tuple-element.311), channel_id=1, source_target_pairs={{0,8},{4,12},{8,0},{12,4},{16,24},{20,28},{24,16},{28,20},{1,9},{5... | collective-permute-start | bytes 1179656 | tf_op jit(solution)/shard_map/ppermute | solution.py:84
  448.9 17.9 %collective-permute-start.9 = (bf16[4,64,768]{2,1,0:T(8,128)(2,1)S(1)}, bf16[4,64,768]{2,1,0:T(8,128)(2,1)}, u32[]{:S(2)}, u32[]{:S(2)}) collective-permute-start(bf16[4,64,768]{2,1,0:T(8,128)(2,1)S(1)} %get-tuple-element.313), channel_id=1, source_target_pairs={{0,16},{4,20},{8,24},{12,28},{16,0},{20,4},{24,8},{28,12},{1,17},{... | collective-permute-start | bytes 1179656 | tf_op jit(solution)/shard_map/ppermute | solution.py:84
  468.3 6.4 collective-permute-start.11
  469.7 10.2 %collective-permute-start.12 = (bf16[64,768]{1,0:T(8,128)(2,1)S(1)}, bf16[64,768]{1,0:T(8,128)(2,1)S(1)}, u32[]{:S(2)}, u32[]{:S(2)}) collective-permute-start(bf16[64,768]{1,0:T(8,128)(2,1)S(1)} %get-tuple-element.380), channel_id=1, source_target_pairs={{0,2},{1,3},{2,0},{3,1},{4,6},{5,7},{6,4},{7,5},{8,10},{9,11},{10,... | collective-permute-start | bytes 294920 | tf_op jit(solution)/shard_map/ppermute | solution.py:84
  470.7 9.2 collective-permute-start.13
  594.6 154.7 %collective-permute-start.28 = (bf16[4,4,192,768]{3,2,1,0:T(8,128)(2,1)}, bf16[4,4,192,768]{3,2,1,0:T(8,128)(2,1)}, u32[]{:S(2)}, u32[]{:S(2)}) collective-permute-start(bf16[4,4,192,768]{3,2,1,0:T(8,128)(2,1)} %get-tuple-element.322), channel_id=1, source_target_pairs={{0,4},{4,0},{8,12},{12,8},{16,20},{20,16},{24,28},{28,24},{1,5},{5... | collective-permute-start | bytes 14155784 | tf_op jit(solution)/shard_map/ppermute | solution.py:84
  602.0 34.9 %collective-permute-start.14 = (bf16[4,4,96,768]{3,2,1,0:T(8,128)(2,1)}, bf16[4,4,96,768]{3,2,1,0:T(8,128)(2,1)}, u32[]{:S(2)}, u32[]{:S(2)}) collective-permute-start(bf16[4,4,96,768]{3,2,1,0:T(8,128)(2,1)} %pad_maximum_fusion.3), channel_id=1, source_target_pairs={{0,4},{4,0},{8,12},{12,8},{16,20},{20,16},{24,28},{28,24},{1,5},{5... | collective-permute-start | bytes 7077896 | tf_op jit(solution)/shard_map/ppermute | solution.py:84
  608.7 35.0 %collective-permute-start.21 = (bf16[4,4,96,768]{3,2,1,0:T(8,128)(2,1)}, bf16[4,4,96,768]{3,2,1,0:T(8,128)(2,1)}, u32[]{:S(2)}, u32[]{:S(2)}) collective-permute-start(bf16[4,4,96,768]{3,2,1,0:T(8,128)(2,1)} %pad_maximum_fusion.4), channel_id=1, source_target_pairs={{0,4},{4,0},{8,12},{12,8},{16,20},{20,16},{24,28},{28,24},{1,5},{5... | collective-permute-start | bytes 7077896 | tf_op jit(solution)/shard_map/ppermute | solution.py:84
  634.0 108.1 %all-to-all-start.8 = ((bf16[32,41,768]{2,1,0:T(8,128)(2,1)}), bf16[32,41,768]{2,1,0:T(8,128)(2,1)S(1)}, u32[]{:S(2)}, u32[]{:S(2)}) async-start(bf16[32,41,768]{2,1,0:T(8,128)(2,1)} %pad_maximum_fusion.2), calls=%async_computation.8 | async-start | bytes 4718592 | tf_op jit(solution)/shard_map/all_to_all | solution.py:588
  640.1 33.3 %collective-permute-start.15 = (bf16[4,96,768]{2,1,0:T(8,128)(2,1)S(1)}, bf16[4,96,768]{2,1,0:T(8,128)(2,1)S(1)}, u32[]{:S(2)}, u32[]{:S(2)}) collective-permute-start(bf16[4,96,768]{2,1,0:T(8,128)(2,1)S(1)} %get-tuple-element.300), channel_id=1, source_target_pairs={{0,8},{4,12},{8,0},{12,4},{16,24},{20,28},{24,16},{28,20},{1,9},{5... | collective-permute-start | bytes 1769480 | tf_op jit(solution)/shard_map/ppermute | solution.py:84
  641.9 33.1 %collective-permute-start.16 = (bf16[4,96,768]{2,1,0:T(8,128)(2,1)S(1)}, bf16[4,96,768]{2,1,0:T(8,128)(2,1)S(1)}, u32[]{:S(2)}, u32[]{:S(2)}) collective-permute-start(bf16[4,96,768]{2,1,0:T(8,128)(2,1)S(1)} %get-tuple-element.302), channel_id=1, source_target_pairs={{0,16},{4,20},{8,24},{12,28},{16,0},{20,4},{24,8},{28,12},{1,17},{... | collective-permute-start | bytes 1769480 | tf_op jit(solution)/shard_map/ppermute | solution.py:84
  643.3 50.8 %collective-permute-start.17 = (bf16[4,96,768]{2,1,0:T(8,128)(2,1)S(1)}, bf16[4,96,768]{2,1,0:T(8,128)(2,1)S(1)}, u32[]{:S(2)}, u32[]{:S(2)}) collective-permute-start(bf16[4,96,768]{2,1,0:T(8,128)(2,1)S(1)} %get-tuple-element.301), channel_id=1, source_target_pairs={{0,24},{4,28},{8,16},{12,20},{16,8},{20,12},{24,0},{28,4},{1,25},{... | collective-permute-start | bytes 1769480 | tf_op jit(solution)/shard_map/ppermute | solution.py:84
  645.8 59.9 %collective-permute-start.22 = (bf16[4,96,768]{2,1,0:T(8,128)(2,1)S(1)}, bf16[4,96,768]{2,1,0:T(8,128)(2,1)S(1)}, u32[]{:S(2)}, u32[]{:S(2)}) collective-permute-start(bf16[4,96,768]{2,1,0:T(8,128)(2,1)S(1)} %get-tuple-element.303), channel_id=1, source_target_pairs={{0,8},{4,12},{8,0},{12,4},{16,24},{20,28},{24,16},{28,20},{1,9},{5... | collective-permute-start | bytes 1769480 | tf_op jit(solution)/shard_map/ppermute | solution.py:84
  673.4 33.1 %collective-permute-start.23 = (bf16[4,96,768]{2,1,0:T(8,128)(2,1)S(1)}, bf16[4,96,768]{2,1,0:T(8,128)(2,1)S(1)}, u32[]{:S(2)}, u32[]{:S(2)}) collective-permute-start(bf16[4,96,768]{2,1,0:T(8,128)(2,1)S(1)} %get-tuple-element.305), channel_id=1, source_target_pairs={{0,16},{4,20},{8,24},{12,28},{16,0},{20,4},{24,8},{28,12},{1,17},{... | collective-permute-start | bytes 1769480 | tf_op jit(solution)/shard_map/ppermute | solution.py:84
  674.9 43.9 %collective-permute-start.24 = (bf16[4,96,768]{2,1,0:T(8,128)(2,1)S(1)}, bf16[4,96,768]{2,1,0:T(8,128)(2,1)S(1)}, u32[]{:S(2)}, u32[]{:S(2)}) collective-permute-start(bf16[4,96,768]{2,1,0:T(8,128)(2,1)S(1)} %get-tuple-element.304), channel_id=1, source_target_pairs={{0,24},{4,28},{8,16},{12,20},{16,8},{20,12},{24,0},{28,4},{1,25},{... | collective-permute-start | bytes 1769480 | tf_op jit(solution)/shard_map/ppermute | solution.py:84
  694.1 80.4 %collective-permute-start.35 = (bf16[4,4,192,768]{3,2,1,0:T(8,128)(2,1)}, bf16[4,4,192,768]{3,2,1,0:T(8,128)(2,1)}, u32[]{:S(2)}, u32[]{:S(2)}) collective-permute-start(bf16[4,4,192,768]{3,2,1,0:T(8,128)(2,1)} %get-tuple-element.333), channel_id=1, source_target_pairs={{0,4},{4,0},{8,12},{12,8},{16,20},{20,16},{24,28},{28,24},{1,5},{5... | collective-permute-start | bytes 14155784 | tf_op jit(solution)/shard_map/ppermute | solution.py:84
  705.7 15.8 %collective-permute-start.18 = (bf16[96,768]{1,0:T(8,128)(2,1)S(1)}, bf16[96,768]{1,0:T(8,128)(2,1)S(1)}, u32[]{:S(2)}, u32[]{:S(2)}) collective-permute-start(bf16[96,768]{1,0:T(8,128)(2,1)S(1)} %get-tuple-element.370), channel_id=1, source_target_pairs={{0,1},{1,0},{2,3},{3,2},{4,5},{5,4},{6,7},{7,6},{8,9},{9,8},{10,11... | collective-permute-start | bytes 442376 | tf_op jit(solution)/shard_map/ppermute | solution.py:84
  706.5 15.1 %collective-permute-start.19 = (bf16[96,768]{1,0:T(8,128)(2,1)S(1)}, bf16[96,768]{1,0:T(8,128)(2,1)S(1)}, u32[]{:S(2)}, u32[]{:S(2)}) collective-permute-start(bf16[96,768]{1,0:T(8,128)(2,1)S(1)} %get-tuple-element.372), channel_id=1, source_target_pairs={{0,2},{1,3},{2,0},{3,1},{4,6},{5,7},{6,4},{7,5},{8,10},{9,11},{10,... | collective-permute-start | bytes 442376 | tf_op jit(solution)/shard_map/ppermute | solution.py:84
  718.8 8.5 collective-permute-start.20
  721.5 9.8 %collective-permute-start.25 = (bf16[96,768]{1,0:T(8,128)(2,1)S(1)}, bf16[96,768]{1,0:T(8,128)(2,1)S(1)}, u32[]{:S(2)}, u32[]{:S(2)}) collective-permute-start(bf16[96,768]{1,0:T(8,128)(2,1)S(1)} %get-tuple-element.373), channel_id=1, source_target_pairs={{0,1},{1,0},{2,3},{3,2},{4,5},{5,4},{6,7},{7,6},{8,9},{9,8},{10,11... | collective-permute-start | bytes 442376 | tf_op jit(solution)/shard_map/ppermute | solution.py:84
  721.6 16.2 %collective-permute-start.26 = (bf16[96,768]{1,0:T(8,128)(2,1)S(1)}, bf16[96,768]{1,0:T(8,128)(2,1)S(1)}, u32[]{:S(2)}, u32[]{:S(2)}) collective-permute-start(bf16[96,768]{1,0:T(8,128)(2,1)S(1)} %get-tuple-element.375), channel_id=1, source_target_pairs={{0,2},{1,3},{2,0},{3,1},{4,6},{5,7},{6,4},{7,5},{8,10},{9,11},{10,... | collective-permute-start | bytes 442376 | tf_op jit(solution)/shard_map/ppermute | solution.py:84
  727.4 10.5 %collective-permute-start.27 = (bf16[96,768]{1,0:T(8,128)(2,1)S(1)}, bf16[96,768]{1,0:T(8,128)(2,1)S(1)}, u32[]{:S(2)}, u32[]{:S(2)}) collective-permute-start(bf16[96,768]{1,0:T(8,128)(2,1)S(1)} %get-tuple-element.374), channel_id=1, source_target_pairs={{0,3},{1,2},{2,1},{3,0},{4,7},{5,6},{6,5},{7,4},{8,11},{9,10},{10,... | collective-permute-start | bytes 442376 | tf_op jit(solution)/shard_map/ppermute | solution.py:84
  758.4 29.1 %collective-permute-start.29 = (bf16[4,192,768]{2,1,0:T(8,128)(2,1)}, bf16[4,192,768]{2,1,0:T(8,128)(2,1)S(1)}, u32[]{:S(2)}, u32[]{:S(2)}) collective-permute-start(bf16[4,192,768]{2,1,0:T(8,128)(2,1)} %get-tuple-element.274), channel_id=1, source_target_pairs={{0,8},{4,12},{8,0},{12,4},{16,24},{20,28},{24,16},{28,20},{1,9},{5... | collective-permute-start | bytes 3538952 | tf_op jit(solution)/shard_map/ppermute | solution.py:84
  772.6 54.4 %collective-permute-start.30 = (bf16[4,192,768]{2,1,0:T(8,128)(2,1)}, bf16[4,192,768]{2,1,0:T(8,128)(2,1)}, u32[]{:S(2)}, u32[]{:S(2)}) collective-permute-start(bf16[4,192,768]{2,1,0:T(8,128)(2,1)} %get-tuple-element.276), channel_id=1, source_target_pairs={{0,16},{4,20},{8,24},{12,28},{16,0},{20,4},{24,8},{28,12},{1,17},{... | collective-permute-start | bytes 3538952 | tf_op jit(solution)/shard_map/ppermute | solution.py:84
  773.1 53.9 %collective-permute-start.31 = (bf16[4,192,768]{2,1,0:T(8,128)(2,1)}, bf16[4,192,768]{2,1,0:T(8,128)(2,1)}, u32[]{:S(2)}, u32[]{:S(2)}) collective-permute-start(bf16[4,192,768]{2,1,0:T(8,128)(2,1)} %get-tuple-element.275), channel_id=1, source_target_pairs={{0,24},{4,28},{8,16},{12,20},{16,8},{20,12},{24,0},{28,4},{1,25},{... | collective-permute-start | bytes 3538952 | tf_op jit(solution)/shard_map/ppermute | solution.py:84
  783.0 55.1 %collective-permute-start.36 = (bf16[4,192,768]{2,1,0:T(8,128)(2,1)}, bf16[4,192,768]{2,1,0:T(8,128)(2,1)}, u32[]{:S(2)}, u32[]{:S(2)}) collective-permute-start(bf16[4,192,768]{2,1,0:T(8,128)(2,1)} %get-tuple-element.283), channel_id=1, source_target_pairs={{0,8},{4,12},{8,0},{12,4},{16,24},{20,28},{24,16},{28,20},{1,9},{5... | collective-permute-start | bytes 3538952 | tf_op jit(solution)/shard_map/ppermute | solution.py:84
  784.5 90.5 %collective-permute-start.37 = (bf16[4,192,768]{2,1,0:T(8,128)(2,1)}, bf16[4,192,768]{2,1,0:T(8,128)(2,1)}, u32[]{:S(2)}, u32[]{:S(2)}) collective-permute-start(bf16[4,192,768]{2,1,0:T(8,128)(2,1)} %get-tuple-element.285), channel_id=1, source_target_pairs={{0,16},{4,20},{8,24},{12,28},{16,0},{20,4},{24,8},{28,12},{1,17},{... | collective-permute-start | bytes 3538952 | tf_op jit(solution)/shard_map/ppermute | solution.py:84
  787.4 87.6 %collective-permute-start.38 = (bf16[4,192,768]{2,1,0:T(8,128)(2,1)}, bf16[4,192,768]{2,1,0:T(8,128)(2,1)}, u32[]{:S(2)}, u32[]{:S(2)}) collective-permute-start(bf16[4,192,768]{2,1,0:T(8,128)(2,1)} %get-tuple-element.284), channel_id=1, source_target_pairs={{0,24},{4,28},{8,16},{12,20},{16,8},{20,12},{24,0},{28,4},{1,25},{... | collective-permute-start | bytes 3538952 | tf_op jit(solution)/shard_map/ppermute | solution.py:84
  829.6 52.2 %collective-permute-start.32 = (bf16[192,768]{1,0:T(8,128)(2,1)S(1)}, bf16[192,768]{1,0:T(8,128)(2,1)S(1)}, u32[]{:S(2)}, u32[]{:S(2)}) collective-permute-start(bf16[192,768]{1,0:T(8,128)(2,1)S(1)} %get-tuple-element.318), channel_id=1, source_target_pairs={{0,1},{1,0},{2,3},{3,2},{4,5},{5,4},{6,7},{7,6},{8,9},{9,8},{10,11... | collective-permute-start | bytes 884744 | tf_op jit(solution)/shard_map/ppermute | solution.py:84
  832.0 52.3 %collective-permute-start.33 = (bf16[192,768]{1,0:T(8,128)(2,1)S(1)}, bf16[192,768]{1,0:T(8,128)(2,1)S(1)}, u32[]{:S(2)}, u32[]{:S(2)}) collective-permute-start(bf16[192,768]{1,0:T(8,128)(2,1)S(1)} %get-tuple-element.320), channel_id=1, source_target_pairs={{0,2},{1,3},{2,0},{3,1},{4,6},{5,7},{6,4},{7,5},{8,10},{9,11},{10,... | collective-permute-start | bytes 884744 | tf_op jit(solution)/shard_map/ppermute | solution.py:84
  838.1 46.2 %collective-permute-start.34 = (bf16[192,768]{1,0:T(8,128)(2,1)S(1)}, bf16[192,768]{1,0:T(8,128)(2,1)S(1)}, u32[]{:S(2)}, u32[]{:S(2)}) collective-permute-start(bf16[192,768]{1,0:T(8,128)(2,1)S(1)} %get-tuple-element.319), channel_id=1, source_target_pairs={{0,3},{1,2},{2,1},{3,0},{4,7},{5,6},{6,5},{7,4},{8,11},{9,10},{10,... | collective-permute-start | bytes 884744 | tf_op jit(solution)/shard_map/ppermute | solution.py:84
  878.0 14.1 %collective-permute-start.39 = (bf16[192,768]{1,0:T(8,128)(2,1)S(1)}, bf16[192,768]{1,0:T(8,128)(2,1)S(1)}, u32[]{:S(2)}, u32[]{:S(2)}) collective-permute-start(bf16[192,768]{1,0:T(8,128)(2,1)S(1)} %get-tuple-element.329), channel_id=1, source_target_pairs={{0,1},{1,0},{2,3},{3,2},{4,5},{5,4},{6,7},{7,6},{8,9},{9,8},{10,11... | collective-permute-start | bytes 884744 | tf_op jit(solution)/shard_map/ppermute | solution.py:84
  881.8 22.7 %collective-permute-start.40 = (bf16[192,768]{1,0:T(8,128)(2,1)S(1)}, bf16[192,768]{1,0:T(8,128)(2,1)S(1)}, u32[]{:S(2)}, u32[]{:S(2)}) collective-permute-start(bf16[192,768]{1,0:T(8,128)(2,1)S(1)} %get-tuple-element.331), channel_id=1, source_target_pairs={{0,2},{1,3},{2,0},{3,1},{4,6},{5,7},{6,4},{7,5},{8,10},{9,11},{10,... | collective-permute-start | bytes 884744 | tf_op jit(solution)/shard_map/ppermute | solution.py:84
  881.8 22.7 %collective-permute-start.41 = (bf16[192,768]{1,0:T(8,128)(2,1)S(1)}, bf16[192,768]{1,0:T(8,128)(2,1)S(1)}, u32[]{:S(2)}, u32[]{:S(2)}) collective-permute-start(bf16[192,768]{1,0:T(8,128)(2,1)S(1)} %get-tuple-element.330), channel_id=1, source_target_pairs={{0,3},{1,2},{2,1},{3,0},{4,7},{5,6},{6,5},{7,4},{8,11},{9,10},{10,... | collective-permute-start | bytes 884744 | tf_op jit(solution)/shard_map/ppermute | solution.py:84
  (158 other events, 3513.8 us)
Sparse Core Ops, SparseCore 0:
  11.4 122.2 all-gather.3
  137.3 80.4 all-gather.5
  221.2 79.9 all-gather.7

commit v2 on v1

--- a/solution.py
+++ b/solution.py
@@ -4,6 +4,7 @@
 import jax.numpy as jnp
 from jax import lax
 from jax.experimental import pallas as pl
+from jax.experimental.pallas import tpu as pltpu
 from jax.sharding import PartitionSpec as P
 
 HEADS = 12
@@ -117,13 +118,17 @@
     return total
 
 
+def head_quads(value, flip):
+    return swapped(value, "dp", 2 * flip)
+
+
 def scatter_rows(partial):
     quads, fsdp = lax.axis_size("dp") // 2, lax.axis_size("fsdp")
     width = partial.shape[1]
     part = partial.astype(jnp.bfloat16).reshape(2, quads, fsdp, -1, width)
     part = sum_low([part[0], swapped(part[1], "dp", 1)]).astype(jnp.bfloat16)
     part = sum_low(
-        [part[0]] + [swapped(part[flip], "dp", 2 * flip) for flip in range(1, quads)]
+        [part[0]] + [head_quads(part[flip], flip) for flip in range(1, quads)]
     ).astype(jnp.bfloat16)
     return sum_low([part[0]] + [swapped(part[flip], "fsdp", flip) for flip in range(1, fsdp)])
 
@@ -292,6 +297,35 @@
     )
     fresh = weight - learn_rate * (rise + decay * weight)
     return (fresh, jnp.stack([first, root]), fresh.astype(jnp.bfloat16))
+
+
+def adam_kernel(decay, scale_ref, weight_ref, moments_ref, grad_ref, fresh_ref, state_ref, copy_ref):
+    fresh, state, copy = adam_update(
+        weight_ref[...], moments_ref[...], grad_ref[...] / scale_ref[0] * scale_ref[1], decay
+    )
+    fresh_ref[...], state_ref[...], copy_ref[...] = fresh, state, copy
+
+
+def adam_blocks(weight, moments, grad, count, factor, decay):
+    rows, width = weight.shape
+    step = rows if rows <= 320 else max(size for size in range(16, 321, 16) if rows % size == 0)
+    flat = pl.BlockSpec((step, width), lambda at: (at, 0))
+    pair = pl.BlockSpec((2, step, width), lambda at: (0, at, 0))
+    return pl.pallas_call(
+        functools.partial(adam_kernel, decay),
+        grid=(rows // step,),
+        in_specs=[pl.BlockSpec(memory_space=pltpu.SMEM), flat, pair, flat],
+        out_specs=[flat, pair, flat],
+        out_shape=[
+            jax.ShapeDtypeStruct(weight.shape, jnp.float32),
+            jax.ShapeDtypeStruct(moments.shape, jnp.float32),
+            jax.ShapeDtypeStruct(weight.shape, jnp.bfloat16),
+        ],
+        cost_estimate=pl.CostEstimate(
+            flops=20 * rows * width, transcendentals=rows * width, bytes_accessed=30 * rows * width
+        ),
+        name="adam_blocks",
+    )(jnp.stack([count, factor]), weight, moments, grad)
 
 
 def shards(
@@ -332,7 +366,7 @@
     vector_share = vector_params.shape[0]
     block = 8 * width + hidden_width
     vector_rows = -(-vector_share // width)
-    small_rows = position_share + vector_rows
+    small_rows = -(-(position_share + vector_rows) // 16) * 16
 
     words = token_ids.reshape(tokens)
     owner = words // rows_each
@@ -377,6 +411,55 @@
         return jnp.dot(seat_matrix(turn), rows, preferred_element_type=jnp.float32)
 
     heard_first = requests(0, targets, loss_mask)
+    fold = hidden_share // row_share
+    position_lanes = position_share * width // row_share
+    vector_lanes = 128 * -(-vector_share // (128 * row_share))
+    small = [
+        position_table.astype(low).reshape(row_share, position_lanes),
+        jnp.pad(vector_params.astype(low), (0, row_share * vector_lanes - vector_share)).reshape(
+            row_share, vector_lanes
+        ),
+    ]
+    mixed_share = [
+        jnp.concatenate(
+            (small if layer == 0 else [])
+            + [attend_weight[layer].astype(low), project_weight[layer].astype(low), expand_weight[layer].astype(low)]
+            + [
+                contract_weight[layer, at : at + row_share].astype(low)
+                for at in range(0, hidden_share, row_share)
+            ],
+            axis=1,
+        )
+        for layer in range(layers)
+    ]
+    mixed_all = []
+    for layer in range(layers):
+        mixed_all.append(lax.all_gather(mixed_share[layer], BOTH, axis=0, tiled=True))
+    small_all, mixed_all[0] = (
+        mixed_all[0][:, : position_lanes + vector_lanes],
+        mixed_all[0][:, position_lanes + vector_lanes :],
+    )
+    contract_at = 4 * width + hidden_width
+    contract_all = [
+        jnp.stack(
+            [
+                share[:, contract_at + at * width : contract_at + (at + 1) * width].reshape(
+                    devices, row_share, width
+                )
+                for at in range(fold)
+            ],
+            axis=1,
+        ).reshape(hidden_width, width)
+        for share in mixed_all
+    ]
+    attend_all = [share[:, : 3 * width] for share in mixed_all]
+    project_all = [share[:, 3 * width : 4 * width] for share in mixed_all]
+    expand_all = [share[:, 4 * width : contract_at] for share in mixed_all]
+    position_all = small_all[:, :position_lanes].reshape(-1, width)
+    vectors_f = (
+        small_all[:, position_lanes:].reshape(devices, -1)[:, :vector_share].reshape(-1).astype(jnp.float32)
+    )
+
     turns = jnp.max(heard_first[:, slots_each]) // slots_each + 1
     embedded = looked_up(0, heard_first)
     _, embedded = lax.while_loop(
@@ -385,33 +468,14 @@
         (jnp.int32(1), embedded),
     )
 
-    small = jnp.concatenate(
-        [
-            position_table.astype(low),
-            jnp.pad(vector_params.astype(low), (0, vector_rows * width - vector_share)).reshape(vector_rows, width),
-        ]
-    )
-    mixed_share = [
-        jnp.concatenate(
-            [attend_weight[layer], project_weight[layer], expand_weight[layer]], axis=1
-        ).astype(low)
-        for layer in range(layers)
-    ]
-    small_all = spread(small).reshape(devices, small_rows, width)
-    mixed_all = [lax.all_gather(share, BOTH, axis=0, tiled=True) for share in mixed_share]
-    contract_all = lax.all_gather(contract_weight.astype(low), BOTH, axis=1, tiled=True)
-    attend_all = [share[:, : 3 * width] for share in mixed_all]
-    project_all = [share[:, 3 * width : 4 * width] for share in mixed_all]
-    expand_all = [share[:, 4 * width :] for share in mixed_all]
-    position_all = small_all[:, :position_share].reshape(-1, width)
-    vectors_f = (
-        small_all[:, position_share:].reshape(devices, -1)[:, :vector_share].reshape(-1).astype(jnp.float32)
-    )
-
     order = me ^ relative_offsets()
     marks = jnp.take(heard_first[:, slots_each + 1 :].reshape(devices, 2, -1), order, axis=0)
     target_local = marks[:, 0].reshape(-1) - me * rows_each
     valid = marks[:, 1].reshape(-1).astype(jnp.float32)
+
+    hit = jnp.arange(rows_each, dtype=jnp.int32)[None, :] == target_local[:, None]
+    target_rows = jnp.dot(hit.astype(low), table_b, preferred_element_type=jnp.float32).astype(low)
+    embedded, target_rows = lax.optimization_barrier((embedded, target_rows))
 
     placed = [positions_of(doc_lengths[micro, 0], doc_order[micro, 0], slot) for micro in range(micro_count)]
     position = jnp.concatenate([pair[0] for pair in placed])
@@ -482,9 +546,10 @@
     )
     rows_all = gather_rows(final.astype(low))
     logits = times_transpose(rows_all, table_b)
-    hit = jnp.arange(rows_each, dtype=jnp.int32)[None, :] == target_local[:, None]
     peak = jnp.max(logits, axis=1)
-    totals = jnp.sum(jnp.exp(logits - peak[:, None]), axis=1)
+    raised = jnp.exp(logits - peak[:, None])
+    totals = jnp.sum(raised, axis=1)
+    soft_rows = jnp.dot(raised.astype(low), table_b, preferred_element_type=jnp.float32)
     chosen = jnp.sum(jnp.where(hit, logits, 0.0), axis=1)
     stats = jnp.stack([peak.reshape(devices, -1), totals.reshape(devices, -1)], axis=1)
     inverse = jnp.argsort(order)
@@ -498,8 +563,12 @@
     grad_logits = (
         (jnp.exp(logits - log_rows[:, None]) - hit.astype(jnp.float32)) * valid[:, None]
     ).astype(low)
-    grad_final = scatter_rows(jnp.dot(grad_logits, table_b, preferred_element_type=jnp.float32))
+    share_rows = jnp.exp(peak - log_rows) * valid
+    grad_final = scatter_rows(
+        share_rows[:, None] * soft_rows - valid[:, None] * target_rows.astype(jnp.float32)
+    )
     table_grad = outer_sum(grad_logits, rows_all)
+    grad_final, table_grad = lax.optimization_barrier((grad_final, table_grad))
     grad_rows, grad_final_gain, grad_final_bias = norm_backward(
         grad_final, scaled_final, inverse_final, final_gain
     )
@@ -548,9 +617,6 @@
             wide_sent[layer + 1] = send_deep(wide_sent[layer + 1])
         grad_mixed = attend_backward(mixed_b, document, log_total, grad_attended)
         attend_grad = outer_sum(normed_b, grad_mixed).astype(low)
-        narrow_sent[layer] = send_core(
-            lanes_to_rows(attend_grad, devices, width) + lanes_to_rows(project_grad, devices, width)
-        )
         grad_mixed_f = grad_mixed.astype(jnp.float32)
         grad_query_bias = jnp.sum(grad_mixed_f[:, :width], axis=0)
         grad_value_bias = jnp.sum(grad_mixed_f[:, 2 * width :], axis=0)
@@ -559,7 +625,6 @@
             grad_normed, scaled_one, inverse_one, gain_one
         )
         grad_state = grad_middle + grad_in
-        narrow_sent[layer] = send_quads(narrow_sent[layer])
         layer_grads[layer] = jnp.concatenate(
             [
                 grad_gain_one,
@@ -574,33 +639,28 @@
             ]
         )
 
-    grad_embedded = grad_state.astype(low)
-    position_grad = outer_sum(position_hot, grad_embedded).astype(low)
-    vector_grad = jnp.concatenate(layer_grads + [grad_final_gain, grad_final_bias])
-    vector_grad = jnp.pad(
-        vector_grad.astype(low).reshape(devices, vector_share),
-        ((0, 0), (0, vector_rows * width - vector_share)),
-    )
+        narrow = lanes_to_rows(attend_grad, devices, width) + lanes_to_rows(project_grad, devices, width)
+        if layer == 0:
+            grad_embedded = grad_state.astype(low)
+            position_grad = outer_sum(position_hot, grad_embedded).astype(low)
+            vector_grad = jnp.concatenate(layer_grads + [grad_final_gain, grad_final_bias]).astype(low)
+            vector_grad = jnp.pad(
+                vector_grad.reshape(devices, vector_share),
+                ((0, 0), (0, (small_rows - position_share) * width - vector_share)),
+            )
+            small_grad = [
+                position_grad.reshape(devices, position_share, width),
+                vector_grad.reshape(devices, small_rows - position_share, width),
+            ]
+            narrow = narrow + [jnp.concatenate(small_grad, axis=1)]
+        narrow_sent[layer] = send_core(narrow)
+        narrow_sent[layer] = send_quads(narrow_sent[layer])
 
     def returned(turn):
         return outer_sum(seat_matrix(turn), grad_embedded).astype(low).reshape(devices, slots_each, width)
 
-    came = lax.all_to_all(
-        jnp.concatenate(
-            [
-                returned(0),
-                position_grad.reshape(devices, position_share, width),
-                vector_grad.reshape(devices, vector_rows, width),
-            ],
-            axis=1,
-        ),
-        BOTH,
-        0,
-        0,
-        tiled=True,
-    )
-    small_sum = jnp.sum(came[:, slots_each:].astype(jnp.float32), axis=0)
-    table_grad = table_grad + outer_sum(wanted_of(heard_first), came[:, :slots_each].reshape(slots_all, width))
+    came = lax.all_to_all(returned(0), BOTH, 0, 0, tiled=True)
+    table_grad = table_grad + outer_sum(wanted_of(heard_first), came.reshape(slots_all, width))
 
     def later_turn(carry):
         turn, total = carry
@@ -621,8 +681,9 @@
     )
     attend_sum = jnp.stack([rows_to_lanes(total[: 3 * row_share], 3) for total in narrow_sums])
     project_sum = jnp.stack([total[3 * row_share : 4 * row_share] for total in narrow_sums])
+    small_sum = narrow_sums[0][4 * row_share :]
     position_sum = small_sum[:position_share]
-    vector_sum = small_sum[position_share:].reshape(-1)[:vector_share]
+    vector_sum = small_sum[position_share : position_share + vector_rows].reshape(-1)[:vector_share]
 
     sums = (table_sum, position_sum, attend_sum, project_sum, expand_sum, contract_sum, vector_sum)
     squares = jnp.zeros((), jnp.float32)
@@ -652,8 +713,18 @@
         vector_moments,
     )
     decays = (decay_rate, decay_rate, decay_rate, decay_rate, decay_rate, decay_rate, 0.0)
+
+    def updated(weight, moment, grad, decay):
+        if weight.ndim < 2:
+            return adam_update(weight, moment, grad / count * factor, decay)
+        lanes = weight.shape[-1]
+        fresh, pair, copy = adam_blocks(
+            weight.reshape(-1, lanes), moment.reshape(2, -1, lanes), grad.reshape(-1, lanes), count, factor, decay
+        )
+        return (fresh.reshape(weight.shape), pair.reshape(moment.shape), copy.reshape(weight.shape))
+
     table_new, position_new, attend_new, project_new, expand_new, contract_new, vector_new = [
-        adam_update(weight, moment, grad / count * factor, decay)
+        updated(weight, moment, grad, decay)
         for weight, moment, grad, decay in zip(weights, moments, sums, decays)
     ]
     return (

time: 989 us -> 922 us (0.932)
  waiting for transfers between devices: 440 us -> 384 us
  other arithmetic: 120 us -> 85.4 us
  Pallas kernels: 58.5 us -> 77 us
  matrix products: 169 us -> 181 us
    pallas_call x0 -> x6, Pallas kernels: none -> 29 us  [adam_blocks(): pl.pallas_call(functools.partial(adam_kernel, decay), grid=(rows // step,...]
    another operation x9 -> x1, other arithmetic: 25.3 us -> 0.6 us  [adam_update(): return (fresh, jnp.stack([first, root]), fresh.astype(jnp.bfloat16))]
    ppermute x42, waiting for transfers between devices: 217 us -> 195 us  [swapped(): lax.ppermute(value, axis, [(index, index ^ flip) for index in range(size)])]
    all_to_all x2 -> x1, waiting for transfers between devices: 33.9 us -> 13.4 us  [spread(): lax.all_to_all(jnp.broadcast_to(value[None], (count,) + value.shape), BOT...]
    all_to_all x1, waiting for transfers between devices: 53.9 us -> 41.9 us  [looked_up(): rows = lax.all_to_all(rows, BOTH, 0, 0, tiled=True)]
    dot_general x9, matrix products: 46.2 us -> 56.6 us  [times_transpose(): lax.dot_general(left, right, (((1,), (1,)), ((), ())), preferred_element_...]
    pallas_call x2, Pallas kernels: 29.9 us -> 19.6 us  [attend_forward(): pl.pallas_call(functools.partial(attend_kernel, width // HEADS), grid=(do...]
    dot_general x1 -> x2, matrix products: 11 us -> 20.6 us  [the longest x1 10.7 us: shards(): jnp.dot(raised.astype(low), table_b, preferred_element_type=jnp.float32)]
  transfers between devices with their start and end apart: 50 -> 48, of which waited for: 28 -> 26; matrix products, arithmetic and copies ran while one was open for 15% -> 14% of each run, Pallas kernels for 1% -> 0%
where the time goes in v2:
time: 922 us; the launch traced here: 912 us
  waiting for transfers between devices  384 us (42%)
  matrix products  181 us (20%)
  other arithmetic  85.4 us (9%)
  Pallas kernels  77 us (8%)
  local copies, waits for them, and re-layouts  73.6 us (8%)
  starting transfers between devices  69.7 us (8%)
  between operations  30.4 us (3%)
  blocking collectives  10.9 us (1%)
    ppermute x42, waiting for transfers between devices, swapped(): lax.ppermute(value, axis, [(index, index ^ flip) for index in range(size)])  195 us
    all_gather x2, waiting for transfers between devices, shards(): lax.all_gather(mixed_share[layer], BOTH, axis=0, tiled=True)  133 us
    dot_general x12, matrix products, outer_sum(): lax.dot_general(left, right, (((0,), (0,)), ((), ())), preferred_element_...  57.8 us
    dot_general x9, matrix products, times_transpose(): lax.dot_general(left, right, (((1,), (1,)), ((), ())), preferred_element_...  56.6 us
    ppermute x42, starting transfers between devices, swapped(): lax.ppermute(value, axis, [(index, index ^ flip) for index in range(size)])  49.1 us
    all_to_all x1, waiting for transfers between devices, looked_up(): rows = lax.all_to_all(rows, BOTH, 0, 0, tiled=True)  41.9 us
    unnamed x272, local copies, waits for them, and re-layouts  37.5 us
    pallas_call x6, Pallas kernels, adam_blocks(): pl.pallas_call(functools.partial(adam_kernel, decay), grid=(rows // step,...  29 us
  transfers between devices with their start and end apart: 48, of which 26 were waited for; matrix products, arithmetic and copies ran while one was open for 14% of the time, Pallas kernels for 0%

profile of v2, /device:TPU:0, one launch (start us, length us, event | category | flops | bytes accessed | tf_op | source)
XLA Modules:
  0.0 912.3 jit_solution(15230790532627131751)
XLA Ops:
  22.1 7.3 all-to-all-start.4
  37.7 6.1 fusion.70
  43.8 5.8 all-to-all-start.5
  57.5 9.8 %fusion.53 = bf16[2048,768]{1,0:T(8,128)(2,1)} fusion(bf16[1600,768]{1,0:T(8,128)(2,1)} %convert_element_type.486, s32[2048]{0:T(1024)S(1)} %sub.258), kind=kOutput, calls=%fused_computation.91 | convolution fusion | flops 5038014464 | bytes 5611520 | tf_op jit(solution)/shard_map/dot_general | solution.py:477
  67.3 41.9 %all-to-all-done.5 = bf16[32,32,768]{2,1,0:T(8,128)(2,1)S(1)} async-done(((bf16[32,32,768]{2,1,0:T(8,128)(2,1)}), bf16[32,32,768]{2,1,0:T(8,128)(2,1)S(1)}, u32[]{:S(2)}, u32[]{:S(2)}) %all-to-all-start.5) | async-done | bytes 1572896 | tf_op jit(solution)/shard_map/all_to_all | solution.py:410
  110.8 31.3 %all-gather.5.cloned.1.call-done = bf16[768,9216]{1,0:T(8,128)(2,1)} async-done(((bf16[24,9216]{1,0:T(8,128)(2,1)}), bf16[768,9216]{1,0:T(8,128)(2,1)}) %all-gather.5.cloned.1.call-update) | async-done | bytes 14155792 | tf_op jit(solution)/shard_map/all_gather | solution.py:437
  147.3 101.9 %all-gather.3.cloned.1.call-done = bf16[768,9600]{1,0:T(8,128)(2,1)} async-done(((bf16[24,9600]{1,0:T(8,128)(2,1)}), bf16[768,9600]{1,0:T(8,128)(2,1)}) %all-gather.3.cloned.1.call-update) | async-done | bytes 14745616 | tf_op jit(solution)/shard_map/all_gather | solution.py:437
  254.5 5.6 fusion.39.mixed_ref
  260.1 9.8 %attend_forward.2 = (bf16[512,768]{1,0:T(8,128)(2,1)}, f32[512,768]{1,0:T(8,128)}) custom-call(s32[2,1,256]{2,1,0:T(1,128)} %broadcast_in_dim.134.row_ref, s32[2,256,1]{2,1,0:T(8,128)} %copy.195.column_ref, bf16[512,2304]{1,0:T(8,128)(2,1)} %fusion.39.mixed_ref), custom_call_target="tpu_custom_call" | custom-call | flops 402653184 | bytes 6291456 | tf_op jit(solution)/shard_map/attend_forward/pallas_call | solution.py:259
  276.2 6.6 fusion.47
  287.3 5.7 fusion.40.mixed_ref
  293.1 9.8 %attend_forward.3 = (bf16[512,768]{1,0:T(8,128)(2,1)}, f32[512,768]{1,0:T(8,128)}) custom-call(s32[2,1,256]{2,1,0:T(1,128)} %broadcast_in_dim.134.row_ref, s32[2,256,1]{2,1,0:T(8,128)} %copy.195.column_ref, bf16[512,2304]{1,0:T(8,128)(2,1)} %fusion.40.mixed_ref), custom_call_target="tpu_custom_call" | custom-call | flops 402653184 | bytes 6291456 | tf_op jit(solution)/shard_map/attend_forward/pallas_call | solution.py:259
  305.7 5.7 fusion.43
  334.7 9.4 %collective-permute-done.5 = bf16[4,64,768]{2,1,0:T(8,128)(2,1)S(1)} collective-permute-done((bf16[4,64,768]{2,1,0:T(8,128)(2,1)S(1)}, bf16[4,64,768]{2,1,0:T(8,128)(2,1)S(1)}, u32[]{:S(2)}, u32[]{:S(2)}) %collective-permute-start.5) | collective-permute-done | bytes 393248 | tf_op jit(solution)/shard_map/ppermute | solution.py:85
  344.1 7.0 collective-permute-done.4
  357.7 8.2 fusion.179
  365.9 6.8 select_reduce_fusion.2
  379.0 13.4 %all-to-all-done.6 = f32[32,32,128]{2,1,0:T(8,128)S(1)} async-done(((f32[32,32,128]{2,1,0:T(8,128)}), f32[32,32,128]{2,1,0:T(8,128)S(1)}, u32[]{:S(2)}, u32[]{:S(2)}) %all-to-all-start.6) | async-done | bytes 524320 | tf_op jit(solution)/shard_map/all_to_all | solution.py:90
  397.1 10.7 %subtract_convert_fusion = bf16[2048,768]{1,0:T(8,128)(2,1)S(1)} fusion(bf16[2048,768]{1,0:T(8,128)(2,1)} %fusion.53, bf16[1600,768]{1,0:T(8,128)(2,1)} %get-tuple-element.667, f32[2048,1600]{0,1:T(8,128)} %get-tuple-element.491, f32[2048]{0:T(1024)S(1)} %get-tuple-element.490, f32[2048]{0:T(1024)S(1)} %convert_element_type.520, ...), kind=kOutput, calls=%fused_computation.63 | convolution fusion | flops 5047582720 | bytes 21880832 | tf_op jit(solution)/shard_map/dot_general | solution.py:552
  419.5 11.7 %fusion.19 = f32[1600,768]{1,0:T(8,128)} fusion(bf16[2048,768]{1,0:T(8,128)(2,1)S(1)} %bitcast.553, f32[2048,1600]{0,1:T(8,128)} %get-tuple-element.491, f32[2048]{0:T(1024)S(1)} %convert_element_type.520, f32[2048]{0:T(1024)S(1)} %select_n.292, s32[2048]{0:T(1024)S(1)} %sub.258), kind=kOutput, calls=%fused_computation.43 | convolution fusion | flops 5052825600 | bytes 21192704 | tf_op jit(solution)/shard_map/dot_general | solution.py:69
  431.2 5.6 collective-permute-done.9
  449.7 9.6 %fusion.181 = (bf16[3072]{0:T(1024)(128)(2,1)S(1)}, bf16[512,3072]{1,0:T(8,128)(2,1)S(1)}) fusion(f32[512,3072]{1,0:T(8,128)} %copy-done.98, f32[3072]{0:T(1024)S(1)} %copy-done.68, bf16[3072,768]{1,0:T(8,128)(2,1)} %bitcast.532, f32[512,768]{1,0:T(8,128)S(1)} %fusion.104), kind=kOutput, calls=%fused_computation.505 | convolution fusion | flops 2449339392 | bytes 15747072 | tf_op jit(solution)/shard_map/dot_general | solution.py:75
  459.3 6.5 multiply_reduce_fusion.1
  470.1 14.3 %attend_backward.2 = bf16[512,2304]{1,0:T(8,128)(2,1)} custom-call(s32[2,1,256]{2,1,0:T(1,128)} %broadcast_in_dim.134.row_ref, s32[2,256,1]{2,1,0:T(8,128)} %copy.195.column_ref, bf16[512,2304]{1,0:T(8,128)(2,1)} %fusion.40.mixed_ref, f32[512,768]{1,0:T(8,128)} %get-tuple-element.202.log_ref, bf16[512,768]{1,0:T(8,128)(2,1)} %convolution_convert_fusion.9.grad_ref), custom_call_target="tpu_custom_call" | custom-call | flops 1006632960 | bytes 6291456 | tf_op jit(solution)/shard_map/attend_backward/pallas_call | solution.py:276
  484.4 5.6 multiply_reduce_fusion.2
  490.7 9.3 %fusion.180 = (bf16[3072]{0:T(1024)(128)(2,1)S(1)}, bf16[512,3072]{1,0:T(8,128)(2,1)S(1)}) fusion(f32[512,3072]{1,0:T(8,128)} %copy-done.97, f32[3072]{0:T(1024)S(1)} %copy-done.67, bf16[3072,768]{1,0:T(8,128)(2,1)} %bitcast.537, f32[512,768]{1,0:T(8,128)S(1)} %get-tuple-element.294), kind=kOutput, calls=%fused_computation.504 | convolution fusion | flops 2449339392 | bytes 15747072 | tf_op jit(solution)/shard_map/dot_general | solution.py:75
  500.0 6.5 multiply_reduce_fusion.3
  512.5 14.1 %attend_backward.3 = bf16[512,2304]{1,0:T(8,128)(2,1)} custom-call(s32[2,1,256]{2,1,0:T(1,128)} %broadcast_in_dim.134.row_ref, s32[2,256,1]{2,1,0:T(8,128)} %copy.195.column_ref, bf16[512,2304]{1,0:T(8,128)(2,1)} %fusion.39.mixed_ref, f32[512,768]{1,0:T(8,128)} %get-tuple-element.203.log_ref, bf16[512,768]{1,0:T(8,128)(2,1)} %convolution_convert_fusion.8.grad_ref), custom_call_target="tpu_custom_call" | custom-call | flops 1006632960 | bytes 6291456 | tf_op jit(solution)/shard_map/attend_backward/pallas_call | solution.py:276
  539.9 9.0 convolution_convert_fusion.1
  548.9 6.5 convolution_convert_fusion
  555.4 6.0 convolution_convert_fusion.3
  561.4 4.4 multiply_reduce_fusion.4
  602.1 5.0 convolution_convert_fusion.2
  621.9 16.7 %collective-permute-done.24 = bf16[4,96,768]{2,1,0:T(8,128)(2,1)S(1)} collective-permute-done((bf16[4,96,768]{2,1,0:T(8,128)(2,1)S(1)}, bf16[4,96,768]{2,1,0:T(8,128)(2,1)S(1)}, u32[]{:S(2)}, u32[]{:S(2)}) %collective-permute-start.24) | collective-permute-done | bytes 589856 | tf_op jit(solution)/shard_map/ppermute | solution.py:85
  638.6 10.4 %collective-permute-done.23 = bf16[4,96,768]{2,1,0:T(8,128)(2,1)S(1)} collective-permute-done((bf16[4,96,768]{2,1,0:T(8,128)(2,1)S(1)}, bf16[4,96,768]{2,1,0:T(8,128)(2,1)S(1)}, u32[]{:S(2)}, u32[]{:S(2)}) %collective-permute-start.23) | collective-permute-done | bytes 589856 | tf_op jit(solution)/shard_map/ppermute | solution.py:85
  657.1 5.1 fusion.15
  665.4 4.4 multiply_reduce_fusion
  674.3 14.7 %collective-permute-done.17 = bf16[4,112,768]{2,1,0:T(8,128)(2,1)S(1)} collective-permute-done((bf16[4,112,768]{2,1,0:T(8,128)(2,1)S(1)}, bf16[4,112,768]{2,1,0:T(8,128)(2,1)S(1)}, u32[]{:S(2)}, u32[]{:S(2)}) %collective-permute-start.17) | collective-permute-done | bytes 688160 | tf_op jit(solution)/shard_map/ppermute | solution.py:85
  689.0 13.0 %collective-permute-done.16 = bf16[4,112,768]{2,1,0:T(8,128)(2,1)S(1)} collective-permute-done((bf16[4,112,768]{2,1,0:T(8,128)(2,1)S(1)}, bf16[4,112,768]{2,1,0:T(8,128)(2,1)S(1)}, u32[]{:S(2)}, u32[]{:S(2)}) %collective-permute-start.16) | collective-permute-done | bytes 688160 | tf_op jit(solution)/shard_map/ppermute | solution.py:85
  708.0 5.3 add_convert_fusion
  733.7 12.2 %collective-permute-done.38 = bf16[4,192,768]{2,1,0:T(8,128)(2,1)S(1)} collective-permute-done((bf16[4,192,768]{2,1,0:T(8,128)(2,1)S(1)}, bf16[4,192,768]{2,1,0:T(8,128)(2,1)S(1)}, u32[]{:S(2)}, u32[]{:S(2)}) %collective-permute-start.38) | collective-permute-done | bytes 1179680 | tf_op jit(solution)/shard_map/ppermute | solution.py:85
  754.5 16.8 %collective-permute-done.37 = bf16[4,192,768]{2,1,0:T(8,128)(2,1)S(1)} collective-permute-done((bf16[4,192,768]{2,1,0:T(8,128)(2,1)}, bf16[4,192,768]{2,1,0:T(8,128)(2,1)S(1)}, u32[]{:S(2)}, u32[]{:S(2)}) %collective-permute-start.37) | collective-permute-done | bytes 1179680 | tf_op jit(solution)/shard_map/ppermute | solution.py:85
  777.4 19.3 %collective-permute-done.31 = bf16[4,192,768]{2,1,0:T(8,128)(2,1)} collective-permute-done((bf16[4,192,768]{2,1,0:T(8,128)(2,1)}, bf16[4,192,768]{2,1,0:T(8,128)(2,1)}, u32[]{:S(2)}, u32[]{:S(2)}) %collective-permute-start.31) | collective-permute-done | bytes 1179680 | tf_op jit(solution)/shard_map/ppermute | solution.py:85
  797.3 22.8 %collective-permute-done.30 = bf16[4,192,768]{2,1,0:T(8,128)(2,1)} collective-permute-done((bf16[4,192,768]{2,1,0:T(8,128)(2,1)}, bf16[4,192,768]{2,1,0:T(8,128)(2,1)}, u32[]{:S(2)}, u32[]{:S(2)}) %collective-permute-start.30) | collective-permute-done | bytes 1179680 | tf_op jit(solution)/shard_map/ppermute | solution.py:85
  827.8 7.2 collective-permute-done.34
  835.0 16.1 %collective-permute-done.33 = bf16[192,768]{1,0:T(8,128)(2,1)S(1)} collective-permute-done((bf16[192,768]{1,0:T(8,128)(2,1)S(1)}, bf16[192,768]{1,0:T(8,128)(2,1)S(1)}, u32[]{:S(2)}, u32[]{:S(2)}) %collective-permute-start.33) | collective-permute-done | bytes 294944 | tf_op jit(solution)/shard_map/ppermute | solution.py:85
  856.5 10.9 %all_to_all.83 = f32[32,1,3]{2,1,0:T(1,128)S(1)} all-to-all(f32[32,1,3]{2,1,0:T(1,128)S(1)} %broadcast_in_dim.149), channel_id=1, replica_groups=mesh['dp'=8,'fsdp'=4] {'dp','fsdp'}, dimensions={0} | all-to-all | bytes 768 | tf_op jit(solution)/shard_map/all_to_all | solution.py:90
  872.7 16.0 %adam_blocks.6 = (f32[1600,768]{1,0:T(8,128)}, f32[2,1600,768]{2,1,0:T(8,128)}, bf16[1600,768]{1,0:T(8,128)(2,1)}) custom-call(f32[2]{0:T(128)} %pad_maximum_fusion.15.scale_ref, f32[1600,768]{1,0:T(8,128)} %weight_ref.2, f32[2,1600,768]{2,1,0:T(8,128)} %moments_ref.2, f32[1600,768]{1,0:T(8,128)} %get-tuple-element.204.grad_ref), custom_call_target="tpu_custom_call" | custom-call | flops 24576000 | bytes 36864000 | tf_op jit(solution)/shard_map/adam_blocks/pallas_call | solution.py:314
  (592 shorter events, 273.7 us)
Async XLA Ops:
  7.2 135.0 %all-gather.5.cloned.1.call-start = ((), (), s32[]{:S(2)}) async-start(), calls=%async_computation.10 | async-start | bytes 14598144 | tf_op jit(solution)/shard_map/all_gather | solution.py:437
  13.9 235.3 %all-gather.3.cloned.1.call-start = ((), (), s32[]{:S(2)}) async-start(), calls=%async_computation.9 | async-start | bytes 15206400 | tf_op jit(solution)/shard_map/all_gather | solution.py:437
  22.1 15.6 %all-to-all-start.4 = ((s32[32,1,161]{2,1,0:T(1,128)}), s32[32,1,161]{2,1,0:T(1,128)S(1)}, u32[]{:S(2)}, u32[]{:S(2)}) async-start(s32[32,1,161]{2,1,0:T(1,128)} %all_to_all.57), calls=%async_computation.4 | async-start | bytes 65536 | tf_op jit(solution)/shard_map/all_to_all | solution.py:397
  43.8 65.5 %all-to-all-start.5 = ((bf16[32,32,768]{2,1,0:T(8,128)(2,1)}), bf16[32,32,768]{2,1,0:T(8,128)(2,1)S(1)}, u32[]{:S(2)}, u32[]{:S(2)}) async-start(bf16[32,32,768]{2,1,0:T(8,128)(2,1)} %bitcast.9), calls=%async_computation.5 | async-start | bytes 3145728 | tf_op jit(solution)/shard_map/all_to_all | solution.py:410
  319.4 7.6 collective-permute-start.2
  321.2 9.9 %collective-permute-start.1 = (bf16[64,768]{1,0:T(8,128)(2,1)S(1)}, bf16[64,768]{1,0:T(8,128)(2,1)S(1)}, u32[]{:S(2)}, u32[]{:S(2)}) collective-permute-start(bf16[64,768]{1,0:T(8,128)(2,1)S(1)} %add_convert_fusion.9), channel_id=1, source_target_pairs={{0,2},{1,3},{2,0},{3,1},{4,6},{5,7},{6,4},{7,5},{8,10},{9,11},{10,... | collective-permute-start | bytes 294920 | tf_op jit(solution)/shard_map/ppermute | solution.py:85
  321.8 9.3 %collective-permute-start = (bf16[64,768]{1,0:T(8,128)(2,1)S(1)}, bf16[64,768]{1,0:T(8,128)(2,1)S(1)}, u32[]{:S(2)}, u32[]{:S(2)}) collective-permute-start(bf16[64,768]{1,0:T(8,128)(2,1)S(1)} %add_convert_fusion.9), channel_id=1, source_target_pairs={{0,1},{1,0},{2,3},{3,2},{4,5},{5,4},{6,7},{7,6},{8,9},{9,8},{10,11... | collective-permute-start | bytes 294920 | tf_op jit(solution)/shard_map/ppermute | solution.py:85
  331.2 13.0 %collective-permute-start.5 = (bf16[4,64,768]{2,1,0:T(8,128)(2,1)S(1)}, bf16[4,64,768]{2,1,0:T(8,128)(2,1)S(1)}, u32[]{:S(2)}, u32[]{:S(2)}) collective-permute-start(bf16[4,64,768]{2,1,0:T(8,128)(2,1)S(1)} %get-tuple-element.413), channel_id=1, source_target_pairs={{0,24},{4,28},{8,16},{12,20},{16,8},{20,12},{24,0},{28,4},{1,25},{... | collective-permute-start | bytes 1179656 | tf_op jit(solution)/shard_map/ppermute | solution.py:85
  332.7 18.4 %collective-permute-start.4 = (bf16[4,64,768]{2,1,0:T(8,128)(2,1)S(1)}, bf16[4,64,768]{2,1,0:T(8,128)(2,1)S(1)}, u32[]{:S(2)}, u32[]{:S(2)}) collective-permute-start(bf16[4,64,768]{2,1,0:T(8,128)(2,1)S(1)} %get-tuple-element.413), channel_id=1, source_target_pairs={{0,16},{4,20},{8,24},{12,28},{16,0},{20,4},{24,8},{28,12},{1,17},{... | collective-permute-start | bytes 1179656 | tf_op jit(solution)/shard_map/ppermute | solution.py:85
  334.1 17.1 %collective-permute-start.3 = (bf16[4,64,768]{2,1,0:T(8,128)(2,1)S(1)}, bf16[4,64,768]{2,1,0:T(8,128)(2,1)S(1)}, u32[]{:S(2)}, u32[]{:S(2)}) collective-permute-start(bf16[4,64,768]{2,1,0:T(8,128)(2,1)S(1)} %get-tuple-element.413), channel_id=1, source_target_pairs={{0,8},{4,12},{8,0},{12,4},{16,24},{20,28},{24,16},{28,20},{1,9},{5... | collective-permute-start | bytes 1179656 | tf_op jit(solution)/shard_map/ppermute | solution.py:85
  351.4 3.5 collective-permute-start.6
  374.6 17.9 %all-to-all-start.6 = ((f32[32,32,128]{2,1,0:T(8,128)}), f32[32,32,128]{2,1,0:T(8,128)S(1)}, u32[]{:S(2)}, u32[]{:S(2)}) async-start(f32[32,32,128]{2,1,0:T(8,128)} %broadcast_in_dim.146), calls=%async_computation.6 | async-start | bytes 1048576 | tf_op jit(solution)/shard_map/all_to_all | solution.py:90
  409.2 4.7 collective-permute-start.7
  416.0 15.2 %collective-permute-start.10 = (bf16[4,64,768]{2,1,0:T(8,128)(2,1)S(1)}, bf16[4,64,768]{2,1,0:T(8,128)(2,1)S(1)}, u32[]{:S(2)}, u32[]{:S(2)}) collective-permute-start(bf16[4,64,768]{2,1,0:T(8,128)(2,1)S(1)} %get-tuple-element.343), channel_id=1, source_target_pairs={{0,24},{4,28},{8,16},{12,20},{16,8},{20,12},{24,0},{28,4},{1,25},{... | collective-permute-start | bytes 1179656 | tf_op jit(solution)/shard_map/ppermute | solution.py:85
  417.5 19.3 %collective-permute-start.9 = (bf16[4,64,768]{2,1,0:T(8,128)(2,1)S(1)}, bf16[4,64,768]{2,1,0:T(8,128)(2,1)S(1)}, u32[]{:S(2)}, u32[]{:S(2)}) collective-permute-start(bf16[4,64,768]{2,1,0:T(8,128)(2,1)S(1)} %get-tuple-element.344), channel_id=1, source_target_pairs={{0,16},{4,20},{8,24},{12,28},{16,0},{20,4},{24,8},{28,12},{1,17},{... | collective-permute-start | bytes 1179656 | tf_op jit(solution)/shard_map/ppermute | solution.py:85
  419.0 17.9 %collective-permute-start.8 = (bf16[4,64,768]{2,1,0:T(8,128)(2,1)S(1)}, bf16[4,64,768]{2,1,0:T(8,128)(2,1)S(1)}, u32[]{:S(2)}, u32[]{:S(2)}) collective-permute-start(bf16[4,64,768]{2,1,0:T(8,128)(2,1)S(1)} %get-tuple-element.342), channel_id=1, source_target_pairs={{0,8},{4,12},{8,0},{12,4},{16,24},{20,28},{24,16},{28,20},{1,9},{5... | collective-permute-start | bytes 1179656 | tf_op jit(solution)/shard_map/ppermute | solution.py:85
  437.1 7.6 collective-permute-start.13
  438.9 9.6 %collective-permute-start.12 = (bf16[64,768]{1,0:T(8,128)(2,1)S(1)}, bf16[64,768]{1,0:T(8,128)(2,1)S(1)}, u32[]{:S(2)}, u32[]{:S(2)}) collective-permute-start(bf16[64,768]{1,0:T(8,128)(2,1)S(1)} %get-tuple-element.411), channel_id=1, source_target_pairs={{0,2},{1,3},{2,0},{3,1},{4,6},{5,7},{6,4},{7,5},{8,10},{9,11},{10,... | collective-permute-start | bytes 294920 | tf_op jit(solution)/shard_map/ppermute | solution.py:85
  439.6 8.9 collective-permute-start.11
  579.1 38.4 %collective-permute-start.14 = (bf16[4,4,112,768]{3,2,1,0:T(8,128)(2,1)}, bf16[4,4,112,768]{3,2,1,0:T(8,128)(2,1)}, u32[]{:S(2)}, u32[]{:S(2)}) collective-permute-start(bf16[4,4,112,768]{3,2,1,0:T(8,128)(2,1)} %get-tuple-element.388), channel_id=1, source_target_pairs={{0,4},{4,0},{8,12},{12,8},{16,20},{20,16},{24,28},{28,24},{1,5},{5... | collective-permute-start | bytes 8257544 | tf_op jit(solution)/shard_map/ppermute | solution.py:85
  586.0 26.2 %collective-permute-start.21 = (bf16[4,4,96,768]{3,2,1,0:T(8,128)(2,1)}, bf16[4,4,96,768]{3,2,1,0:T(8,128)(2,1)}, u32[]{:S(2)}, u32[]{:S(2)}) collective-permute-start(bf16[4,4,96,768]{3,2,1,0:T(8,128)(2,1)} %pad_maximum_fusion.3), channel_id=1, source_target_pairs={{0,4},{4,0},{8,12},{12,8},{16,20},{20,16},{24,28},{28,24},{1,5},{5... | collective-permute-start | bytes 7077896 | tf_op jit(solution)/shard_map/ppermute | solution.py:85
  592.4 115.6 %collective-permute-start.35 = (bf16[4,4,192,768]{3,2,1,0:T(8,128)(2,1)}, bf16[4,4,192,768]{3,2,1,0:T(8,128)(2,1)}, u32[]{:S(2)}, u32[]{:S(2)}) collective-permute-start(bf16[4,4,192,768]{3,2,1,0:T(8,128)(2,1)} %get-tuple-element.362), channel_id=1, source_target_pairs={{0,4},{4,0},{8,12},{12,8},{16,20},{20,16},{24,28},{28,24},{1,5},{5... | collective-permute-start | bytes 14155784 | tf_op jit(solution)/shard_map/ppermute | solution.py:85
  598.3 58.8 %all-to-all-start.7 = ((bf16[32,32,768]{2,1,0:T(8,128)(2,1)}), bf16[32,32,768]{2,1,0:T(8,128)(2,1)}, u32[]{:S(2)}, u32[]{:S(2)}) async-start(bf16[32,32,768]{2,1,0:T(8,128)(2,1)} %bitcast.564), calls=%async_computation.7 | async-start | bytes 3145728 | tf_op jit(solution)/shard_map/all_to_all | solution.py:662
  612.0 112.1 %collective-permute-start.28 = (bf16[4,4,192,768]{3,2,1,0:T(8,128)(2,1)}, bf16[4,4,192,768]{3,2,1,0:T(8,128)(2,1)}, u32[]{:S(2)}, u32[]{:S(2)}) collective-permute-start(bf16[4,4,192,768]{3,2,1,0:T(8,128)(2,1)} %get-tuple-element.351), channel_id=1, source_target_pairs={{0,4},{4,0},{8,12},{12,8},{16,20},{20,16},{24,28},{28,24},{1,5},{5... | collective-permute-start | bytes 14155784 | tf_op jit(solution)/shard_map/ppermute | solution.py:85
  614.3 24.2 %collective-permute-start.24 = (bf16[4,96,768]{2,1,0:T(8,128)(2,1)S(1)}, bf16[4,96,768]{2,1,0:T(8,128)(2,1)S(1)}, u32[]{:S(2)}, u32[]{:S(2)}) collective-permute-start(bf16[4,96,768]{2,1,0:T(8,128)(2,1)S(1)} %get-tuple-element.339), channel_id=1, source_target_pairs={{0,24},{4,28},{8,16},{12,20},{16,8},{20,12},{24,0},{28,4},{1,25},{... | collective-permute-start | bytes 1769480 | tf_op jit(solution)/shard_map/ppermute | solution.py:85
  617.0 32.0 %collective-permute-start.23 = (bf16[4,96,768]{2,1,0:T(8,128)(2,1)S(1)}, bf16[4,96,768]{2,1,0:T(8,128)(2,1)S(1)}, u32[]{:S(2)}, u32[]{:S(2)}) collective-permute-start(bf16[4,96,768]{2,1,0:T(8,128)(2,1)S(1)} %get-tuple-element.340), channel_id=1, source_target_pairs={{0,16},{4,20},{8,24},{12,28},{16,0},{20,4},{24,8},{28,12},{1,17},{... | collective-permute-start | bytes 1769480 | tf_op jit(solution)/shard_map/ppermute | solution.py:85
  617.5 33.7 %collective-permute-start.22 = (bf16[4,96,768]{2,1,0:T(8,128)(2,1)S(1)}, bf16[4,96,768]{2,1,0:T(8,128)(2,1)S(1)}, u32[]{:S(2)}, u32[]{:S(2)}) collective-permute-start(bf16[4,96,768]{2,1,0:T(8,128)(2,1)S(1)} %get-tuple-element.338), channel_id=1, source_target_pairs={{0,8},{4,12},{8,0},{12,4},{16,24},{20,28},{24,16},{28,20},{1,9},{5... | collective-permute-start | bytes 1769480 | tf_op jit(solution)/shard_map/ppermute | solution.py:85
  652.4 17.4 %collective-permute-start.27 = (bf16[96,768]{1,0:T(8,128)(2,1)}, bf16[96,768]{1,0:T(8,128)(2,1)S(1)}, u32[]{:S(2)}, u32[]{:S(2)}) collective-permute-start(bf16[96,768]{1,0:T(8,128)(2,1)} %get-tuple-element.405), channel_id=1, source_target_pairs={{0,3},{1,2},{2,1},{3,0},{4,7},{5,6},{6,5},{7,4},{8,11},{9,10},{10,... | collective-permute-start | bytes 442376 | tf_op jit(solution)/shard_map/ppermute | solution.py:85
  654.3 17.5 %collective-permute-start.26 = (bf16[96,768]{1,0:T(8,128)(2,1)}, bf16[96,768]{1,0:T(8,128)(2,1)S(1)}, u32[]{:S(2)}, u32[]{:S(2)}) collective-permute-start(bf16[96,768]{1,0:T(8,128)(2,1)} %get-tuple-element.406), channel_id=1, source_target_pairs={{0,2},{1,3},{2,0},{3,1},{4,6},{5,7},{6,4},{7,5},{8,10},{9,11},{10,... | collective-permute-start | bytes 442376 | tf_op jit(solution)/shard_map/ppermute | solution.py:85
  656.5 16.4 %collective-permute-start.25 = (bf16[96,768]{1,0:T(8,128)(2,1)}, bf16[96,768]{1,0:T(8,128)(2,1)S(1)}, u32[]{:S(2)}, u32[]{:S(2)}) collective-permute-start(bf16[96,768]{1,0:T(8,128)(2,1)} %get-tuple-element.404), channel_id=1, source_target_pairs={{0,1},{1,0},{2,3},{3,2},{4,5},{5,4},{6,7},{7,6},{8,9},{9,8},{10,11... | collective-permute-start | bytes 442376 | tf_op jit(solution)/shard_map/ppermute | solution.py:85
  669.8 19.3 %collective-permute-start.17 = (bf16[4,112,768]{2,1,0:T(8,128)(2,1)S(1)}, bf16[4,112,768]{2,1,0:T(8,128)(2,1)S(1)}, u32[]{:S(2)}, u32[]{:S(2)}) collective-permute-start(bf16[4,112,768]{2,1,0:T(8,128)(2,1)S(1)} %copy-done.44), channel_id=1, source_target_pairs={{0,24},{4,28},{8,16},{12,20},{16,8},{20,12},{24,0},{28,4},{1,25},{... | collective-permute-start | bytes 2064392 | tf_op jit(solution)/shard_map/ppermute | solution.py:85
  671.8 30.2 %collective-permute-start.16 = (bf16[4,112,768]{2,1,0:T(8,128)(2,1)S(1)}, bf16[4,112,768]{2,1,0:T(8,128)(2,1)S(1)}, u32[]{:S(2)}, u32[]{:S(2)}) collective-permute-start(bf16[4,112,768]{2,1,0:T(8,128)(2,1)S(1)} %copy-done.43), channel_id=1, source_target_pairs={{0,16},{4,20},{8,24},{12,28},{16,0},{20,4},{24,8},{28,12},{1,17},{... | collective-permute-start | bytes 2064392 | tf_op jit(solution)/shard_map/ppermute | solution.py:85
  672.9 29.1 %collective-permute-start.15 = (bf16[4,112,768]{2,1,0:T(8,128)(2,1)S(1)}, bf16[4,112,768]{2,1,0:T(8,128)(2,1)S(1)}, u32[]{:S(2)}, u32[]{:S(2)}) collective-permute-start(bf16[4,112,768]{2,1,0:T(8,128)(2,1)S(1)} %copy-done.42), channel_id=1, source_target_pairs={{0,8},{4,12},{8,0},{12,4},{16,24},{20,28},{24,16},{28,20},{1,9},{5... | collective-permute-start | bytes 2064392 | tf_op jit(solution)/shard_map/ppermute | solution.py:85
  703.5 14.5 %collective-permute-start.20 = (bf16[112,768]{1,0:T(8,128)(2,1)S(1)}, bf16[112,768]{1,0:T(8,128)(2,1)S(1)}, u32[]{:S(2)}, u32[]{:S(2)}) collective-permute-start(bf16[112,768]{1,0:T(8,128)(2,1)S(1)} %get-tuple-element.390), channel_id=1, source_target_pairs={{0,3},{1,2},{2,1},{3,0},{4,7},{5,6},{6,5},{7,4},{8,11},{9,10},{10,... | collective-permute-start | bytes 516104 | tf_op jit(solution)/shard_map/ppermute | solution.py:85
  705.9 15.9 %collective-permute-start.19 = (bf16[112,768]{1,0:T(8,128)(2,1)S(1)}, bf16[112,768]{1,0:T(8,128)(2,1)S(1)}, u32[]{:S(2)}, u32[]{:S(2)}) collective-permute-start(bf16[112,768]{1,0:T(8,128)(2,1)S(1)} %get-tuple-element.391), channel_id=1, source_target_pairs={{0,2},{1,3},{2,0},{3,1},{4,6},{5,7},{6,4},{7,5},{8,10},{9,11},{10,... | collective-permute-start | bytes 516104 | tf_op jit(solution)/shard_map/ppermute | solution.py:85
  706.5 15.3 %collective-permute-start.18 = (bf16[112,768]{1,0:T(8,128)(2,1)S(1)}, bf16[112,768]{1,0:T(8,128)(2,1)S(1)}, u32[]{:S(2)}, u32[]{:S(2)}) collective-permute-start(bf16[112,768]{1,0:T(8,128)(2,1)S(1)} %get-tuple-element.389), channel_id=1, source_target_pairs={{0,1},{1,0},{2,3},{3,2},{4,5},{5,4},{6,7},{7,6},{8,9},{9,8},{10,11... | collective-permute-start | bytes 516104 | tf_op jit(solution)/shard_map/ppermute | solution.py:85
  716.2 29.8 %collective-permute-start.38 = (bf16[4,192,768]{2,1,0:T(8,128)(2,1)S(1)}, bf16[4,192,768]{2,1,0:T(8,128)(2,1)S(1)}, u32[]{:S(2)}, u32[]{:S(2)}) collective-permute-start(bf16[4,192,768]{2,1,0:T(8,128)(2,1)S(1)} %get-tuple-element.319), channel_id=1, source_target_pairs={{0,24},{4,28},{8,16},{12,20},{16,8},{20,12},{24,0},{28,4},{1,25},{... | collective-permute-start | bytes 3538952 | tf_op jit(solution)/shard_map/ppermute | solution.py:85
  722.0 49.4 %collective-permute-start.37 = (bf16[4,192,768]{2,1,0:T(8,128)(2,1)}, bf16[4,192,768]{2,1,0:T(8,128)(2,1)S(1)}, u32[]{:S(2)}, u32[]{:S(2)}) collective-permute-start(bf16[4,192,768]{2,1,0:T(8,128)(2,1)} %get-tuple-element.320), channel_id=1, source_target_pairs={{0,16},{4,20},{8,24},{12,28},{16,0},{20,4},{24,8},{28,12},{1,17},{... | collective-permute-start | bytes 3538952 | tf_op jit(solution)/shard_map/ppermute | solution.py:85
  723.1 49.2 %collective-permute-start.36 = (bf16[4,192,768]{2,1,0:T(8,128)(2,1)}, bf16[4,192,768]{2,1,0:T(8,128)(2,1)}, u32[]{:S(2)}, u32[]{:S(2)}) collective-permute-start(bf16[4,192,768]{2,1,0:T(8,128)(2,1)} %get-tuple-element.318), channel_id=1, source_target_pairs={{0,8},{4,12},{8,0},{12,4},{16,24},{20,28},{24,16},{28,20},{1,9},{5... | collective-permute-start | bytes 3538952 | tf_op jit(solution)/shard_map/ppermute | solution.py:85
  731.2 65.5 %collective-permute-start.31 = (bf16[4,192,768]{2,1,0:T(8,128)(2,1)}, bf16[4,192,768]{2,1,0:T(8,128)(2,1)}, u32[]{:S(2)}, u32[]{:S(2)}) collective-permute-start(bf16[4,192,768]{2,1,0:T(8,128)(2,1)} %get-tuple-element.310), channel_id=1, source_target_pairs={{0,24},{4,28},{8,16},{12,20},{16,8},{20,12},{24,0},{28,4},{1,25},{... | collective-permute-start | bytes 3538952 | tf_op jit(solution)/shard_map/ppermute | solution.py:85
  732.6 87.4 %collective-permute-start.30 = (bf16[4,192,768]{2,1,0:T(8,128)(2,1)}, bf16[4,192,768]{2,1,0:T(8,128)(2,1)}, u32[]{:S(2)}, u32[]{:S(2)}) collective-permute-start(bf16[4,192,768]{2,1,0:T(8,128)(2,1)} %get-tuple-element.311), channel_id=1, source_target_pairs={{0,16},{4,20},{8,24},{12,28},{16,0},{20,4},{24,8},{28,12},{1,17},{... | collective-permute-start | bytes 3538952 | tf_op jit(solution)/shard_map/ppermute | solution.py:85
  746.0 74.1 %collective-permute-start.29 = (bf16[4,192,768]{2,1,0:T(8,128)(2,1)}, bf16[4,192,768]{2,1,0:T(8,128)(2,1)}, u32[]{:S(2)}, u32[]{:S(2)}) collective-permute-start(bf16[4,192,768]{2,1,0:T(8,128)(2,1)} %get-tuple-element.309), channel_id=1, source_target_pairs={{0,8},{4,12},{8,0},{12,4},{16,24},{20,28},{24,16},{28,20},{1,9},{5... | collective-permute-start | bytes 3538952 | tf_op jit(solution)/shard_map/ppermute | solution.py:85
  775.0 50.6 %collective-permute-start.41 = (bf16[192,768]{1,0:T(8,128)(2,1)S(1)}, bf16[192,768]{1,0:T(8,128)(2,1)S(1)}, u32[]{:S(2)}, u32[]{:S(2)}) collective-permute-start(bf16[192,768]{1,0:T(8,128)(2,1)S(1)} %get-tuple-element.359), channel_id=1, source_target_pairs={{0,3},{1,2},{2,1},{3,0},{4,7},{5,6},{6,5},{7,4},{8,11},{9,10},{10,... | collective-permute-start | bytes 884744 | tf_op jit(solution)/shard_map/ppermute | solution.py:85
  777.4 50.1 %collective-permute-start.40 = (bf16[192,768]{1,0:T(8,128)(2,1)S(1)}, bf16[192,768]{1,0:T(8,128)(2,1)S(1)}, u32[]{:S(2)}, u32[]{:S(2)}) collective-permute-start(bf16[192,768]{1,0:T(8,128)(2,1)S(1)} %get-tuple-element.360), channel_id=1, source_target_pairs={{0,2},{1,3},{2,0},{3,1},{4,6},{5,7},{6,4},{7,5},{8,10},{9,11},{10,... | collective-permute-start | bytes 884744 | tf_op jit(solution)/shard_map/ppermute | solution.py:85
  796.7 30.9 %collective-permute-start.39 = (bf16[192,768]{1,0:T(8,128)(2,1)S(1)}, bf16[192,768]{1,0:T(8,128)(2,1)S(1)}, u32[]{:S(2)}, u32[]{:S(2)}) collective-permute-start(bf16[192,768]{1,0:T(8,128)(2,1)S(1)} %get-tuple-element.358), channel_id=1, source_target_pairs={{0,1},{1,0},{2,3},{3,2},{4,5},{5,4},{6,7},{7,6},{8,9},{9,8},{10,11... | collective-permute-start | bytes 884744 | tf_op jit(solution)/shard_map/ppermute | solution.py:85
  823.1 11.9 %collective-permute-start.34 = (bf16[192,768]{1,0:T(8,128)(2,1)S(1)}, bf16[192,768]{1,0:T(8,128)(2,1)S(1)}, u32[]{:S(2)}, u32[]{:S(2)}) collective-permute-start(bf16[192,768]{1,0:T(8,128)(2,1)S(1)} %get-tuple-element.348), channel_id=1, source_target_pairs={{0,3},{1,2},{2,1},{3,0},{4,7},{5,6},{6,5},{7,4},{8,11},{9,10},{10,... | collective-permute-start | bytes 884744 | tf_op jit(solution)/shard_map/ppermute | solution.py:85
  825.5 25.6 %collective-permute-start.33 = (bf16[192,768]{1,0:T(8,128)(2,1)S(1)}, bf16[192,768]{1,0:T(8,128)(2,1)S(1)}, u32[]{:S(2)}, u32[]{:S(2)}) collective-permute-start(bf16[192,768]{1,0:T(8,128)(2,1)S(1)} %get-tuple-element.349), channel_id=1, source_target_pairs={{0,2},{1,3},{2,0},{3,1},{4,6},{5,7},{6,4},{7,5},{8,10},{9,11},{10,... | collective-permute-start | bytes 884744 | tf_op jit(solution)/shard_map/ppermute | solution.py:85
  825.5 25.6 %collective-permute-start.32 = (bf16[192,768]{1,0:T(8,128)(2,1)S(1)}, bf16[192,768]{1,0:T(8,128)(2,1)S(1)}, u32[]{:S(2)}, u32[]{:S(2)}) collective-permute-start(bf16[192,768]{1,0:T(8,128)(2,1)S(1)} %get-tuple-element.347), channel_id=1, source_target_pairs={{0,1},{1,0},{2,3},{3,2},{4,5},{5,4},{6,7},{7,6},{8,9},{9,8},{10,11... | collective-permute-start | bytes 884744 | tf_op jit(solution)/shard_map/ppermute | solution.py:85
  (115 other events, 1002.7 us)
Sparse Core Ops, SparseCore 0:
  14.0 128.0 all-gather.4
  145.6 103.5 all-gather.2

commit v3 on v2

--- a/solution.py
+++ b/solution.py
@@ -308,7 +308,7 @@
 
 def adam_blocks(weight, moments, grad, count, factor, decay):
     rows, width = weight.shape
-    step = rows if rows <= 320 else max(size for size in range(16, 321, 16) if rows % size == 0)
+    step = rows if rows <= 320 else max(size for size in range(16, 161, 16) if rows % size == 0)
     flat = pl.BlockSpec((step, width), lambda at: (at, 0))
     pair = pl.BlockSpec((2, step, width), lambda at: (0, at, 0))
     return pl.pallas_call(
@@ -549,7 +549,9 @@
     peak = jnp.max(logits, axis=1)
     raised = jnp.exp(logits - peak[:, None])
     totals = jnp.sum(raised, axis=1)
-    soft_rows = jnp.dot(raised.astype(low), table_b, preferred_element_type=jnp.float32)
+    soft_rows = lax.optimization_barrier(
+        jnp.dot(raised.astype(low), table_b, preferred_element_type=jnp.float32)
+    )
     chosen = jnp.sum(jnp.where(hit, logits, 0.0), axis=1)
     stats = jnp.stack([peak.reshape(devices, -1), totals.reshape(devices, -1)], axis=1)
     inverse = jnp.argsort(order)
@@ -660,14 +662,14 @@
         return outer_sum(seat_matrix(turn), grad_embedded).astype(low).reshape(devices, slots_each, width)
 
     came = lax.all_to_all(returned(0), BOTH, 0, 0, tiled=True)
-    table_grad = table_grad + outer_sum(wanted_of(heard_first), came.reshape(slots_all, width))
 
     def later_turn(carry):
         turn, total = carry
         rows = lax.all_to_all(returned(turn), BOTH, 0, 0, tiled=True).reshape(slots_all, width)
         return (turn + 1, total + outer_sum(wanted_of(requests(turn)), rows))
 
-    _, table_sum = lax.while_loop(lambda carry: carry[0] < turns, later_turn, (jnp.int32(1), table_grad))
+    _, table_grad = lax.while_loop(lambda carry: carry[0] < turns, later_turn, (jnp.int32(1), table_grad))
+    table_sum = table_grad + outer_sum(wanted_of(heard_first), came.reshape(slots_all, width))
     for layer in range(1, layers):
         narrow_sent[layer] = send_deep(narrow_sent[layer])
     wide_sent[0] = send_deep(wide_sent[0])

time: 922 us -> 946 us (1.026)
  local copies, waits for them, and re-layouts: 73.6 us -> 98.9 us
  waiting for transfers between devices: 384 us -> 368 us
    unnamed x272 -> x254, local copies, waits for them, and re-layouts: 37.5 us -> 58.3 us
    all_to_all x1, waiting for transfers between devices: 13.4 us -> 1.72 us  [spread(): lax.all_to_all(jnp.broadcast_to(value[None], (count,) + value.shape), BOT...]
  transfers between devices with their start and end apart: 48 -> 48, of which waited for: 26 -> 28; matrix products, arithmetic and copies ran while one was open for 14% -> 14% of each run, Pallas kernels for 0% -> 0%
where the time goes in v3:
time: 946 us; the launch traced here: 935 us
  waiting for transfers between devices  368 us (39%)
  matrix products  190 us (20%)
  local copies, waits for them, and re-layouts  98.9 us (10%)
  other arithmetic  87.3 us (9%)
  Pallas kernels  77.7 us (8%)
  starting transfers between devices  71.5 us (8%)
  between operations  30.3 us (3%)
  blocking collectives  11.1 us (1%)
    ppermute x42, waiting for transfers between devices, swapped(): lax.ppermute(value, axis, [(index, index ^ flip) for index in range(size)])  193 us
    all_gather x2, waiting for transfers between devices, shards(): lax.all_gather(mixed_share[layer], BOTH, axis=0, tiled=True)  128 us
    dot_general x9, matrix products, times_transpose(): lax.dot_general(left, right, (((1,), (1,)), ((), ())), preferred_element_...  62.9 us
    dot_general x12, matrix products, outer_sum(): lax.dot_general(left, right, (((0,), (0,)), ((), ())), preferred_element_...  60.1 us
    unnamed x254, local copies, waits for them, and re-layouts  58.3 us
    ppermute x42, starting transfers between devices, swapped(): lax.ppermute(value, axis, [(index, index ^ flip) for index in range(size)])  51.2 us
    all_to_all x1, waiting for transfers between devices, looked_up(): rows = lax.all_to_all(rows, BOTH, 0, 0, tiled=True)  45 us
    pallas_call x6, Pallas kernels, adam_blocks(): pl.pallas_call(functools.partial(adam_kernel, decay), grid=(rows // step,...  29.7 us
  transfers between devices with their start and end apart: 48, of which 28 were waited for; matrix products, arithmetic and copies ran while one was open for 14% of the time, Pallas kernels for 0%

profile of v3, /device:TPU:0, one launch (start us, length us, event | category | flops | bytes accessed | tf_op | source)
XLA Modules:
  0.0 935.4 jit_solution(2888815943695350419)
XLA Ops:
  25.1 7.3 all-to-all-start.4
  40.8 6.1 fusion.69
  46.8 5.9 all-to-all-start.5
  60.5 9.8 %fusion.52 = bf16[2048,768]{1,0:T(8,128)(2,1)} fusion(bf16[1600,768]{1,0:T(8,128)(2,1)} %convert_element_type.486, s32[2048]{0:T(1024)S(1)} %sub.258), kind=kOutput, calls=%fused_computation.92 | convolution fusion | flops 5038014464 | bytes 5611520 | tf_op jit(solution)/shard_map/dot_general | solution.py:477
  70.4 45.0 %all-to-all-done.5 = bf16[32,32,768]{2,1,0:T(8,128)(2,1)S(1)} async-done(((bf16[32,32,768]{2,1,0:T(8,128)(2,1)}), bf16[32,32,768]{2,1,0:T(8,128)(2,1)S(1)}, u32[]{:S(2)}, u32[]{:S(2)}) %all-to-all-start.5) | async-done | bytes 1572896 | tf_op jit(solution)/shard_map/all_to_all | solution.py:410
  116.6 26.1 %all-gather.5.cloned.1.call-done = bf16[768,9216]{1,0:T(8,128)(2,1)} async-done(((bf16[24,9216]{1,0:T(8,128)(2,1)}), bf16[768,9216]{1,0:T(8,128)(2,1)}) %all-gather.5.cloned.1.call-update) | async-done | bytes 14155792 | tf_op jit(solution)/shard_map/all_gather | solution.py:437
  147.8 101.8 %all-gather.3.cloned.1.call-done = bf16[768,9600]{1,0:T(8,128)(2,1)} async-done(((bf16[24,9600]{1,0:T(8,128)(2,1)}), bf16[768,9600]{1,0:T(8,128)(2,1)}) %all-gather.3.cloned.1.call-update) | async-done | bytes 14745616 | tf_op jit(solution)/shard_map/all_gather | solution.py:437
  255.0 5.6 fusion.39.mixed_ref
  260.5 9.8 %attend_forward.2 = (bf16[512,768]{1,0:T(8,128)(2,1)}, f32[512,768]{1,0:T(8,128)}) custom-call(s32[2,1,256]{2,1,0:T(1,128)} %broadcast_in_dim.134.row_ref, s32[2,256,1]{2,1,0:T(8,128)} %copy.195.column_ref, bf16[512,2304]{1,0:T(8,128)(2,1)} %fusion.39.mixed_ref), custom_call_target="tpu_custom_call" | custom-call | flops 402653184 | bytes 6291456 | tf_op jit(solution)/shard_map/attend_forward/pallas_call | solution.py:259
  276.7 6.8 fusion.47
  288.0 5.8 fusion.40.mixed_ref
  293.8 9.8 %attend_forward.3 = (bf16[512,768]{1,0:T(8,128)(2,1)}, f32[512,768]{1,0:T(8,128)}) custom-call(s32[2,1,256]{2,1,0:T(1,128)} %broadcast_in_dim.134.row_ref, s32[2,256,1]{2,1,0:T(8,128)} %copy.195.column_ref, bf16[512,2304]{1,0:T(8,128)(2,1)} %fusion.40.mixed_ref), custom_call_target="tpu_custom_call" | custom-call | flops 402653184 | bytes 6291456 | tf_op jit(solution)/shard_map/attend_forward/pallas_call | solution.py:259
  306.4 5.6 fusion.43
  335.3 9.4 %collective-permute-done.5 = bf16[4,64,768]{2,1,0:T(8,128)(2,1)S(1)} collective-permute-done((bf16[4,64,768]{2,1,0:T(8,128)(2,1)S(1)}, bf16[4,64,768]{2,1,0:T(8,128)(2,1)S(1)}, u32[]{:S(2)}, u32[]{:S(2)}) %collective-permute-start.5) | collective-permute-done | bytes 393248 | tf_op jit(solution)/shard_map/ppermute | solution.py:85
  344.8 7.0 collective-permute-done.4
  355.8 11.2 %fusion.178 = (f32[2048]{0:T(1024)S(1)}, f32[2048,1600]{0,1:T(8,128)}) fusion(bf16[2048,768]{1,0:T(8,128)(2,1)S(1)} %bitcast.550, bf16[1600,768]{1,0:T(8,128)(2,1)} %convert_element_type.486), kind=kOutput, calls=%fused_computation.504 | convolution fusion | flops 5036439552 | bytes 18718720 | tf_op jit(solution)/shard_map/dot_general | solution.py:75
  367.2 6.8 select_reduce_fusion.2
  379.3 11.7 %fusion.17 = f32[2048,768]{1,0:T(8,128)} fusion(bf16[1600,768]{1,0:T(8,128)(2,1)} %convert_element_type.486, f32[2048,1600]{0,1:T(8,128)} %get-tuple-element.491, f32[2048]{0:T(1024)S(1)} %get-tuple-element.490), kind=kOutput, calls=%fused_computation.42 | convolution fusion | flops 5039718400 | bytes 21864448 | tf_op jit(solution)/shard_map/dot_general | solution.py:553
  398.2 4.3 subtract_convert_fusion
  414.2 11.7 %fusion.19 = f32[1600,768]{1,0:T(8,128)} fusion(bf16[2048,768]{1,0:T(8,128)(2,1)S(1)} %bitcast.551, f32[2048,1600]{0,1:T(8,128)} %get-tuple-element.491, f32[2048]{0:T(1024)S(1)} %convert_element_type.520, f32[2048]{0:T(1024)S(1)} %select_n.292, s32[2048]{0:T(1024)S(1)} %sub.258), kind=kOutput, calls=%fused_computation.43 | convolution fusion | flops 5052825600 | bytes 21192704 | tf_op jit(solution)/shard_map/dot_general | solution.py:69
  425.8 5.6 collective-permute-done.9
  444.4 10.3 %fusion.180 = (bf16[3072]{0:T(1024)(128)(2,1)}, bf16[512,3072]{1,0:T(8,128)(2,1)S(1)}) fusion(f32[512,3072]{1,0:T(8,128)} %copy-done.89, f32[3072]{0:T(1024)S(1)} %copy-done.59, bf16[3072,768]{1,0:T(8,128)(2,1)} %bitcast.530, f32[512,768]{1,0:T(8,128)S(1)} %fusion.103), kind=kOutput, calls=%fused_computation.506 | convolution fusion | flops 2449339392 | bytes 15747072 | tf_op jit(solution)/shard_map/dot_general | solution.py:75
  454.7 7.1 multiply_reduce_fusion.1
  466.0 14.1 %attend_backward.2 = bf16[512,2304]{1,0:T(8,128)(2,1)} custom-call(s32[2,1,256]{2,1,0:T(1,128)} %broadcast_in_dim.134.row_ref, s32[2,256,1]{2,1,0:T(8,128)} %copy.195.column_ref, bf16[512,2304]{1,0:T(8,128)(2,1)} %fusion.40.mixed_ref, f32[512,768]{1,0:T(8,128)} %get-tuple-element.202.log_ref, bf16[512,768]{1,0:T(8,128)(2,1)} %convolution_convert_fusion.9.grad_ref), custom_call_target="tpu_custom_call" | custom-call | flops 1006632960 | bytes 6291456 | tf_op jit(solution)/shard_map/attend_backward/pallas_call | solution.py:276
  480.1 6.2 multiply_reduce_fusion.2
  486.9 9.9 %fusion.179 = (bf16[3072]{0:T(1024)(128)(2,1)}, bf16[512,3072]{1,0:T(8,128)(2,1)S(1)}) fusion(f32[512,3072]{1,0:T(8,128)} %copy-done.88, f32[3072]{0:T(1024)S(1)} %copy-done.58, bf16[3072,768]{1,0:T(8,128)(2,1)} %bitcast.535, f32[512,768]{1,0:T(8,128)S(1)} %get-tuple-element.294), kind=kOutput, calls=%fused_computation.505 | convolution fusion | flops 2449339392 | bytes 15747072 | tf_op jit(solution)/shard_map/dot_general | solution.py:75
  496.8 7.1 multiply_reduce_fusion.3
  509.9 14.3 %attend_backward.3 = bf16[512,2304]{1,0:T(8,128)(2,1)} custom-call(s32[2,1,256]{2,1,0:T(1,128)} %broadcast_in_dim.134.row_ref, s32[2,256,1]{2,1,0:T(8,128)} %copy.195.column_ref, bf16[512,2304]{1,0:T(8,128)(2,1)} %fusion.39.mixed_ref, f32[512,768]{1,0:T(8,128)} %get-tuple-element.203.log_ref, bf16[512,768]{1,0:T(8,128)(2,1)} %convolution_convert_fusion.8.grad_ref), custom_call_target="tpu_custom_call" | custom-call | flops 1006632960 | bytes 6291456 | tf_op jit(solution)/shard_map/attend_backward/pallas_call | solution.py:276
  528.3 5.1 multiply_reduce_fusion.4
  545.8 9.3 convolution_convert_fusion.1
  555.1 4.9 convolution_convert_fusion
  560.0 5.6 convolution_convert_fusion.3
  565.7 4.9 convolution_convert_fusion.2
  630.1 4.2 bitcast_dynamic-update-slice_fusion.3
  649.5 16.6 %collective-permute-done.24 = bf16[4,96,768]{2,1,0:T(8,128)(2,1)S(1)} collective-permute-done((bf16[4,96,768]{2,1,0:T(8,128)(2,1)S(1)}, bf16[4,96,768]{2,1,0:T(8,128)(2,1)S(1)}, u32[]{:S(2)}, u32[]{:S(2)}) %collective-permute-start.24) | collective-permute-done | bytes 589856 | tf_op jit(solution)/shard_map/ppermute | solution.py:85
  666.1 10.3 %collective-permute-done.23 = bf16[4,96,768]{2,1,0:T(8,128)(2,1)S(1)} collective-permute-done((bf16[4,96,768]{2,1,0:T(8,128)(2,1)S(1)}, bf16[4,96,768]{2,1,0:T(8,128)(2,1)S(1)}, u32[]{:S(2)}, u32[]{:S(2)}) %collective-permute-start.23) | collective-permute-done | bytes 589856 | tf_op jit(solution)/shard_map/ppermute | solution.py:85
  683.6 9.5 %multiply_reduce_fusion = (f32[]{:T(128)}, f32[1600,768]{1,0:T(8,128)}) fusion(f32[1600,768]{1,0:T(8,128)} %get-tuple-element.204, bf16[1024,768]{1,0:T(8,128)(2,1)} %bitcast.72, s32[1024]{0:T(1024)S(1)} %copy-done.67), kind=kOutput, calls=%fused_computation.73 | convolution fusion | flops 2521907200 | bytes 11407364 | tf_op jit(solution)/shard_map/dot_general | solution.py:69
  699.5 12.9 %collective-permute-done.17 = bf16[4,112,768]{2,1,0:T(8,128)(2,1)S(1)} collective-permute-done((bf16[4,112,768]{2,1,0:T(8,128)(2,1)S(1)}, bf16[4,112,768]{2,1,0:T(8,128)(2,1)S(1)}, u32[]{:S(2)}, u32[]{:S(2)}) %collective-permute-start.17) | collective-permute-done | bytes 688160 | tf_op jit(solution)/shard_map/ppermute | solution.py:85
  712.4 12.7 %collective-permute-done.16 = bf16[4,112,768]{2,1,0:T(8,128)(2,1)S(1)} collective-permute-done((bf16[4,112,768]{2,1,0:T(8,128)(2,1)S(1)}, bf16[4,112,768]{2,1,0:T(8,128)(2,1)S(1)}, u32[]{:S(2)}, u32[]{:S(2)}) %collective-permute-start.16) | collective-permute-done | bytes 688160 | tf_op jit(solution)/shard_map/ppermute | solution.py:85
  729.9 5.3 add_convert_fusion
  756.1 11.9 %collective-permute-done.38 = bf16[4,192,768]{2,1,0:T(8,128)(2,1)S(1)} collective-permute-done((bf16[4,192,768]{2,1,0:T(8,128)(2,1)S(1)}, bf16[4,192,768]{2,1,0:T(8,128)(2,1)S(1)}, u32[]{:S(2)}, u32[]{:S(2)}) %collective-permute-start.38) | collective-permute-done | bytes 1179680 | tf_op jit(solution)/shard_map/ppermute | solution.py:85
  777.0 16.4 %collective-permute-done.37 = bf16[4,192,768]{2,1,0:T(8,128)(2,1)} collective-permute-done((bf16[4,192,768]{2,1,0:T(8,128)(2,1)}, bf16[4,192,768]{2,1,0:T(8,128)(2,1)}, u32[]{:S(2)}, u32[]{:S(2)}) %collective-permute-start.37) | collective-permute-done | bytes 1179680 | tf_op jit(solution)/shard_map/ppermute | solution.py:85
  798.4 20.2 %collective-permute-done.31 = bf16[4,192,768]{2,1,0:T(8,128)(2,1)S(1)} collective-permute-done((bf16[4,192,768]{2,1,0:T(8,128)(2,1)}, bf16[4,192,768]{2,1,0:T(8,128)(2,1)S(1)}, u32[]{:S(2)}, u32[]{:S(2)}) %collective-permute-start.31) | collective-permute-done | bytes 1179680 | tf_op jit(solution)/shard_map/ppermute | solution.py:85
  819.4 22.7 %collective-permute-done.30 = bf16[4,192,768]{2,1,0:T(8,128)(2,1)} collective-permute-done((bf16[4,192,768]{2,1,0:T(8,128)(2,1)}, bf16[4,192,768]{2,1,0:T(8,128)(2,1)}, u32[]{:S(2)}, u32[]{:S(2)}) %collective-permute-start.30) | collective-permute-done | bytes 1179680 | tf_op jit(solution)/shard_map/ppermute | solution.py:85
  849.6 7.2 collective-permute-done.34
  856.8 16.3 %collective-permute-done.33 = bf16[192,768]{1,0:T(8,128)(2,1)S(1)} collective-permute-done((bf16[192,768]{1,0:T(8,128)(2,1)S(1)}, bf16[192,768]{1,0:T(8,128)(2,1)S(1)}, u32[]{:S(2)}, u32[]{:S(2)}) %collective-permute-start.33) | collective-permute-done | bytes 294944 | tf_op jit(solution)/shard_map/ppermute | solution.py:85
  878.5 11.1 %all_to_all.83 = f32[32,1,3]{2,1,0:T(1,128)S(1)} all-to-all(f32[32,1,3]{2,1,0:T(1,128)S(1)} %broadcast_in_dim.149), channel_id=1, replica_groups=mesh['dp'=8,'fsdp'=4] {'dp','fsdp'}, dimensions={0} | all-to-all | bytes 768 | tf_op jit(solution)/shard_map/all_to_all | solution.py:90
  895.0 16.7 %adam_blocks.6 = (f32[1600,768]{1,0:T(8,128)}, f32[2,1600,768]{2,1,0:T(8,128)}, bf16[1600,768]{1,0:T(8,128)(2,1)}) custom-call(f32[2]{0:T(128)} %pad_maximum_fusion.15.scale_ref, f32[1600,768]{1,0:T(8,128)} %weight_ref.2, f32[2,1600,768]{2,1,0:T(8,128)} %moments_ref.2, f32[1600,768]{1,0:T(8,128)} %get-tuple-element.497.grad_ref), custom_call_target="tpu_custom_call" | custom-call | flops 24576000 | bytes 36864000 | tf_op jit(solution)/shard_map/adam_blocks/pallas_call | solution.py:314
  (572 shorter events, 299.3 us)
Async XLA Ops:
  7.2 135.5 %all-gather.5.cloned.1.call-start = ((), (), s32[]{:S(2)}) async-start(), calls=%async_computation.10 | async-start | bytes 14598144 | tf_op jit(solution)/shard_map/all_gather | solution.py:437
  13.9 235.8 %all-gather.3.cloned.1.call-start = ((), (), s32[]{:S(2)}) async-start(), calls=%async_computation.9 | async-start | bytes 15206400 | tf_op jit(solution)/shard_map/all_gather | solution.py:437
  25.1 15.6 %all-to-all-start.4 = ((s32[32,1,161]{2,1,0:T(1,128)}), s32[32,1,161]{2,1,0:T(1,128)S(1)}, u32[]{:S(2)}, u32[]{:S(2)}) async-start(s32[32,1,161]{2,1,0:T(1,128)} %all_to_all.57), calls=%async_computation.4 | async-start | bytes 65536 | tf_op jit(solution)/shard_map/all_to_all | solution.py:397
  46.8 68.5 %all-to-all-start.5 = ((bf16[32,32,768]{2,1,0:T(8,128)(2,1)}), bf16[32,32,768]{2,1,0:T(8,128)(2,1)S(1)}, u32[]{:S(2)}, u32[]{:S(2)}) async-start(bf16[32,32,768]{2,1,0:T(8,128)(2,1)} %bitcast.9), calls=%async_computation.5 | async-start | bytes 3145728 | tf_op jit(solution)/shard_map/all_to_all | solution.py:410
  320.0 7.6 collective-permute-start.2
  321.8 9.9 %collective-permute-start.1 = (bf16[64,768]{1,0:T(8,128)(2,1)S(1)}, bf16[64,768]{1,0:T(8,128)(2,1)S(1)}, u32[]{:S(2)}, u32[]{:S(2)}) collective-permute-start(bf16[64,768]{1,0:T(8,128)(2,1)S(1)} %add_convert_fusion.9), channel_id=1, source_target_pairs={{0,2},{1,3},{2,0},{3,1},{4,6},{5,7},{6,4},{7,5},{8,10},{9,11},{10,... | collective-permute-start | bytes 294920 | tf_op jit(solution)/shard_map/ppermute | solution.py:85
  322.5 9.2 collective-permute-start
  331.8 13.0 %collective-permute-start.5 = (bf16[4,64,768]{2,1,0:T(8,128)(2,1)S(1)}, bf16[4,64,768]{2,1,0:T(8,128)(2,1)S(1)}, u32[]{:S(2)}, u32[]{:S(2)}) collective-permute-start(bf16[4,64,768]{2,1,0:T(8,128)(2,1)S(1)} %get-tuple-element.413), channel_id=1, source_target_pairs={{0,24},{4,28},{8,16},{12,20},{16,8},{20,12},{24,0},{28,4},{1,25},{... | collective-permute-start | bytes 1179656 | tf_op jit(solution)/shard_map/ppermute | solution.py:85
  333.3 18.4 %collective-permute-start.4 = (bf16[4,64,768]{2,1,0:T(8,128)(2,1)S(1)}, bf16[4,64,768]{2,1,0:T(8,128)(2,1)S(1)}, u32[]{:S(2)}, u32[]{:S(2)}) collective-permute-start(bf16[4,64,768]{2,1,0:T(8,128)(2,1)S(1)} %get-tuple-element.413), channel_id=1, source_target_pairs={{0,16},{4,20},{8,24},{12,28},{16,0},{20,4},{24,8},{28,12},{1,17},{... | collective-permute-start | bytes 1179656 | tf_op jit(solution)/shard_map/ppermute | solution.py:85
  334.7 17.1 %collective-permute-start.3 = (bf16[4,64,768]{2,1,0:T(8,128)(2,1)S(1)}, bf16[4,64,768]{2,1,0:T(8,128)(2,1)S(1)}, u32[]{:S(2)}, u32[]{:S(2)}) collective-permute-start(bf16[4,64,768]{2,1,0:T(8,128)(2,1)S(1)} %get-tuple-element.413), channel_id=1, source_target_pairs={{0,8},{4,12},{8,0},{12,4},{16,24},{20,28},{24,16},{28,20},{1,9},{5... | collective-permute-start | bytes 1179656 | tf_op jit(solution)/shard_map/ppermute | solution.py:85
  352.1 3.5 collective-permute-start.6
  375.8 17.7 %all-to-all-start.6 = ((f32[32,32,128]{2,1,0:T(8,128)}), f32[32,32,128]{2,1,0:T(8,128)S(1)}, u32[]{:S(2)}, u32[]{:S(2)}) async-start(f32[32,32,128]{2,1,0:T(8,128)} %broadcast_in_dim.146), calls=%async_computation.6 | async-start | bytes 1048576 | tf_op jit(solution)/shard_map/all_to_all | solution.py:90
  403.8 4.7 collective-permute-start.7
  410.6 15.2 %collective-permute-start.10 = (bf16[4,64,768]{2,1,0:T(8,128)(2,1)S(1)}, bf16[4,64,768]{2,1,0:T(8,128)(2,1)S(1)}, u32[]{:S(2)}, u32[]{:S(2)}) collective-permute-start(bf16[4,64,768]{2,1,0:T(8,128)(2,1)S(1)} %get-tuple-element.343), channel_id=1, source_target_pairs={{0,24},{4,28},{8,16},{12,20},{16,8},{20,12},{24,0},{28,4},{1,25},{... | collective-permute-start | bytes 1179656 | tf_op jit(solution)/shard_map/ppermute | solution.py:85
  412.1 19.3 %collective-permute-start.9 = (bf16[4,64,768]{2,1,0:T(8,128)(2,1)S(1)}, bf16[4,64,768]{2,1,0:T(8,128)(2,1)S(1)}, u32[]{:S(2)}, u32[]{:S(2)}) collective-permute-start(bf16[4,64,768]{2,1,0:T(8,128)(2,1)S(1)} %get-tuple-element.344), channel_id=1, source_target_pairs={{0,16},{4,20},{8,24},{12,28},{16,0},{20,4},{24,8},{28,12},{1,17},{... | collective-permute-start | bytes 1179656 | tf_op jit(solution)/shard_map/ppermute | solution.py:85
  413.6 17.9 %collective-permute-start.8 = (bf16[4,64,768]{2,1,0:T(8,128)(2,1)S(1)}, bf16[4,64,768]{2,1,0:T(8,128)(2,1)S(1)}, u32[]{:S(2)}, u32[]{:S(2)}) collective-permute-start(bf16[4,64,768]{2,1,0:T(8,128)(2,1)S(1)} %get-tuple-element.342), channel_id=1, source_target_pairs={{0,8},{4,12},{8,0},{12,4},{16,24},{20,28},{24,16},{28,20},{1,9},{5... | collective-permute-start | bytes 1179656 | tf_op jit(solution)/shard_map/ppermute | solution.py:85
  431.7 7.6 collective-permute-start.13
  433.5 9.6 %collective-permute-start.12 = (bf16[64,768]{1,0:T(8,128)(2,1)S(1)}, bf16[64,768]{1,0:T(8,128)(2,1)S(1)}, u32[]{:S(2)}, u32[]{:S(2)}) collective-permute-start(bf16[64,768]{1,0:T(8,128)(2,1)S(1)} %get-tuple-element.411), channel_id=1, source_target_pairs={{0,2},{1,3},{2,0},{3,1},{4,6},{5,7},{6,4},{7,5},{8,10},{9,11},{10,... | collective-permute-start | bytes 294920 | tf_op jit(solution)/shard_map/ppermute | solution.py:85
  434.2 8.9 collective-permute-start.11
  609.9 35.4 %collective-permute-start.14 = (bf16[4,4,112,768]{3,2,1,0:T(8,128)(2,1)}, bf16[4,4,112,768]{3,2,1,0:T(8,128)(2,1)}, u32[]{:S(2)}, u32[]{:S(2)}) collective-permute-start(bf16[4,4,112,768]{3,2,1,0:T(8,128)(2,1)} %get-tuple-element.388), channel_id=1, source_target_pairs={{0,4},{4,0},{8,12},{12,8},{16,20},{20,16},{24,28},{28,24},{1,5},{5... | collective-permute-start | bytes 8257544 | tf_op jit(solution)/shard_map/ppermute | solution.py:85
  616.6 22.2 %collective-permute-start.21 = (bf16[4,4,96,768]{3,2,1,0:T(8,128)(2,1)}, bf16[4,4,96,768]{3,2,1,0:T(8,128)(2,1)}, u32[]{:S(2)}, u32[]{:S(2)}) collective-permute-start(bf16[4,4,96,768]{3,2,1,0:T(8,128)(2,1)} %pad_maximum_fusion.3), channel_id=1, source_target_pairs={{0,4},{4,0},{8,12},{12,8},{16,20},{20,16},{24,28},{28,24},{1,5},{5... | collective-permute-start | bytes 7077896 | tf_op jit(solution)/shard_map/ppermute | solution.py:85
  624.1 59.5 %all-to-all-start.7 = ((bf16[32,32,768]{2,1,0:T(8,128)(2,1)}), bf16[32,32,768]{2,1,0:T(8,128)(2,1)}, u32[]{:S(2)}, u32[]{:S(2)}) async-start(bf16[32,32,768]{2,1,0:T(8,128)(2,1)} %bitcast.562), calls=%async_computation.7 | async-start | bytes 3145728 | tf_op jit(solution)/shard_map/all_to_all | solution.py:664
  630.0 99.9 %collective-permute-start.35 = (bf16[4,4,192,768]{3,2,1,0:T(8,128)(2,1)}, bf16[4,4,192,768]{3,2,1,0:T(8,128)(2,1)}, u32[]{:S(2)}, u32[]{:S(2)}) collective-permute-start(bf16[4,4,192,768]{3,2,1,0:T(8,128)(2,1)} %get-tuple-element.362), channel_id=1, source_target_pairs={{0,4},{4,0},{8,12},{12,8},{16,20},{20,16},{24,28},{28,24},{1,5},{5... | collective-permute-start | bytes 14155784 | tf_op jit(solution)/shard_map/ppermute | solution.py:85
  638.4 108.6 %collective-permute-start.28 = (bf16[4,4,192,768]{3,2,1,0:T(8,128)(2,1)}, bf16[4,4,192,768]{3,2,1,0:T(8,128)(2,1)}, u32[]{:S(2)}, u32[]{:S(2)}) collective-permute-start(bf16[4,4,192,768]{3,2,1,0:T(8,128)(2,1)} %get-tuple-element.351), channel_id=1, source_target_pairs={{0,4},{4,0},{8,12},{12,8},{16,20},{20,16},{24,28},{28,24},{1,5},{5... | collective-permute-start | bytes 14155784 | tf_op jit(solution)/shard_map/ppermute | solution.py:85
  642.2 24.0 %collective-permute-start.24 = (bf16[4,96,768]{2,1,0:T(8,128)(2,1)S(1)}, bf16[4,96,768]{2,1,0:T(8,128)(2,1)S(1)}, u32[]{:S(2)}, u32[]{:S(2)}) collective-permute-start(bf16[4,96,768]{2,1,0:T(8,128)(2,1)S(1)} %get-tuple-element.339), channel_id=1, source_target_pairs={{0,24},{4,28},{8,16},{12,20},{16,8},{20,12},{24,0},{28,4},{1,25},{... | collective-permute-start | bytes 1769480 | tf_op jit(solution)/shard_map/ppermute | solution.py:85
  644.8 31.7 %collective-permute-start.23 = (bf16[4,96,768]{2,1,0:T(8,128)(2,1)S(1)}, bf16[4,96,768]{2,1,0:T(8,128)(2,1)S(1)}, u32[]{:S(2)}, u32[]{:S(2)}) collective-permute-start(bf16[4,96,768]{2,1,0:T(8,128)(2,1)S(1)} %get-tuple-element.340), channel_id=1, source_target_pairs={{0,16},{4,20},{8,24},{12,28},{16,0},{20,4},{24,8},{28,12},{1,17},{... | collective-permute-start | bytes 1769480 | tf_op jit(solution)/shard_map/ppermute | solution.py:85
  645.3 32.8 %collective-permute-start.22 = (bf16[4,96,768]{2,1,0:T(8,128)(2,1)S(1)}, bf16[4,96,768]{2,1,0:T(8,128)(2,1)S(1)}, u32[]{:S(2)}, u32[]{:S(2)}) collective-permute-start(bf16[4,96,768]{2,1,0:T(8,128)(2,1)S(1)} %get-tuple-element.338), channel_id=1, source_target_pairs={{0,8},{4,12},{8,0},{12,4},{16,24},{20,28},{24,16},{28,20},{1,9},{5... | collective-permute-start | bytes 1769480 | tf_op jit(solution)/shard_map/ppermute | solution.py:85
  679.2 13.9 %collective-permute-start.27 = (bf16[96,768]{1,0:T(8,128)(2,1)}, bf16[96,768]{1,0:T(8,128)(2,1)S(1)}, u32[]{:S(2)}, u32[]{:S(2)}) collective-permute-start(bf16[96,768]{1,0:T(8,128)(2,1)} %get-tuple-element.405), channel_id=1, source_target_pairs={{0,3},{1,2},{2,1},{3,0},{4,7},{5,6},{6,5},{7,4},{8,11},{9,10},{10,... | collective-permute-start | bytes 442376 | tf_op jit(solution)/shard_map/ppermute | solution.py:85
  680.8 15.5 %collective-permute-start.26 = (bf16[96,768]{1,0:T(8,128)(2,1)}, bf16[96,768]{1,0:T(8,128)(2,1)}, u32[]{:S(2)}, u32[]{:S(2)}) collective-permute-start(bf16[96,768]{1,0:T(8,128)(2,1)} %get-tuple-element.406), channel_id=1, source_target_pairs={{0,2},{1,3},{2,0},{3,1},{4,6},{5,7},{6,4},{7,5},{8,10},{9,11},{10,... | collective-permute-start | bytes 442376 | tf_op jit(solution)/shard_map/ppermute | solution.py:85
  683.3 14.2 %collective-permute-start.25 = (bf16[96,768]{1,0:T(8,128)(2,1)}, bf16[96,768]{1,0:T(8,128)(2,1)}, u32[]{:S(2)}, u32[]{:S(2)}) collective-permute-start(bf16[96,768]{1,0:T(8,128)(2,1)} %get-tuple-element.404), channel_id=1, source_target_pairs={{0,1},{1,0},{2,3},{3,2},{4,5},{5,4},{6,7},{7,6},{8,9},{9,8},{10,11... | collective-permute-start | bytes 442376 | tf_op jit(solution)/shard_map/ppermute | solution.py:85
  693.1 19.3 %collective-permute-start.17 = (bf16[4,112,768]{2,1,0:T(8,128)(2,1)S(1)}, bf16[4,112,768]{2,1,0:T(8,128)(2,1)S(1)}, u32[]{:S(2)}, u32[]{:S(2)}) collective-permute-start(bf16[4,112,768]{2,1,0:T(8,128)(2,1)S(1)} %copy-done.41), channel_id=1, source_target_pairs={{0,24},{4,28},{8,16},{12,20},{16,8},{20,12},{24,0},{28,4},{1,25},{... | collective-permute-start | bytes 2064392 | tf_op jit(solution)/shard_map/ppermute | solution.py:85
  696.3 28.7 %collective-permute-start.16 = (bf16[4,112,768]{2,1,0:T(8,128)(2,1)S(1)}, bf16[4,112,768]{2,1,0:T(8,128)(2,1)S(1)}, u32[]{:S(2)}, u32[]{:S(2)}) collective-permute-start(bf16[4,112,768]{2,1,0:T(8,128)(2,1)S(1)} %copy-done.40), channel_id=1, source_target_pairs={{0,16},{4,20},{8,24},{12,28},{16,0},{20,4},{24,8},{28,12},{1,17},{... | collective-permute-start | bytes 2064392 | tf_op jit(solution)/shard_map/ppermute | solution.py:85
  697.5 27.5 %collective-permute-start.15 = (bf16[4,112,768]{2,1,0:T(8,128)(2,1)S(1)}, bf16[4,112,768]{2,1,0:T(8,128)(2,1)S(1)}, u32[]{:S(2)}, u32[]{:S(2)}) collective-permute-start(bf16[4,112,768]{2,1,0:T(8,128)(2,1)S(1)} %copy-done.39), channel_id=1, source_target_pairs={{0,8},{4,12},{8,0},{12,4},{16,24},{20,28},{24,16},{28,20},{1,9},{5... | collective-permute-start | bytes 2064392 | tf_op jit(solution)/shard_map/ppermute | solution.py:85
  725.5 15.1 %collective-permute-start.20 = (bf16[112,768]{1,0:T(8,128)(2,1)S(1)}, bf16[112,768]{1,0:T(8,128)(2,1)S(1)}, u32[]{:S(2)}, u32[]{:S(2)}) collective-permute-start(bf16[112,768]{1,0:T(8,128)(2,1)S(1)} %get-tuple-element.390), channel_id=1, source_target_pairs={{0,3},{1,2},{2,1},{3,0},{4,7},{5,6},{6,5},{7,4},{8,11},{9,10},{10,... | collective-permute-start | bytes 516104 | tf_op jit(solution)/shard_map/ppermute | solution.py:85
  727.7 16.3 %collective-permute-start.19 = (bf16[112,768]{1,0:T(8,128)(2,1)S(1)}, bf16[112,768]{1,0:T(8,128)(2,1)S(1)}, u32[]{:S(2)}, u32[]{:S(2)}) collective-permute-start(bf16[112,768]{1,0:T(8,128)(2,1)S(1)} %get-tuple-element.391), channel_id=1, source_target_pairs={{0,2},{1,3},{2,0},{3,1},{4,6},{5,7},{6,4},{7,5},{8,10},{9,11},{10,... | collective-permute-start | bytes 516104 | tf_op jit(solution)/shard_map/ppermute | solution.py:85
  728.7 15.3 %collective-permute-start.18 = (bf16[112,768]{1,0:T(8,128)(2,1)S(1)}, bf16[112,768]{1,0:T(8,128)(2,1)S(1)}, u32[]{:S(2)}, u32[]{:S(2)}) collective-permute-start(bf16[112,768]{1,0:T(8,128)(2,1)S(1)} %get-tuple-element.389), channel_id=1, source_target_pairs={{0,1},{1,0},{2,3},{3,2},{4,5},{5,4},{6,7},{7,6},{8,9},{9,8},{10,11... | collective-permute-start | bytes 516104 | tf_op jit(solution)/shard_map/ppermute | solution.py:85
  738.2 29.8 %collective-permute-start.38 = (bf16[4,192,768]{2,1,0:T(8,128)(2,1)S(1)}, bf16[4,192,768]{2,1,0:T(8,128)(2,1)S(1)}, u32[]{:S(2)}, u32[]{:S(2)}) collective-permute-start(bf16[4,192,768]{2,1,0:T(8,128)(2,1)S(1)} %get-tuple-element.319), channel_id=1, source_target_pairs={{0,24},{4,28},{8,16},{12,20},{16,8},{20,12},{24,0},{28,4},{1,25},{... | collective-permute-start | bytes 3538952 | tf_op jit(solution)/shard_map/ppermute | solution.py:85
  744.2 49.2 %collective-permute-start.37 = (bf16[4,192,768]{2,1,0:T(8,128)(2,1)}, bf16[4,192,768]{2,1,0:T(8,128)(2,1)}, u32[]{:S(2)}, u32[]{:S(2)}) collective-permute-start(bf16[4,192,768]{2,1,0:T(8,128)(2,1)} %get-tuple-element.320), channel_id=1, source_target_pairs={{0,16},{4,20},{8,24},{12,28},{16,0},{20,4},{24,8},{28,12},{1,17},{... | collective-permute-start | bytes 3538952 | tf_op jit(solution)/shard_map/ppermute | solution.py:85
  745.4 47.9 %collective-permute-start.36 = (bf16[4,192,768]{2,1,0:T(8,128)(2,1)}, bf16[4,192,768]{2,1,0:T(8,128)(2,1)}, u32[]{:S(2)}, u32[]{:S(2)}) collective-permute-start(bf16[4,192,768]{2,1,0:T(8,128)(2,1)} %get-tuple-element.318), channel_id=1, source_target_pairs={{0,8},{4,12},{8,0},{12,4},{16,24},{20,28},{24,16},{28,20},{1,9},{5... | collective-permute-start | bytes 3538952 | tf_op jit(solution)/shard_map/ppermute | solution.py:85
  754.1 64.5 %collective-permute-start.31 = (bf16[4,192,768]{2,1,0:T(8,128)(2,1)}, bf16[4,192,768]{2,1,0:T(8,128)(2,1)S(1)}, u32[]{:S(2)}, u32[]{:S(2)}) collective-permute-start(bf16[4,192,768]{2,1,0:T(8,128)(2,1)} %get-tuple-element.310), channel_id=1, source_target_pairs={{0,24},{4,28},{8,16},{12,20},{16,8},{20,12},{24,0},{28,4},{1,25},{... | collective-permute-start | bytes 3538952 | tf_op jit(solution)/shard_map/ppermute | solution.py:85
  754.9 87.2 %collective-permute-start.30 = (bf16[4,192,768]{2,1,0:T(8,128)(2,1)}, bf16[4,192,768]{2,1,0:T(8,128)(2,1)}, u32[]{:S(2)}, u32[]{:S(2)}) collective-permute-start(bf16[4,192,768]{2,1,0:T(8,128)(2,1)} %get-tuple-element.311), channel_id=1, source_target_pairs={{0,16},{4,20},{8,24},{12,28},{16,0},{20,4},{24,8},{28,12},{1,17},{... | collective-permute-start | bytes 3538952 | tf_op jit(solution)/shard_map/ppermute | solution.py:85
  767.9 74.1 %collective-permute-start.29 = (bf16[4,192,768]{2,1,0:T(8,128)(2,1)}, bf16[4,192,768]{2,1,0:T(8,128)(2,1)}, u32[]{:S(2)}, u32[]{:S(2)}) collective-permute-start(bf16[4,192,768]{2,1,0:T(8,128)(2,1)} %get-tuple-element.309), channel_id=1, source_target_pairs={{0,8},{4,12},{8,0},{12,4},{16,24},{20,28},{24,16},{28,20},{1,9},{5... | collective-permute-start | bytes 3538952 | tf_op jit(solution)/shard_map/ppermute | solution.py:85
  796.0 51.3 %collective-permute-start.41 = (bf16[192,768]{1,0:T(8,128)(2,1)S(1)}, bf16[192,768]{1,0:T(8,128)(2,1)S(1)}, u32[]{:S(2)}, u32[]{:S(2)}) collective-permute-start(bf16[192,768]{1,0:T(8,128)(2,1)S(1)} %get-tuple-element.359), channel_id=1, source_target_pairs={{0,3},{1,2},{2,1},{3,0},{4,7},{5,6},{6,5},{7,4},{8,11},{9,10},{10,... | collective-permute-start | bytes 884744 | tf_op jit(solution)/shard_map/ppermute | solution.py:85
  798.3 51.1 %collective-permute-start.40 = (bf16[192,768]{1,0:T(8,128)(2,1)S(1)}, bf16[192,768]{1,0:T(8,128)(2,1)S(1)}, u32[]{:S(2)}, u32[]{:S(2)}) collective-permute-start(bf16[192,768]{1,0:T(8,128)(2,1)S(1)} %get-tuple-element.360), channel_id=1, source_target_pairs={{0,2},{1,3},{2,0},{3,1},{4,6},{5,7},{6,4},{7,5},{8,10},{9,11},{10,... | collective-permute-start | bytes 884744 | tf_op jit(solution)/shard_map/ppermute | solution.py:85
  818.5 30.9 %collective-permute-start.39 = (bf16[192,768]{1,0:T(8,128)(2,1)S(1)}, bf16[192,768]{1,0:T(8,128)(2,1)S(1)}, u32[]{:S(2)}, u32[]{:S(2)}) collective-permute-start(bf16[192,768]{1,0:T(8,128)(2,1)S(1)} %get-tuple-element.358), channel_id=1, source_target_pairs={{0,1},{1,0},{2,3},{3,2},{4,5},{5,4},{6,7},{7,6},{8,9},{9,8},{10,11... | collective-permute-start | bytes 884744 | tf_op jit(solution)/shard_map/ppermute | solution.py:85
  844.9 11.9 %collective-permute-start.34 = (bf16[192,768]{1,0:T(8,128)(2,1)S(1)}, bf16[192,768]{1,0:T(8,128)(2,1)S(1)}, u32[]{:S(2)}, u32[]{:S(2)}) collective-permute-start(bf16[192,768]{1,0:T(8,128)(2,1)S(1)} %get-tuple-element.348), channel_id=1, source_target_pairs={{0,3},{1,2},{2,1},{3,0},{4,7},{5,6},{6,5},{7,4},{8,11},{9,10},{10,... | collective-permute-start | bytes 884744 | tf_op jit(solution)/shard_map/ppermute | solution.py:85
  847.3 25.9 %collective-permute-start.33 = (bf16[192,768]{1,0:T(8,128)(2,1)S(1)}, bf16[192,768]{1,0:T(8,128)(2,1)S(1)}, u32[]{:S(2)}, u32[]{:S(2)}) collective-permute-start(bf16[192,768]{1,0:T(8,128)(2,1)S(1)} %get-tuple-element.349), channel_id=1, source_target_pairs={{0,2},{1,3},{2,0},{3,1},{4,6},{5,7},{6,4},{7,5},{8,10},{9,11},{10,... | collective-permute-start | bytes 884744 | tf_op jit(solution)/shard_map/ppermute | solution.py:85
  847.3 25.9 %collective-permute-start.32 = (bf16[192,768]{1,0:T(8,128)(2,1)S(1)}, bf16[192,768]{1,0:T(8,128)(2,1)S(1)}, u32[]{:S(2)}, u32[]{:S(2)}) collective-permute-start(bf16[192,768]{1,0:T(8,128)(2,1)S(1)} %get-tuple-element.347), channel_id=1, source_target_pairs={{0,1},{1,0},{2,3},{3,2},{4,5},{5,4},{6,7},{7,6},{8,9},{9,8},{10,11... | collective-permute-start | bytes 884744 | tf_op jit(solution)/shard_map/ppermute | solution.py:85
  (106 other events, 833.9 us)
Sparse Core Ops, SparseCore 0:
  14.0 128.6 all-gather.4
  146.1 103.4 all-gather.2
